TPU v7x, 512 devices: a whole 4x4x16 slice. The times are simulated.
512 devices in a mesh: fsdp: 32 (over x, z_hi, core), ctx: 16 (over y, z_lo).
Axes of the slice: x: 4, y: 4, z: 16 (z_hi: 4, z_lo: 4; z = z_hi * 4 + z_lo), core: 2. Of those that a mesh axis runs over, the one named last changes fastest.
Arguments:
- features: bfloat16 [3, 16384, 8192], P(None, 'ctx', 'fsdp'), may hold values from -6 to 6
- short_taps: float32 [3, 3, 8192], P(None, None, 'fsdp'), may hold values from -3.5 to 3.5
- decay_rates: float32 [512, 16], P('fsdp'), may hold values from 1.5258789e-05 to 0.1
- mode_gains: float32 [512, 16], P('fsdp'), may hold values from -2.5 to 2.5
- cotangent: bfloat16 [16384, 8192], P('ctx', 'fsdp'), may hold values from -6 to 6
Outputs:
- mixer_output: bfloat16 [16384, 8192], P('ctx', 'fsdp')
- feature_grads: bfloat16 [3, 16384, 8192], P(None, 'ctx', 'fsdp')
- gain_grads: float32 [512, 16], P('fsdp')
- rate_grads: float32 [512, 16], P('fsdp')
All inputs are finite; a program needn't handle non-finite values.
Results may differ from a plain program's by a relative error of at most 0.0048.
Values may be sent and summed in bfloat16 or wider, within the bound.
A program may use at most 64 MiB of HBM per device.

v0:
```python
import jax
import jax.numpy as jnp
from jax import lax
from jax.experimental import pallas as pl
from jax.experimental.pallas import tpu as pltpu
from jax.sharding import PartitionSpec as P
import functools

MESH = pl.DeviceIdType.MESH

precise = lax.Precision.HIGHEST
threepass = lax.Precision.HIGH


def gather_kernel(axis, count, x_ref, o_ref, held, send_sem, recv_sem):
    me = lax.axis_index(axis)

    def device(peer):
        if axis == "ctx":
            return (lax.axis_index("fsdp"), peer)
        return (peer, lax.axis_index("ctx"))

    barrier = pltpu.get_barrier_semaphore()
    for step in range(1, count):
        pl.semaphore_signal(
            barrier, inc=1, device_id=device(lax.rem(me + step, count)), device_id_type=MESH
        )
    pl.semaphore_wait(barrier, count - 1)
    copies = []
    for step in range(1, count):
        copy = pltpu.make_async_remote_copy(
            src_ref=x_ref,
            dst_ref=held.at[me],
            send_sem=send_sem.at[step - 1],
            recv_sem=recv_sem.at[step - 1],
            device_id=device(lax.rem(me + step, count)),
            device_id_type=MESH,
        )
        copy.start()
        copies.append(copy)
    for copy in copies:
        copy.wait()
    held[me] = x_ref[...]
    o_ref[...] = held[...]


def gather_along(value, axis, collective_id):
    count = lax.axis_size(axis)
    return pl.pallas_call(
        functools.partial(gather_kernel, axis, count),
        out_shape=jax.ShapeDtypeStruct((count,) + value.shape, value.dtype),
        in_specs=[pl.BlockSpec(memory_space=pltpu.VMEM)],
        out_specs=pl.BlockSpec(memory_space=pltpu.VMEM),
        scratch_shapes=[
            pltpu.VMEM((count,) + value.shape, value.dtype),
            pltpu.SemaphoreType.DMA((count - 1,)),
            pltpu.SemaphoreType.DMA((count - 1,)),
        ],
        compiler_params=pltpu.CompilerParams(collective_id=collective_id, has_side_effects=True),
    )(value)


def passed_along(value, axis, steps):
    count = lax.axis_size(axis)
    leading, last = (max(0, -steps), min(count, count - steps))
    return lax.ppermute(value, axis, [(source, source + steps) for source in range(leading, last)])


def short_conv(taps_table, row_data, tokens, rim_rows, forward):
    summed = jnp.zeros((3, tokens, row_data.shape[2]), jnp.float32)
    for offset in range(taps_table.shape[1]):
        start_row = rim_rows - offset if forward else offset
        summed = (
            summed + taps_table[:, offset, None, :] * row_data[:, start_row : start_row + tokens, :]
        )
    return summed


def per_device(features, short_taps, decay_rates, mode_gains, cotangent):
    tokens = features.shape[1]
    channels = features.shape[2]
    group_count = decay_rates.shape[0]
    order_count = decay_rates.shape[1]
    members = channels // group_count
    rim_rows = short_taps.shape[1] - 1
    block_len = 128
    block_count = tokens // block_len
    ctx_count = lax.axis_size("ctx")
    ctx_index = lax.axis_index("ctx")
    earlier_rows = passed_along(features[:, tokens - rim_rows :, :], "ctx", 1)
    extended = jnp.concatenate([earlier_rows, features], axis=1)
    shaped = short_conv(short_taps, extended, tokens, rim_rows, True)
    query_part, key_part, value_part = (shaped[0], shaped[1], shaped[2])
    product = (key_part * value_part).astype(jnp.bfloat16)
    adjoint = cotangent * query_part
    grouped_z = product.reshape(tokens, group_count, members)
    grouped_e = adjoint.reshape(tokens, group_count, members)
    mode_coefs = mode_gains * jnp.sqrt(2.0 * decay_rates)
    rate_axis = decay_rates[:, :, None]
    lag_axis = jnp.arange(block_len, dtype=jnp.float32)[None, None, :]
    block_pow = jnp.exp(-rate_axis * lag_axis)
    block_after = block_pow * jnp.exp(-rate_axis)
    block_moments = jnp.stack([block_after, (lag_axis + 1.0) * block_after])
    coef_after = mode_coefs[:, :, None] * block_after
    tail_axis = block_len - 1.0 - lag_axis
    tail_pow = jnp.exp(-rate_axis * tail_axis)
    block_ends = jnp.stack([tail_pow, -tail_axis * tail_pow])
    coef_tail = mode_coefs[:, :, None] * jnp.exp(-rate_axis * (tail_axis + 1.0))
    lag_index = (
        jnp.arange(block_len, dtype=jnp.int32)[:, None]
        - jnp.arange(block_len, dtype=jnp.int32)[None, :]
    )
    lag_value = jnp.maximum(lag_index, 0).astype(jnp.float32)
    pair_pow = jnp.exp(-decay_rates[:, :, None, None] * lag_value[None, None])
    toeplitz = jnp.where(
        lag_index[None] >= 0, jnp.sum(mode_coefs[:, :, None, None] * pair_pow, axis=1), 0.0
    )
    z_blocks = grouped_z.reshape(block_count, block_len, group_count, members)
    e_blocks = grouped_e.reshape(block_count, block_len, group_count, members)

    z_wide = z_blocks.astype(jnp.float32)
    block_ids = jnp.arange(block_count, dtype=jnp.float32)
    block_steps = (block_ids[:, None] - 1.0 - block_ids[None, :])[:, :, None, None, None]
    span_weight = jnp.where(
        block_steps >= 0,
        jnp.exp(-decay_rates.T[None, None, :, :, None] * (block_len * jnp.maximum(block_steps, 0.0))),
        0.0,
    )
    inside_fwd = jnp.einsum("gts,bsgm->btgm", toeplitz, z_wide, precision=threepass)
    fresh_fwd = jnp.einsum("kgns,bsgm->kbngm", block_ends, z_wide, precision=threepass)
    start_states = jnp.sum(span_weight * fresh_fwd[0][None], axis=1)
    start_lagged = jnp.sum(
        span_weight * (fresh_fwd[1][None] - block_len * block_steps * fresh_fwd[0][None]), axis=1
    )
    moments = jnp.einsum("kgnt,btgm->kbngm", block_moments, e_blocks, precision=precise)
    first_acc = jnp.sum(moments[0] * start_states, axis=(0, 3))
    lag_acc = jnp.sum(moments[0] * start_lagged - moments[1] * start_states, axis=(0, 3))
    gram_acc = jnp.einsum("btgm,bsgm->gts", e_blocks, z_wide, precision=precise)
    pair_mask = jnp.where(lag_index[None, None] >= 0, pair_pow, 0.0)
    first_in = jnp.sum(pair_mask * gram_acc[:, None], axis=(2, 3))
    lag_in = jnp.sum((pair_mask * lag_value[None, None]) * gram_acc[:, None], axis=(2, 3))
    first_local = first_acc.T + first_in
    lag_local = lag_acc.T - lag_in
    inside_bwd = jnp.einsum("gts,btgm->bsgm", toeplitz, e_blocks, precision=precise)
    fresh_bwd = jnp.einsum("gnt,btgm->bngm", block_pow, e_blocks, precision=precise)
    later_states = jnp.sum(jnp.swapaxes(span_weight, 0, 1) * fresh_bwd[None], axis=1)
    rates_ng = decay_rates.T[None, :, :, None]
    from_first = jnp.exp(-rates_ng * (block_len * block_ids[:, None, None, None]))
    from_last = jnp.exp(-rates_ng * (block_len * (block_count - 1.0 - block_ids[:, None, None, None])))
    end_state = jnp.sum(from_last * fresh_fwd[0], axis=0)
    end_lagged = jnp.sum(
        from_last
        * (fresh_fwd[1] - block_len * (block_count - 1.0 - block_ids[:, None, None, None]) * fresh_fwd[0]),
        axis=0,
    )
    start_state = jnp.sum(from_first * fresh_bwd, axis=0)
    second_moment = jnp.sum(
        from_first * (moments[1] + block_len * block_ids[:, None, None, None] * moments[0]), axis=0
    )
    local_states = jnp.stack([end_state, end_lagged, start_state]).reshape(3, order_count, channels)
    partial_rows = jnp.stack([first_local, lag_local]).reshape(-1, channels)
    partial_slot = jnp.zeros((order_count, channels), jnp.float32)
    partial_slot = partial_slot.at[: partial_rows.shape[0]].set(partial_rows)
    local_states = jnp.concatenate(
        [local_states, second_moment.reshape(1, order_count, channels), partial_slot[None]]
    )
    rate_cols = jnp.repeat(decay_rates.T, members, axis=1)
    everyone = gather_along(local_states, "ctx", 0)
    device_ids = jnp.arange(ctx_count, dtype=jnp.int32)
    ahead_steps = (ctx_index - 1 - device_ids).astype(jnp.float32)[:, None, None]
    behind_steps = (device_ids - ctx_index - 1).astype(jnp.float32)[:, None, None]
    ahead_weight = jnp.where(
        ahead_steps >= 0, jnp.exp(-rate_cols[None] * (tokens * jnp.maximum(ahead_steps, 0.0))), 0.0
    )
    behind_weight = jnp.where(
        behind_steps >= 0,
        jnp.exp(-rate_cols[None] * (tokens * jnp.maximum(behind_steps, 0.0))),
        0.0,
    )
    prev_state = jnp.sum(ahead_weight * everyone[:, 0], axis=0)
    next_state = jnp.sum(behind_weight * everyone[:, 2], axis=0)
    all_ids = device_ids.astype(jnp.float32)
    pair_steps = (all_ids[:, None] - 1.0 - all_ids[None, :])[:, :, None, None]
    pair_weight = jnp.where(
        pair_steps >= 0, jnp.exp(-rate_cols[None, None] * (tokens * jnp.maximum(pair_steps, 0.0))), 0.0
    )
    all_prev = jnp.sum(pair_weight * everyone[None, :, 0], axis=1)
    all_lagged = jnp.sum(
        pair_weight * (everyone[None, :, 1] - tokens * pair_steps * everyone[None, :, 0]), axis=1
    )
    all_first = jnp.exp(-rate_cols)[None] * everyone[:, 2]
    cross_first = jnp.sum(all_first * all_prev, axis=0)
    cross_lag = jnp.sum(all_first * all_lagged - everyone[:, 3] * all_prev, axis=0)
    cross_first = cross_first.reshape(order_count, group_count, members).sum(axis=2).T
    cross_lag = cross_lag.reshape(order_count, group_count, members).sum(axis=2).T
    gathered_parts = everyone[:, 4, : partial_rows.shape[0]].reshape(
        ctx_count, 2, group_count, order_count
    )
    local_totals = jnp.sum(gathered_parts, axis=0)
    first_total = local_totals[0] + cross_first
    lag_total = local_totals[1] + cross_lag

    prev_grouped = prev_state.reshape(order_count, group_count, members)
    next_grouped = next_state.reshape(order_count, group_count, members)
    start_total = start_states + from_first * prev_grouped[None]
    later_total = later_states + from_last * next_grouped[None]
    carried_fwd = jnp.einsum("gnt,bngm->btgm", coef_after, start_total, precision=precise)
    inner_sum = (inside_fwd + carried_fwd).reshape(tokens, group_count, members)
    carried_bwd = jnp.einsum("gns,bngm->bsgm", coef_tail, later_total, precision=precise)
    product_grad = (inside_bwd + carried_bwd).reshape(tokens, group_count, members)
    gain_part = jnp.sqrt(2.0 * decay_rates) * first_total
    rate_part = mode_coefs * (0.5 * first_total + decay_rates * lag_total)
    inner_flat = inner_sum.reshape(tokens, channels)
    mixer_output = (query_part * inner_flat).astype(jnp.bfloat16)
    grad_flat = product_grad.reshape(tokens, channels)
    feature_adj = jnp.stack([cotangent * inner_flat, grad_flat * value_part, grad_flat * key_part])
    later_rows = passed_along(feature_adj[:, :rim_rows, :], "ctx", -1)
    appended = jnp.concatenate([feature_adj, later_rows], axis=1)
    feature_grads = short_conv(short_taps, appended, tokens, rim_rows, False).astype(jnp.bfloat16)
    filter_local = jnp.stack([gain_part, rate_part])
    entry_count = 2 * group_count * order_count * lax.axis_size("fsdp")
    summed = filter_local
    square_tile = jnp.full((8, 128), jnp.sum(summed * summed), jnp.float32)
    squares = jnp.sum(gather_along(square_tile, "fsdp", 1)[:, 0, 0])
    factor = jnp.minimum(1.0, lax.rsqrt(squares / entry_count + 1e-06))
    clipped = summed * factor
    return (mixer_output, feature_grads, clipped[0], clipped[1])


def solution(mesh):
    return jax.shard_map(
        per_device,
        mesh=mesh,
        in_specs=(
            P(None, "ctx", "fsdp"),
            P(None, None, "fsdp"),
            P("fsdp", None),
            P("fsdp", None),
            P("ctx", "fsdp"),
        ),
        out_specs=(P("ctx", "fsdp"), P(None, "ctx", "fsdp"), P("fsdp", None), P("fsdp", None)),
        check_vma=False,
    )
```

profile of v0, /device:TPU:1, one launch (start us, length us, event | category | flops | bytes accessed | tf_op | source)
XLA Modules:
  0.0 210.3 jit_solution(8671222826404712126)
XLA Ops:
  1.7 4.4 %collective-permute-start = (bf16[3,2,256]{1,2,0:T(8,128)(2,1)S(1)}, bf16[3,2,256]{1,2,0:T(8,128)(2,1)S(1)}, u32[]{:S(2)}, u32[]{:S(2)}) collective-permute-start(bf16[3,2,256]{1,2,0:T(8,128)(2,1)S(1)} %copy.132), channel_id=1, source_target_pairs={{0,1},{1,2},{2,3},{3,4},{4,5},{5,6},{6,7},{7,8},{8,9},{9,10},{10,1... | collective-permute-start | bytes 9224 | tf_op jit(solution)/shard_map/ppermute | solution.py:66
  14.9 1.0 exponential_select_fusion.1
  17.4 1.7 copy.131
  23.0 4.8 %multiply_add_fusion = f32[3,1024,256]{1,2,0:T(8,128)S(1)} fusion(bf16[3,1024,256]{1,2,0:T(8,128)(2,1)} %copy.131, bf16[3,2,256]{1,2,0:T(8,128)(2,1)} %copy-done.21, f32[3,256]{1,0:T(4,128)} %get-tuple-element.84, f32[3,256]{1,0:T(4,128)} %get-tuple-element.85, f32[3,256]{1,0:T(4,128)} %bitcast.199), kind=kLoop, calls=%fused_computation.18 | loop fusion | flops 11010048 | bytes 4730880 | tf_op jit(solution)/shard_map/add | solution.py:74
  29.7 1.3 copy-done
  31.0 1.6 slice_bitcast_fusion.3
  32.6 2.6 %copy.143 = f32[8,16,16,16]{3,2,1,0:T(8,128)} copy(f32[8,16,16,16]{1,3,0,2:T(8,128)} %get-tuple-element.55) | data formatting | bytes 262144 | tf_op jit(solution)/shard_map/mul | solution.py:131
  35.2 2.6 %copy.154 = f32[8,16,16,16]{3,2,1,0:T(8,128)} copy(f32[8,16,16,16]{1,3,0,2:T(8,128)} %get-tuple-element.56) | data formatting | bytes 262144 | tf_op jit(solution)/shard_map/squeeze | solution.py:153
  37.8 5.8 %multiply_reduce_fusion.4 = (f32[8,16,16,16]{3,2,1,0:T(8,128)}, f32[8,16,16,16]{3,2,1,0:T(8,128)}) fusion(f32[8,8]{1,0:T(8,128)S(1)} %copy-done.37, f32[8,16,16,16]{3,2,1,0:T(8,128)} %copy.154, f32[8,16,16,16]{3,2,1,0:T(8,128)} %copy.143, f32[8,8,16,16]{3,2,1,0:T(8,128)} %exponential_select_fusion.1), kind=kLoop, calls=%fused_computation.6 | loop fusion | flops 1507328 | bytes 590080 | tf_op jit(solution)/shard_map/reduce_sum | solution.py:132
  43.6 2.6 %copy.160 = f32[8,16,16,16]{1,3,0,2:T(8,128)} copy(f32[8,16,16,16]{3,2,1,0:T(8,128)} %get-tuple-element.40) | data formatting | bytes 262144 | tf_op jit(solution)/shard_map/reduce_sum | solution.py:131
  46.2 2.6 %copy.156 = f32[8,16,16,16]{1,3,0,2:T(8,128)} copy(f32[8,16,16,16]{3,2,1,0:T(8,128)} %get-tuple-element.39) | data formatting | bytes 262144 | tf_op jit(solution)/shard_map/reduce_sum | solution.py:132
  48.8 1.3 fusion.7
  50.4 1.0 convolution_bitcast_fusion.2
  51.6 2.0 convolution_bitcast_fusion
  53.7 3.4 %multiply_reduce_fusion.8 = (f32[16,16]{0,1:T(8,128)S(1)}, f32[16,16]{0,1:T(8,128)}, f32[16,16,16]{0,2,1:T(8,128)S(1)}, f32[16,16,16]{0,2,1:T(8,128)S(1)}, f32[8,16,16,16]{1,3,0,2:T(8,128)}) fusion(f32[8,16,16,16]{1,3,0,2:T(8,128)S(1)} %copy-done.8, f32[2,8,16,16,16]{2,4,1,3,0:T(8,128)S(1)} %convolution_bitcast_fusion, ...), kind=kOutput, calls=%fused_computation.52 | convolution fusion | flops 50748928 | bytes 1748000 | tf_op jit(solution)/shard_map/gnt,btgm->bngm/dot_general | solution.py:145
  57.1 9.4 %multiply_reduce_fusion.1 = (f32[16,16]{1,0:T(8,128)S(1)}, f32[16,16]{1,0:T(8,128)}, f32[16,128,128]{2,1,0:T(8,128)}) fusion(f32[16,128,128]{2,1,0:T(8,128)S(1)} %convolution_bitcast_fusion.2, f32[128,128]{1,0:T(8,128)S(1)} %copy-done.33, f32[16,16]{1,0:T(8,128)S(1)} %get-tuple-element.78, pred[128,128]{1,0:T(8,128)(4,1)S(1)} %copy-done.22, ...), kind=kLoop, calls=%fused_computation.1 | loop fusion | flops 37486080 | bytes 2183168 | tf_op jit(solution)/shard_map/reduce_sum | solution.py:140
  67.1 1.4 stack.51
  68.5 1.3 bitcast_subtract_fusion
  69.8 1.4 stack.52
  71.8 2.6 %multiply_reduce_fusion.11 = (f32[16,16,16]{0,2,1:T(8,128)S(1)}, f32[16,16,16]{0,2,1:T(8,128)}) fusion(f32[8]{0:T(128)} %copy-done.47, f32[8,16,16]{1,0,2:T(8,128)S(1)} %get-tuple-element.73, f32[2,8,16,16,16]{2,4,0,1,3:T(8,128)} %copy-done), kind=kLoop, calls=%fused_computation.55 | loop fusion | flops 188416 | bytes 303136 | tf_op jit(solution)/shard_map/reduce_sum | solution.py:151
  74.4 1.6 copy.188
  76.0 1.3 constant_dynamic-update-slice_fusion.3
  78.0 1.3 constant_dynamic-update-slice_fusion.2
  79.3 1.3 constant_dynamic-update-slice_fusion.1
  81.3 1.3 fusion.57.x_ref
  82.5 35.1 %shard_map.84 = f32[16,5,16,256]{3,2,1,0:T(8,128)} custom-call(f32[5,16,256]{2,1,0:T(8,128)} %fusion.57.x_ref), custom_call_target="tpu_custom_call" | custom-call | tf_op jit(solution)/shard_map/pallas_call | solution.py:49
  117.7 1.2 slice_bitcast_fusion.6
  118.9 1.5 slice_reduce_fusion
  120.5 3.9 %fusion.10 = f32[16,8,16,128]{3,2,1,0:T(8,128)} fusion(f32[16,128,128]{2,1,0:T(8,128)} %get-tuple-element.49, f32[8,128,16,16]{1,0,3,2:T(8,128)} %bitcast.188, pred[128,128]{1,0:T(8,128)(4,1)} %fusion.56), kind=kOutput, calls=%fused_computation.42 | convolution fusion | flops 402915328 | bytes 3162112 | tf_op jit(solution)/shard_map/gts,btgm->bsgm/dot_general | solution.py:144
  124.4 1.8 fusion.12
  126.2 2.2 %multiply_reduce_fusion.6 = (f32[16,16,256]{2,1,0:T(8,128)S(1)}, f32[16,16,256]{2,1,0:T(8,128)S(1)}) fusion(f32[16,16]{1,0:T(8,128)S(1)} %copy-done.39, f32[16,16,256]{2,1,0:T(8,128)S(1)} %get-tuple-element.58, f32[16,16,256]{2,1,0:T(8,128)S(1)} %get-tuple-element.57, f32[16,16]{1,0:T(8,128)S(1)} %copy-done.38, f32[16,256]{1,0:T(8,128)S(1)} %copy-done.25, ...), kind=kLoop, calls=%fused_computation.8 | loop fusion | flops 8257536 | bytes 1067264 | tf_op jit(solution)/shard_map/reduce_sum | solution.py:188
  133.5 1.2 broadcast_in_dim.122.x_ref
  134.8 24.8 %shard_map.85 = f32[32,8,128]{2,1,0:T(8,128)} custom-call(f32[8,128]{1,0:T(8,128)} %broadcast_in_dim.122.x_ref), custom_call_target="tpu_custom_call" | custom-call | tf_op jit(solution)/shard_map/pallas_call | solution.py:49
  159.6 1.5 slice_reduce_fusion.1
  161.9 2.6 %copy.165 = f32[8,16,16,16]{3,2,1,0:T(8,128)} copy(f32[8,16,16,16]{1,3,0,2:T(8,128)} %get-tuple-element.83) | data formatting | bytes 262144 | tf_op jit(solution)/shard_map/gnt,btgm->bngm/transpose | solution.py:145
  164.4 5.2 %multiply_reduce_fusion.3 = f32[8,16,16,16]{3,2,1,0:T(8,128)} fusion(f32[8,16,16,16]{3,2,1,0:T(8,128)} %copy.165, f32[8,8,16,16]{3,2,1,0:T(8,128)} %select_bitcast_fusion), kind=kLoop, calls=%fused_computation.5 | loop fusion | flops 491520 | bytes 327680 | tf_op jit(solution)/shard_map/reduce_sum | solution.py:146
  169.7 2.6 %copy.168 = f32[8,16,16,16]{1,3,0,2:T(8,128)} copy(f32[8,16,16,16]{3,2,1,0:T(8,128)} %multiply_reduce_fusion.3) | data formatting | bytes 262144 | tf_op jit(solution)/shard_map/reduce_sum | solution.py:146
  172.4 2.7 %fusion.5 = f32[8,128,16,16]{1,3,0,2:T(8,128)S(1)} fusion(f32[16,8,16,128]{3,2,1,0:T(8,128)} %fusion.10, f32[8,16,16,16]{1,3,0,2:T(8,128)} %copy.168, f32[16,16,16]{0,2,1:T(8,128)S(1)} %bitcast.196, f32[8,16,16]{1,0,2:T(8,128)S(1)} %get-tuple-element.73, f32[128]{0:T(128)S(1)} %copy-done.48, f32[16,16]{1,0:T(8,128)S(1)} %copy.136, ...), kind=kOutput, calls=%fused_computation.27 | convolution fusion | flops 50724864 | bytes 2255360 | tf_op jit(solution)/shard_map/gns,bngm->bsgm/dot_general | solution.py:209
  175.1 1.3 copy.169
  176.4 2.4 %reshape_reshape.12 = f32[1,1024,256]{1,2,0:T(8,128)} reshape(f32[8,128,16,16]{1,0,3,2:T(8,128)} %copy.169) | data formatting | bytes 2097152 | tf_op jit(solution)/shard_map/reshape;reshape | solution.py:215
  178.9 2.9 %slice_multiply_fusion.2 = (f32[1,1024,256]{1,2,0:T(8,128)}, f32[1,1024,256]{1,2,0:T(8,128)}) fusion(f32[1,1024,256]{1,2,0:T(8,128)} %reshape_reshape.12, f32[3,1024,256]{1,2,0:T(8,128)S(1)} %multiply_add_fusion), kind=kLoop, calls=%fused_computation.58 | loop fusion | flops 524288 | bytes 5242880 | tf_op jit(solution)/shard_map/mul | solution.py:216
  181.9 2.8 %fusion.6 = f32[8,128,16,16]{1,3,0,2:T(8,128)S(1)} fusion(f32[16,8,16,128]{3,2,1,0:T(8,128)} %fusion.12, f32[8,16,16,16]{1,3,0,2:T(8,128)} %copy.160, f32[16,16,16]{0,2,1:T(8,128)S(1)} %bitcast.195, f32[8,16,16]{1,0,2:T(8,128)S(1)} %get-tuple-element.72, f32[16,16]{1,0:T(8,128)S(1)} %copy-done.27, f32[16,16]{1,0:T(8,128)S(1)} %copy.136, ...), kind=kOutput, calls=%fused_computation.29 | convolution fusion | flops 50757632 | bytes 2255872 | tf_op jit(solution)/shard_map/gnt,bngm->btgm/dot_general | solution.py:207
  185.1 1.2 fusion.8
  187.3 1.4 collective-permute-start.1
  191.1 11.7 %collective-permute-done.1 = f32[3,2,256]{1,2,0:T(8,128)S(1)} collective-permute-done((f32[3,2,256]{1,2,0:T(8,128)S(1)}, f32[3,2,256]{1,2,0:T(8,128)S(1)}, u32[]{:S(2)}, u32[]{:S(2)}) %collective-permute-start.1) | collective-permute-done | bytes 6176 | tf_op jit(solution)/shard_map/ppermute | solution.py:66
  202.9 1.5 pad_maximum_fusion
  204.4 3.3 %fusion.2 = bf16[3,1024,256]{1,2,0:T(8,128)(2,1)} fusion(f32[3,1026,256]{1,2,0:T(8,128)S(1)} %pad_maximum_fusion, f32[3,256]{1,0:T(4,128)S(1)} %copy-done.34, f32[3,256]{1,0:T(4,128)S(1)} %copy-done.35, f32[3,256]{1,0:T(4,128)S(1)} %bitcast.200, f32[1,1024,256]{1,2,0:T(8,128)S(1)} %copy-done.4, f32[1,1024,256]{1,2,0:T(8,128)S(1)} %copy-done.2, ...), kind=kLoop, calls=%fused_computation.14 | loop fusion | flops 6291456 | bytes 11019264 | tf_op jit(solution)/shard_map/convert_element_type | solution.py:219
  207.7 2.6 %copy.174 = bf16[3,1024,256]{2,1,0:T(8,128)(2,1)} copy(bf16[3,1024,256]{1,2,0:T(8,128)(2,1)} %fusion.2) | data formatting | bytes 3145728
  (165 shorter events, 29.0 us)
Async XLA Ops:
  0.6 16.8 %copy-start.17 = (bf16[3,1024,256]{2,1,0:T(8,128)(2,1)S(1)}, bf16[3,1024,256]{2,1,0:T(8,128)(2,1)}, u32[]{:S(2)}) copy-start(bf16[3,1024,256]{2,1,0:T(8,128)(2,1)} %param.7) | copy-start | bytes 4718596
  0.6 19.7 %copy-start.18 = (bf16[1024,256]{1,0:T(8,128)(2,1)S(1)}, bf16[1024,256]{1,0:T(8,128)(2,1)}, u32[]{:S(2)}) copy-start(bf16[1024,256]{1,0:T(8,128)(2,1)} %param.11) | copy-start | bytes 1572868
  1.7 20.6 %collective-permute-start = (bf16[3,2,256]{1,2,0:T(8,128)(2,1)S(1)}, bf16[3,2,256]{1,2,0:T(8,128)(2,1)S(1)}, u32[]{:S(2)}, u32[]{:S(2)}) collective-permute-start(bf16[3,2,256]{1,2,0:T(8,128)(2,1)S(1)} %copy.132), channel_id=1, source_target_pairs={{0,1},{1,2},{2,3},{3,4},{4,5},{5,6},{6,7},{7,8},{8,9},{9,10},{10,1... | collective-permute-start | bytes 9224 | tf_op jit(solution)/shard_map/ppermute | solution.py:66
  6.2 9.9 %copy-start.40 = (f32[8]{0:T(128)}, f32[8]{0:T(128)S(1)}, u32[]{:S(2)}) copy-start(f32[8]{0:T(128)S(1)} %get-tuple-element.89) | copy-start | bytes 100
  6.2 9.9 %copy-start.47 = (f32[8]{0:T(128)}, f32[8]{0:T(128)S(1)}, u32[]{:S(2)}) copy-start(f32[8]{0:T(128)S(1)} %get-tuple-element.88) | copy-start | bytes 100
  6.9 14.6 %copy-start.26 = (f32[16,16]{1,0:T(8,128)}, f32[16,16]{1,0:T(8,128)S(1)}, u32[]{:S(2)}) copy-start(f32[16,16]{1,0:T(8,128)S(1)} %get-tuple-element.76) | copy-start | bytes 3076
  7.7 8.4 %copy-start.28 = (f32[16,16]{0,1:T(8,128)}, f32[16,16]{0,1:T(8,128)S(1)}, u32[]{:S(2)}) copy-start(f32[16,16]{0,1:T(8,128)S(1)} %copy.134) | copy-start | bytes 3076
  13.3 2.8 %copy-start.29 = (f32[16,16]{0,1:T(8,128)}, f32[16,16]{0,1:T(8,128)S(1)}, u32[]{:S(2)}) copy-start(f32[16,16]{0,1:T(8,128)S(1)} %copy.135) | copy-start | bytes 3076
  29.7 1.3 copy-start
  32.6 5.2 %copy-start.37 = (f32[8,8]{1,0:T(8,128)S(1)}, f32[8,8]{1,0:T(8,128)}, u32[]{:S(2)}) copy-start(f32[8,8]{1,0:T(8,128)} %copy.155) | copy-start | bytes 772
  48.8 1.5 copy-start.11
  50.3 3.4 %copy-start.5 = (f32[32,8,8,128]{3,2,1,0:T(8,128)}, f32[32,8,8,128]{3,2,1,0:T(8,128)S(1)}, u32[]{:S(2)}) copy-start(f32[32,8,8,128]{3,2,1,0:T(8,128)S(1)} %copy.201) | copy-start | bytes 3145732
  50.3 1.1 copy-start.19
  50.4 1.3 copy-start.20
  51.4 2.3 %copy-start.8 = (f32[8,16,16,16]{1,3,0,2:T(8,128)S(1)}, f32[8,16,16,16]{1,3,0,2:T(8,128)}, u32[]{:S(2)}) copy-start(f32[8,16,16,16]{1,3,0,2:T(8,128)} %copy.160) | copy-start | bytes 393220
  51.4 2.3 %copy-start.15 = (f32[8,16,16,16]{1,3,0,2:T(8,128)S(1)}, f32[8,16,16,16]{1,3,0,2:T(8,128)}, u32[]{:S(2)}) copy-start(f32[8,16,16,16]{1,3,0,2:T(8,128)} %copy.156) | copy-start | bytes 393220
  51.4 2.3 %copy-start.41 = (f32[8]{0:T(128)S(1)}, f32[8]{0:T(128)}, u32[]{:S(2)}) copy-start(f32[8]{0:T(128)} %copy-done.40) | copy-start | bytes 100
  53.7 3.4 %copy-start.22 = (pred[128,128]{1,0:T(8,128)(4,1)S(1)}, pred[128,128]{1,0:T(8,128)(4,1)}, u32[]{:S(2)}) copy-start(pred[128,128]{1,0:T(8,128)(4,1)} %fusion.56) | copy-start | bytes 49156
  53.7 3.4 %copy-start.33 = (f32[128,128]{1,0:T(8,128)S(1)}, f32[128,128]{1,0:T(8,128)}, u32[]{:S(2)}) copy-start(f32[128,128]{1,0:T(8,128)} %maximum_convert_fusion) | copy-start | bytes 196612
  78.0 46.4 %copy-start.23 = (pred[128,128]{1,0:T(8,128)(4,1)S(1)}, pred[128,128]{1,0:T(8,128)(4,1)}, u32[]{:S(2)}) copy-start(pred[128,128]{1,0:T(8,128)(4,1)} %fusion.56) | copy-start | bytes 49156
  117.7 6.7 %copy-start.12 = (bf16[32,8,8,128]{3,2,1,0:T(8,128)(2,1)S(1)}, bf16[32,8,8,128]{3,2,1,0:T(8,128)(2,1)}, u32[]{:S(2)}) copy-start(bf16[32,8,8,128]{3,2,1,0:T(8,128)(2,1)} %copy-done.10) | copy-start | bytes 1572868
  117.7 6.7 %copy-start.14 = (f32[16,128,128]{2,1,0:T(8,128)S(1)}, f32[16,128,128]{2,1,0:T(8,128)}, u32[]{:S(2)}) copy-start(f32[16,128,128]{2,1,0:T(8,128)} %get-tuple-element.49) | copy-start | bytes 3145732
  118.9 7.3 %copy-start.25 = (f32[16,256]{1,0:T(8,128)S(1)}, f32[16,256]{1,0:T(8,128)}, u32[]{:S(2)}) copy-start(f32[16,256]{1,0:T(8,128)} %copy-done.24) | copy-start | bytes 49156
  118.9 7.3 %copy-start.38 = (f32[16,16]{1,0:T(8,128)S(1)}, f32[16,16]{1,0:T(8,128)}, u32[]{:S(2)}) copy-start(f32[16,16]{1,0:T(8,128)} %get-tuple-element.79) | copy-start | bytes 3076
  118.9 7.3 %copy-start.39 = (f32[16,16]{1,0:T(8,128)S(1)}, f32[16,16]{1,0:T(8,128)}, u32[]{:S(2)}) copy-start(f32[16,16]{1,0:T(8,128)} %get-tuple-element.80) | copy-start | bytes 3076
  118.9 7.3 %copy-start.46 = (pred[16,16]{1,0:T(8,128)(4,1)S(1)}, pred[16,16]{1,0:T(8,128)(4,1)}, u32[]{:S(2)}) copy-start(pred[16,16]{1,0:T(8,128)(4,1)} %subtract_compare_fusion) | copy-start | bytes 772
  120.5 8.0 %copy-start.9 = (f32[16,5,16,256]{3,2,1,0:T(8,128)S(1)}, f32[16,5,16,256]{3,2,1,0:T(8,128)}, u32[]{:S(2)}) copy-start(f32[16,5,16,256]{3,2,1,0:T(8,128)} %shard_map.84) | copy-start | bytes 3932164
  120.5 8.0 %copy-start.32 = (f32[16,256]{1,0:T(8,128)S(1)}, f32[16,256]{1,0:T(8,128)}, u32[]{:S(2)}) copy-start(f32[16,256]{1,0:T(8,128)} %exp.98) | copy-start | bytes 49156
  120.5 8.0 %copy-start.42 = (f32[16]{0:T(128)S(1)}, f32[16]{0:T(128)}, u32[]{:S(2)}) copy-start(f32[16]{0:T(128)} %get-tuple-element.90) | copy-start | bytes 196
  120.5 8.0 %copy-start.43 = (f32[16]{0:T(128)S(1)}, f32[16]{0:T(128)}, u32[]{:S(2)}) copy-start(f32[16]{0:T(128)} %get-tuple-element.91) | copy-start | bytes 196
  120.5 8.0 %copy-start.44 = (pred[16]{0:T(512)(128)(4,1)S(1)}, pred[16]{0:T(512)(128)(4,1)}, u32[]{:S(2)}) copy-start(pred[16]{0:T(512)(128)(4,1)} %get-tuple-element.92) | copy-start | bytes 52
  120.5 8.0 %copy-start.45 = (pred[16]{0:T(512)(128)(4,1)S(1)}, pred[16]{0:T(512)(128)(4,1)}, u32[]{:S(2)}) copy-start(pred[16]{0:T(512)(128)(4,1)} %get-tuple-element.93) | copy-start | bytes 52
  161.8 10.5 %copy-start.31 = (f32[16,256]{1,0:T(8,128)S(1)}, f32[16,256]{1,0:T(8,128)}, u32[]{:S(2)}) copy-start(f32[16,256]{1,0:T(8,128)} %get-tuple-element.44) | copy-start | bytes 49156
  161.9 10.6 %copy-start.48 = (f32[128]{0:T(128)S(1)}, f32[128]{0:T(128)}, u32[]{:S(2)}) copy-start(f32[128]{0:T(128)} %iota_subtract_fusion.2) | copy-start | bytes 1540
  178.9 2.9 %copy-start.30 = (f32[16,256]{1,0:T(8,128)S(1)}, f32[16,256]{1,0:T(8,128)}, u32[]{:S(2)}) copy-start(f32[16,256]{1,0:T(8,128)} %get-tuple-element.43) | copy-start | bytes 49156
  178.9 3.0 %copy-start.27 = (f32[16,16]{1,0:T(8,128)S(1)}, f32[16,16]{1,0:T(8,128)}, u32[]{:S(2)}) copy-start(f32[16,16]{1,0:T(8,128)} %copy-done.26) | copy-start | bytes 3076
  181.9 3.2 %copy-start.13 = (bf16[1024,256]{0,1:T(8,128)(2,1)S(1)}, bf16[1024,256]{0,1:T(8,128)(2,1)}, u32[]{:S(2)}) copy-start(bf16[1024,256]{0,1:T(8,128)(2,1)} %copy.147) | copy-start | bytes 1572868
  184.7 1.6 copy-start.1
  184.7 1.6 copy-start.3
  186.3 1.0 copy-start.6
  186.3 3.8 %copy-start.16 = (bf16[1024,256]{0,1:T(8,128)(2,1)S(1)}, bf16[1024,256]{0,1:T(8,128)(2,1)}, u32[]{:S(2)}) copy-start(bf16[1024,256]{0,1:T(8,128)(2,1)} %get-tuple-element.60) | copy-start | bytes 1572868
  186.3 16.6 %copy-start.2 = (f32[1,1024,256]{1,2,0:T(8,128)S(1)}, f32[1,1024,256]{1,2,0:T(8,128)}, u32[]{:S(2)}) copy-start(f32[1,1024,256]{1,2,0:T(8,128)} %get-tuple-element.53) | copy-start | bytes 3145732
  186.3 16.6 %copy-start.4 = (f32[1,1024,256]{1,2,0:T(8,128)S(1)}, f32[1,1024,256]{1,2,0:T(8,128)}, u32[]{:S(2)}) copy-start(f32[1,1024,256]{1,2,0:T(8,128)} %get-tuple-element.54) | copy-start | bytes 3145732
  187.3 15.5 %collective-permute-start.1 = (f32[3,2,256]{1,2,0:T(8,128)S(1)}, f32[3,2,256]{1,2,0:T(8,128)S(1)}, u32[]{:S(2)}, u32[]{:S(2)}) collective-permute-start(f32[3,2,256]{1,2,0:T(8,128)S(1)} %slice.144), channel_id=1, source_target_pairs={{1,0},{2,1},{3,2},{4,3},{5,4},{6,5},{7,6},{8,7},{9,8},{10,9},{11,1... | collective-permute-start | bytes 18440 | tf_op jit(solution)/shard_map/ppermute | solution.py:66
  191.1 13.2 %copy-start.7 = (f32[1,1024,256]{1,2,0:T(8,128)S(1)}, f32[1,1024,256]{1,2,0:T(8,128)}, u32[]{:S(2)}) copy-start(f32[1,1024,256]{1,2,0:T(8,128)} %copy-done.6) | copy-start | bytes 3145732
  191.1 13.2 %copy-start.34 = (f32[3,256]{1,0:T(4,128)S(1)}, f32[3,256]{1,0:T(4,128)}, u32[]{:S(2)}) copy-start(f32[3,256]{1,0:T(4,128)} %get-tuple-element.84) | copy-start | bytes 9220
  191.1 13.2 %copy-start.35 = (f32[3,256]{1,0:T(4,128)S(1)}, f32[3,256]{1,0:T(4,128)}, u32[]{:S(2)}) copy-start(f32[3,256]{1,0:T(4,128)} %get-tuple-element.85) | copy-start | bytes 9220
  191.1 13.3 %copy-start.36 = (f32[3,1,256]{2,0,1:T(4,128)S(1)}, f32[3,1,256]{2,0,1:T(4,128)}, u32[]{:S(2)}) copy-start(f32[3,1,256]{2,0,1:T(4,128)} %copy.224) | copy-start | bytes 9220
  (3 other events, 2.1 us)
where the time goes:
time: 212 us; the launch traced here: 210 us
  Pallas kernels  60 us (28%)
  other arithmetic  58.1 us (27%)
  local copies, waits for them, and re-layouts  54.3 us (26%)
  matrix products  18.4 us (9%)
  waiting for transfers between devices  11.7 us (6%)
  starting transfers between devices  5.81 us (3%)
    pallas_call x2, Pallas kernels, gather_along(): pl.pallas_call(functools.partial(gather_kernel, axis, count), out_shape=j...  60 us
    unnamed x114, local copies, waits for them, and re-layouts  19 us
    ppermute x2, waiting for transfers between devices, passed_along(): lax.ppermute(value, axis, [(source, source + steps) for source in range(l...  11.7 us
    reduce_sum x1, other arithmetic, per_device(): first_in = jnp.sum(pair_mask * gram_acc[:, None], axis=(2, 3))  9.43 us
    ppermute x2, starting transfers between devices, passed_along(): lax.ppermute(value, axis, [(source, source + steps) for source in range(l...  5.81 us
    reduce_sum x1, other arithmetic, per_device(): jnp.sum(span_weight * (fresh_fwd[1][None] - block_len * block_steps * fre...  5.78 us
    reduce_sum x1, other arithmetic, per_device(): jnp.sum(jnp.swapaxes(span_weight, 0, 1) * fresh_bwd[None], axis=1)  5.23 us
    add x1, other arithmetic, short_conv(): summed + taps_table[:, offset, None, :] * row_data[:, start_row:start_row...  4.8 us
  transfers between devices with their start and end apart: 2, of which 1 were waited for; matrix products, arithmetic and copies ran while one was open for 9% of the time, Pallas kernels for 0%

commit v1 on v0

--- a/solution.py
+++ b/solution.py
@@ -58,6 +58,73 @@
         ],
         compiler_params=pltpu.CompilerParams(collective_id=collective_id, has_side_effects=True),
     )(value)
+
+
+def finish_kernel(
+    fsdp_count, ctx_count, tile_ref, rim_ref, tiles_out, rim_out, tiles_held, rim_held,
+    send_sem, recv_sem, rim_send_sem, rim_recv_sem,
+):
+    f_me = lax.axis_index("fsdp")
+    c_me = lax.axis_index("ctx")
+    left = lax.rem(c_me + ctx_count - 1, ctx_count)
+    right = lax.rem(c_me + 1, ctx_count)
+    barrier = pltpu.get_barrier_semaphore()
+    for step in range(1, fsdp_count):
+        peer = (lax.rem(f_me + step, fsdp_count), c_me)
+        pl.semaphore_signal(barrier, inc=1, device_id=peer, device_id_type=MESH)
+    for side in (left, right):
+        pl.semaphore_signal(barrier, inc=1, device_id=(f_me, side), device_id_type=MESH)
+    pl.semaphore_wait(barrier, fsdp_count + 1)
+    rim_copy = pltpu.make_async_remote_copy(
+        src_ref=rim_ref,
+        dst_ref=rim_held,
+        send_sem=rim_send_sem,
+        recv_sem=rim_recv_sem,
+        device_id=(f_me, left),
+        device_id_type=MESH,
+    )
+    rim_copy.start()
+    copies = []
+    for step in range(1, fsdp_count):
+        copy = pltpu.make_async_remote_copy(
+            src_ref=tile_ref,
+            dst_ref=tiles_held.at[f_me],
+            send_sem=send_sem.at[step - 1],
+            recv_sem=recv_sem.at[step - 1],
+            device_id=(lax.rem(f_me + step, fsdp_count), c_me),
+            device_id_type=MESH,
+        )
+        copy.start()
+        copies.append(copy)
+    for copy in copies:
+        copy.wait()
+    rim_copy.wait()
+    tiles_held[f_me] = tile_ref[...]
+    tiles_out[...] = tiles_held[...]
+    rim_out[...] = rim_held[...]
+
+
+def finish_exchange(tile, rim):
+    fsdp_count = lax.axis_size("fsdp")
+    ctx_count = lax.axis_size("ctx")
+    return pl.pallas_call(
+        functools.partial(finish_kernel, fsdp_count, ctx_count),
+        out_shape=(
+            jax.ShapeDtypeStruct((fsdp_count,) + tile.shape, tile.dtype),
+            jax.ShapeDtypeStruct(rim.shape, rim.dtype),
+        ),
+        in_specs=[pl.BlockSpec(memory_space=pltpu.VMEM)] * 2,
+        out_specs=(pl.BlockSpec(memory_space=pltpu.VMEM), pl.BlockSpec(memory_space=pltpu.VMEM)),
+        scratch_shapes=[
+            pltpu.VMEM((fsdp_count,) + tile.shape, tile.dtype),
+            pltpu.VMEM(rim.shape, rim.dtype),
+            pltpu.SemaphoreType.DMA((fsdp_count - 1,)),
+            pltpu.SemaphoreType.DMA((fsdp_count - 1,)),
+            pltpu.SemaphoreType.DMA(()),
+            pltpu.SemaphoreType.DMA(()),
+        ],
+        compiler_params=pltpu.CompilerParams(collective_id=1, has_side_effects=True),
+    )(tile, rim)
 
 
 def passed_along(value, axis, steps):
@@ -136,9 +203,12 @@
     first_acc = jnp.sum(moments[0] * start_states, axis=(0, 3))
     lag_acc = jnp.sum(moments[0] * start_lagged - moments[1] * start_states, axis=(0, 3))
     gram_acc = jnp.einsum("btgm,bsgm->gts", e_blocks, z_wide, precision=precise)
-    pair_mask = jnp.where(lag_index[None, None] >= 0, pair_pow, 0.0)
-    first_in = jnp.sum(pair_mask * gram_acc[:, None], axis=(2, 3))
-    lag_in = jnp.sum((pair_mask * lag_value[None, None]) * gram_acc[:, None], axis=(2, 3))
+    gram_low = jnp.where(lag_index[None] >= 0, gram_acc, 0.0)
+    gram_pair = jnp.stack([gram_low, gram_low * lag_value[None]])
+    rise_pow = jnp.exp(rate_axis * lag_axis)
+    gram_rise = jnp.einsum("kgts,gns->kgnt", gram_pair, rise_pow, precision=precise)
+    first_in = jnp.sum(block_pow * gram_rise[0], axis=2)
+    lag_in = jnp.sum(block_pow * gram_rise[1], axis=2)
     first_local = first_acc.T + first_in
     lag_local = lag_acc.T - lag_in
     inside_bwd = jnp.einsum("gts,btgm->bsgm", toeplitz, e_blocks, precision=precise)
@@ -157,15 +227,19 @@
     second_moment = jnp.sum(
         from_first * (moments[1] + block_len * block_ids[:, None, None, None] * moments[0]), axis=0
     )
-    local_states = jnp.stack([end_state, end_lagged, start_state]).reshape(3, order_count, channels)
     partial_rows = jnp.stack([first_local, lag_local]).reshape(-1, channels)
-    partial_slot = jnp.zeros((order_count, channels), jnp.float32)
-    partial_slot = partial_slot.at[: partial_rows.shape[0]].set(partial_rows)
-    local_states = jnp.concatenate(
-        [local_states, second_moment.reshape(1, order_count, channels), partial_slot[None]]
+    state_rows = jnp.stack([end_state, end_lagged, start_state, second_moment]).reshape(
+        4 * order_count, channels
+    )
+    payload_rows = -(-(state_rows.shape[0] + partial_rows.shape[0]) // 8) * 8
+    local_states = jnp.zeros((payload_rows, channels), jnp.float32)
+    local_states = local_states.at[: state_rows.shape[0]].set(state_rows)
+    local_states = local_states.at[state_rows.shape[0] : state_rows.shape[0] + partial_rows.shape[0]].set(
+        partial_rows
     )
     rate_cols = jnp.repeat(decay_rates.T, members, axis=1)
-    everyone = gather_along(local_states, "ctx", 0)
+    gathered = gather_along(local_states, "ctx", 0)
+    everyone = gathered[:, : state_rows.shape[0]].reshape(ctx_count, 4, order_count, channels)
     device_ids = jnp.arange(ctx_count, dtype=jnp.int32)
     ahead_steps = (ctx_index - 1 - device_ids).astype(jnp.float32)[:, None, None]
     behind_steps = (device_ids - ctx_index - 1).astype(jnp.float32)[:, None, None]
@@ -193,7 +267,7 @@
     cross_lag = jnp.sum(all_first * all_lagged - everyone[:, 3] * all_prev, axis=0)
     cross_first = cross_first.reshape(order_count, group_count, members).sum(axis=2).T
     cross_lag = cross_lag.reshape(order_count, group_count, members).sum(axis=2).T
-    gathered_parts = everyone[:, 4, : partial_rows.shape[0]].reshape(
+    gathered_parts = gathered[:, state_rows.shape[0] : state_rows.shape[0] + partial_rows.shape[0]].reshape(
         ctx_count, 2, group_count, order_count
     )
     local_totals = jnp.sum(gathered_parts, axis=0)
@@ -214,14 +288,16 @@
     mixer_output = (query_part * inner_flat).astype(jnp.bfloat16)
     grad_flat = product_grad.reshape(tokens, channels)
     feature_adj = jnp.stack([cotangent * inner_flat, grad_flat * value_part, grad_flat * key_part])
-    later_rows = passed_along(feature_adj[:, :rim_rows, :], "ctx", -1)
-    appended = jnp.concatenate([feature_adj, later_rows], axis=1)
-    feature_grads = short_conv(short_taps, appended, tokens, rim_rows, False).astype(jnp.bfloat16)
     filter_local = jnp.stack([gain_part, rate_part])
     entry_count = 2 * group_count * order_count * lax.axis_size("fsdp")
     summed = filter_local
     square_tile = jnp.full((8, 128), jnp.sum(summed * summed), jnp.float32)
-    squares = jnp.sum(gather_along(square_tile, "fsdp", 1)[:, 0, 0])
+    rim_send = feature_adj[:, :rim_rows, :].reshape(3 * rim_rows, channels)
+    square_tiles, rim_got = finish_exchange(square_tile, rim_send)
+    squares = jnp.sum(square_tiles[:, 0, 0])
+    later_rows = jnp.where(ctx_index == ctx_count - 1, 0.0, rim_got).reshape(3, rim_rows, channels)
+    appended = jnp.concatenate([feature_adj, later_rows], axis=1)
+    feature_grads = short_conv(short_taps, appended, tokens, rim_rows, False).astype(jnp.bfloat16)
     factor = jnp.minimum(1.0, lax.rsqrt(squares / entry_count + 1e-06))
     clipped = summed * factor
     return (mixer_output, feature_grads, clipped[0], clipped[1])

time: 212 us -> 195 us (0.920)
  waiting for transfers between devices: 11.7 us -> 0.01 us
  other arithmetic: 58.1 us -> 53.8 us
    pallas_call x0 -> x1, Pallas kernels: none -> 27.8 us  [finish_exchange(): pl.pallas_call(functools.partial(finish_kernel, fsdp_count, ctx_count), o...]
    pallas_call x2 -> x1, Pallas kernels: 60 us -> 32.6 us  [gather_along(): pl.pallas_call(functools.partial(gather_kernel, axis, count), out_shape=j...]
    ppermute x2 -> x1, waiting for transfers between devices: 11.7 us -> 0.01 us  [passed_along(): lax.ppermute(value, axis, [(source, source + steps) for source in range(l...]
    reduce_sum x4 -> x5, other arithmetic: 14.4 us -> 8.57 us  [the longest x1 4.31 us: per_device(): jnp.sum(mode_coefs[:, :, None, None] * pair_pow, axis=1)]
    unnamed x114 -> x116, local copies, waits for them, and re-layouts: 19 us -> 13.7 us
    another operation x2, other arithmetic: 1.62 us -> 5.25 us  [per_device(): jnp.stack([cotangent * inner_flat, grad_flat * value_part, grad_flat * ke...]
    slice x1 -> x3, local copies, waits for them, and re-layouts: 0.05 us -> 3.16 us  [the longest x1 2.36 us: per_device(): gathered[:, :state_rows.shape[0]]]
    ppermute x2 -> x1, starting transfers between devices: 5.81 us -> 4.38 us  [passed_along(): lax.ppermute(value, axis, [(source, source + steps) for source in range(l...]
  transfers between devices with their start and end apart: 2 -> 1, of which waited for: 1 -> 0; matrix products, arithmetic and copies ran while one was open for 9% -> 8% of each run, Pallas kernels for 0% -> 0%
where the time goes in v1:
time: 195 us; the launch traced here: 194 us
  Pallas kernels  60.4 us (31%)
  local copies, waits for them, and re-layouts  54.8 us (28%)
  other arithmetic  53.8 us (28%)
  matrix products  18.5 us (9%)
  starting transfers between devices  4.38 us (2%)
  between operations  2.02 us (1%)
    pallas_call x1, Pallas kernels, gather_along(): pl.pallas_call(functools.partial(gather_kernel, axis, count), out_shape=j...  32.6 us
    pallas_call x1, Pallas kernels, finish_exchange(): pl.pallas_call(functools.partial(finish_kernel, fsdp_count, ctx_count), o...  27.8 us
    unnamed x116, local copies, waits for them, and re-layouts  13.7 us
    reduce_sum x1, other arithmetic, per_device(): jnp.sum(span_weight * (fresh_fwd[1][None] - block_len * block_steps * fre...  5.91 us
    another operation x2, other arithmetic, per_device(): jnp.stack([cotangent * inner_flat, grad_flat * value_part, grad_flat * ke...  5.25 us
    reduce_sum x1, other arithmetic, per_device(): jnp.sum(jnp.swapaxes(span_weight, 0, 1) * fresh_bwd[None], axis=1)  5.17 us
    add x1, other arithmetic, short_conv(): summed + taps_table[:, offset, None, :] * row_data[:, start_row:start_row...  4.79 us
    ppermute x1, starting transfers between devices, passed_along(): lax.ppermute(value, axis, [(source, source + steps) for source in range(l...  4.38 us
  transfers between devices with their start and end apart: 1, of which 0 were waited for; matrix products, arithmetic and copies ran while one was open for 8% of the time, Pallas kernels for 0%

profile of v1, /device:TPU:1, one launch (start us, length us, event | category | flops | bytes accessed | tf_op | source)
XLA Modules:
  0.0 193.8 jit_solution(10142724212735978549)
XLA Ops:
  1.7 4.4 %collective-permute-start = (bf16[3,2,256]{1,2,0:T(8,128)(2,1)S(1)}, bf16[3,2,256]{1,2,0:T(8,128)(2,1)S(1)}, u32[]{:S(2)}, u32[]{:S(2)}) collective-permute-start(bf16[3,2,256]{1,2,0:T(8,128)(2,1)S(1)} %copy.142), channel_id=1, source_target_pairs={{0,1},{1,2},{2,3},{3,4},{4,5},{5,6},{6,7},{7,8},{8,9},{9,10},{10,1... | collective-permute-start | bytes 9224 | tf_op jit(solution)/shard_map/ppermute | solution.py:133
  11.7 1.0 select_bitcast_fusion
  12.8 1.0 exponential_select_fusion.1
  15.2 1.4 copy.144
  16.6 1.7 copy.141
  21.1 1.0 copy.155
  22.7 4.8 %multiply_add_fusion = f32[3,1024,256]{1,2,0:T(8,128)S(1)} fusion(bf16[3,1024,256]{1,2,0:T(8,128)(2,1)} %copy.141, bf16[3,2,256]{1,2,0:T(8,128)(2,1)} %copy-done.22, f32[3,256]{1,0:T(4,128)S(1)} %get-tuple-element.100, f32[3,256]{1,0:T(4,128)S(1)} %get-tuple-element.101, f32[3,256]{1,0:T(4,128)} %bitcast.236), kind=kLoop, calls=%fused_computation.14 | loop fusion | flops 11010048 | bytes 4730880 | tf_op jit(solution)/shard_map/add | solution.py:141
  29.6 1.9 fusion.9
  33.1 1.6 slice_bitcast_fusion.3
  34.6 1.0 multiply_reduce_fusion.10
  35.7 2.6 %copy.153 = f32[8,16,16,16]{3,2,1,0:T(8,128)} copy(f32[8,16,16,16]{1,3,0,2:T(8,128)} %get-tuple-element.70) | data formatting | bytes 262144 | tf_op jit(solution)/shard_map/mul | solution.py:198
  38.3 2.6 %copy.163 = f32[8,16,16,16]{3,2,1,0:T(8,128)} copy(f32[8,16,16,16]{1,3,0,2:T(8,128)} %get-tuple-element.71) | data formatting | bytes 262144 | tf_op jit(solution)/shard_map/squeeze | solution.py:223
  40.8 5.9 %multiply_reduce_fusion.2 = (f32[8,16,16,16]{3,2,1,0:T(8,128)}, f32[8,16,16,16]{3,2,1,0:T(8,128)}) fusion(f32[8,8]{1,0:T(8,128)S(1)} %copy-done.39, f32[8,16,16,16]{3,2,1,0:T(8,128)} %copy.163, f32[8,16,16,16]{3,2,1,0:T(8,128)} %copy.153, f32[8,8,16,16]{3,2,1,0:T(8,128)} %exponential_select_fusion.1), kind=kLoop, calls=%fused_computation.2 | loop fusion | flops 1507328 | bytes 590080 | tf_op jit(solution)/shard_map/reduce_sum | solution.py:199
  46.7 2.7 %copy.165 = f32[8,16,16,16]{1,3,0,2:T(8,128)} copy(f32[8,16,16,16]{3,2,1,0:T(8,128)} %get-tuple-element.53) | data formatting | bytes 262144 | tf_op jit(solution)/shard_map/reduce_sum | solution.py:199
  49.4 2.6 %copy.169 = f32[8,16,16,16]{1,3,0,2:T(8,128)} copy(f32[8,16,16,16]{3,2,1,0:T(8,128)} %get-tuple-element.54) | data formatting | bytes 262144 | tf_op jit(solution)/shard_map/reduce_sum | solution.py:198
  52.0 3.4 %convolution_bitcast_fusion = f32[2,8,16,16,16]{2,4,1,3,0:T(8,128)S(1)} fusion(f32[8,128,16,16]{1,0,3,2:T(8,128)} %bitcast.220, f32[1,16,16,128]{3,2,0,1:T(8,128)S(1)} %copy-done.18, f32[1,16,16,128]{3,2,0,1:T(8,128)S(1)} %copy-done.17), kind=kOutput, calls=%fused_computation.20 | convolution fusion | flops 100728832 | bytes 1572864 | tf_op jit(solution)/shard_map/kgnt,btgm->kbngm/dot_general | solution.py:202
  55.5 3.4 %multiply_reduce_fusion.6 = (f32[16,16]{0,1:T(8,128)S(1)}, f32[16,16]{0,1:T(8,128)S(1)}, f32[16,16,16]{0,2,1:T(8,128)S(1)}, f32[16,16,16]{0,2,1:T(8,128)S(1)}, f32[8,16,16,16]{1,3,0,2:T(8,128)}) fusion(f32[8,16,16,16]{1,3,0,2:T(8,128)S(1)} %copy-done.6, f32[2,8,16,16,16]{2,4,1,3,0:T(8,128)S(1)} %convolution_bitcast_fusion, ...), kind=kOutput, calls=%fused_computation.54 | convolution fusion | flops 50748928 | bytes 1748000 | tf_op jit(solution)/shard_map/gnt,btgm->bngm/dot_general | solution.py:215
  59.5 1.4 stack.70
  60.8 1.3 bitcast_subtract_fusion
  62.9 1.8 pad_maximum_fusion.4
  64.7 2.1 %copy.159 = f32[4,16,16,16]{3,2,1,0:T(8,128)} copy(f32[4,16,16,16]{1,3,2,0:T(8,128)} %pad_maximum_fusion.4) | data formatting | bytes 131072 | tf_op jit(solution)/shard_map/stack | solution.py:231
  66.9 1.3 reshape.445
  69.5 32.6 %shard_map.84 = f32[16,72,256]{2,1,0:T(8,128)} custom-call(f32[72,256]{1,0:T(8,128)} %copy-done.19), custom_call_target="tpu_custom_call" | custom-call | tf_op jit(solution)/shard_map/pallas_call | solution.py:49
  103.0 2.4 %slice.150 = f32[16,64,256]{2,1,0:T(8,128)} slice(f32[16,72,256]{2,1,0:T(8,128)} %shard_map.84), slice={[0:16], [0:64], [0:256]} | slice | bytes 2097152 | tf_op jit(solution)/shard_map/slice | solution.py:242
  106.9 1.2 slice_bitcast_fusion.8
  108.1 2.2 %multiply_reduce_fusion.4 = (f32[16,16,256]{2,1,0:T(8,128)S(1)}, f32[16,16,256]{2,1,0:T(8,128)S(1)}) fusion(f32[16,16]{1,0:T(8,128)S(1)} %copy-done.42, f32[16,16,256]{2,1,0:T(8,128)S(1)} %get-tuple-element.75, f32[16,16,256]{2,1,0:T(8,128)S(1)} %get-tuple-element.74, f32[16,16]{1,0:T(8,128)S(1)} %copy-done.41, f32[16,256]{1,0:T(8,128)S(1)} %copy-done.26, ...), kind=kLoop, calls=%fused_computation.4 | loop fusion | flops 8257536 | bytes 1067264 | tf_op jit(solution)/shard_map/reduce_sum | solution.py:262
  111.6 1.4 multiply_bitcast_fusion.1
  113.1 4.3 %multiply_reduce_fusion = f32[16,128,128]{2,1,0:T(8,128)S(1)} fusion(f32[128,128]{1,0:T(8,128)S(1)} %copy-done.21, f32[16,16]{1,0:T(8,128)S(1)} %get-tuple-element.94, f32[16,16]{1,0:T(8,128)S(1)} %copy.146), kind=kLoop, calls=%fused_computation | loop fusion | flops 12320768 | bytes 1116160 | tf_op jit(solution)/shard_map/reduce_sum | solution.py:183
  117.4 2.2 %fusion.15 = f32[16,8,16,128]{3,2,1,0:T(8,128)} fusion(f32[16,128,128]{2,1,0:T(8,128)S(1)} %multiply_reduce_fusion, f32[8,128,16,16]{1,0,3,2:T(8,128)S(1)} %bitcast.222, pred[128,128]{1,0:T(8,128)(4,1)S(1)} %copy-done.24), kind=kOutput, calls=%fused_computation.43 | convolution fusion | flops 402915328 | bytes 3162112 | tf_op jit(solution)/shard_map/gts,btgm->bsgm/dot_general | solution.py:214
  119.6 1.9 fusion.17
  121.5 2.6 %copy.174 = f32[8,16,16,16]{3,2,1,0:T(8,128)} copy(f32[8,16,16,16]{1,3,0,2:T(8,128)} %get-tuple-element.99) | data formatting | bytes 262144 | tf_op jit(solution)/shard_map/gnt,btgm->bngm/transpose | solution.py:215
  124.1 5.2 %multiply_reduce_fusion.1 = f32[8,16,16,16]{3,2,1,0:T(8,128)} fusion(f32[8,16,16,16]{3,2,1,0:T(8,128)} %copy.174, f32[8,8,16,16]{3,2,1,0:T(8,128)} %select_bitcast_fusion), kind=kLoop, calls=%fused_computation.1 | loop fusion | flops 491520 | bytes 327680 | tf_op jit(solution)/shard_map/reduce_sum | solution.py:216
  129.3 2.6 %copy.177 = f32[8,16,16,16]{1,3,0,2:T(8,128)} copy(f32[8,16,16,16]{3,2,1,0:T(8,128)} %multiply_reduce_fusion.1) | data formatting | bytes 262144 | tf_op jit(solution)/shard_map/reduce_sum | solution.py:216
  132.9 2.9 %fusion.7 = f32[8,128,16,16]{1,3,0,2:T(8,128)S(1)} fusion(f32[16,8,16,128]{3,2,1,0:T(8,128)} %fusion.17, f32[8,16,16,16]{1,3,0,2:T(8,128)} %copy.169, f32[16,16,16]{0,2,1:T(8,128)S(1)} %bitcast.231, f32[8,16,16]{1,0,2:T(8,128)S(1)} %get-tuple-element.89, f32[16,16]{1,0:T(8,128)} %copy-done.27, f32[16,16]{1,0:T(8,128)S(1)} %copy.146, ...), kind=kOutput, calls=%fused_computation.28 | convolution fusion | flops 50757632 | bytes 2255872 | tf_op jit(solution)/shard_map/gnt,bngm->btgm/dot_general | solution.py:281
  135.7 1.3 copy.171
  137.0 1.2 fusion.6
  138.2 1.3 copy.178
  139.5 2.4 %reshape_reshape.12 = f32[1,1024,256]{1,2,0:T(8,128)} reshape(f32[8,128,16,16]{1,0,3,2:T(8,128)} %copy.178) | data formatting | bytes 2097152 | tf_op jit(solution)/shard_map/reshape;reshape | solution.py:289
  141.9 3.0 %fusion.13 = (f32[1,1024,256]{1,2,0:T(8,128)}, bf16[1024,256]{0,1:T(8,128)(2,1)}) fusion(bf16[1024,256]{0,1:T(8,128)(2,1)} %copy.155, f32[32,8,8,128]{3,2,1,0:T(8,128)} %bitcast.229, f32[3,1024,256]{1,2,0:T(8,128)S(1)} %multiply_add_fusion), kind=kLoop, calls=%fused_computation.35 | loop fusion | flops 1048576 | bytes 4194304 | tf_op jit(solution)/shard_map/stack | solution.py:290
  144.9 1.7 slice_multiply_fusion.2
  146.6 2.0 %copy.185 = bf16[1024,256]{1,0:T(8,128)(2,1)} copy(bf16[1024,256]{0,1:T(8,128)(2,1)} %get-tuple-element.73) | data formatting | bytes 1048576
  148.7 2.2 %pad_maximum_fusion.1 = f32[3,1024,256]{1,2,0:T(8,128)S(1)} fusion(f32[1,1024,256]{1,2,0:T(8,128)} %get-tuple-element.69, f32[1,1024,256]{1,2,0:T(8,128)} %get-tuple-element.68, f32[1,1024,256]{1,2,0:T(8,128)} %get-tuple-element.72), kind=kLoop, calls=%fused_computation.13 | loop fusion | flops 1572864 | bytes 6291456 | tf_op jit(solution)/shard_map/stack | solution.py:290
  151.7 1.3 reshape.449.rim_ref
  153.6 1.2 broadcast_in_dim.116.tile_ref
  154.9 27.8 %shard_map.85 = (f32[32,8,128]{2,1,0:T(8,128)}, f32[6,256]{1,0:T(8,128)}) custom-call(f32[8,128]{1,0:T(8,128)} %broadcast_in_dim.116.tile_ref, f32[6,256]{1,0:T(8,128)} %reshape.449.rim_ref), custom_call_target="tpu_custom_call" | custom-call | tf_op jit(solution)/shard_map/pallas_call | solution.py:110
  182.7 1.5 slice_reduce_fusion.1
  187.9 3.3 %fusion.1 = bf16[3,1024,256]{1,2,0:T(8,128)(2,1)} fusion(f32[3,1026,256]{1,2,0:T(8,128)S(1)} %pad_maximum_fusion, f32[3,256]{1,0:T(4,128)S(1)} %copy-done.33, f32[3,256]{1,0:T(4,128)S(1)} %copy-done.35, f32[3,256]{1,0:T(4,128)S(1)} %bitcast.237, f32[1,1024,256]{1,2,0:T(8,128)S(1)} %copy-done.1, f32[1,1024,256]{1,2,0:T(8,128)S(1)} %copy-done, ...), kind=kLoop, calls=%fused_computation.10 | loop fusion | flops 6291456 | bytes 11019264 | tf_op jit(solution)/shard_map/convert_element_type | solution.py:300
  191.3 2.6 %copy.186 = bf16[3,1024,256]{2,1,0:T(8,128)(2,1)} copy(bf16[3,1024,256]{1,2,0:T(8,128)(2,1)} %fusion.1) | data formatting | bytes 3145728
  (173 shorter events, 26.8 us)
Async XLA Ops:
  0.6 15.9 %copy-start.15 = (bf16[3,1024,256]{2,1,0:T(8,128)(2,1)S(1)}, bf16[3,1024,256]{2,1,0:T(8,128)(2,1)}, u32[]{:S(2)}) copy-start(bf16[3,1024,256]{2,1,0:T(8,128)(2,1)} %param.9) | copy-start | bytes 4718596
  0.6 18.3 %copy-start.40 = (f32[16,16]{1,0:T(8,128)S(1)}, f32[16,16]{1,0:T(8,128)}, u32[]{:S(2)}) copy-start(f32[16,16]{1,0:T(8,128)} %param.12) | copy-start | bytes 3076
  0.7 20.4 %copy-start.16 = (bf16[1024,256]{1,0:T(8,128)(2,1)S(1)}, bf16[1024,256]{1,0:T(8,128)(2,1)}, u32[]{:S(2)}) copy-start(bf16[1024,256]{1,0:T(8,128)(2,1)} %param.13) | copy-start | bytes 1572868
  1.7 20.3 %collective-permute-start = (bf16[3,2,256]{1,2,0:T(8,128)(2,1)S(1)}, bf16[3,2,256]{1,2,0:T(8,128)(2,1)S(1)}, u32[]{:S(2)}, u32[]{:S(2)}) collective-permute-start(bf16[3,2,256]{1,2,0:T(8,128)(2,1)S(1)} %copy.142), channel_id=1, source_target_pairs={{0,1},{1,2},{2,3},{3,4},{4,5},{5,6},{6,7},{7,8},{8,9},{9,10},{10,1... | collective-permute-start | bytes 9224 | tf_op jit(solution)/shard_map/ppermute | solution.py:133
  7.3 12.3 %copy-start.43 = (f32[8]{0:T(128)}, f32[8]{0:T(128)S(1)}, u32[]{:S(2)}) copy-start(f32[8]{0:T(128)S(1)} %get-tuple-element.105) | copy-start | bytes 100
  7.3 12.3 %copy-start.49 = (f32[8]{0:T(128)}, f32[8]{0:T(128)S(1)}, u32[]{:S(2)}) copy-start(f32[8]{0:T(128)S(1)} %get-tuple-element.104) | copy-start | bytes 100
  11.6 8.0 %copy-start.27 = (f32[16,16]{1,0:T(8,128)}, f32[16,16]{1,0:T(8,128)S(1)}, u32[]{:S(2)}) copy-start(f32[16,16]{1,0:T(8,128)S(1)} %get-tuple-element.92) | copy-start | bytes 3076
  12.7 14.8 %copy-start.32 = (f32[3,256]{1,0:T(4,128)}, f32[3,256]{1,0:T(4,128)S(1)}, u32[]{:S(2)}) copy-start(f32[3,256]{1,0:T(4,128)S(1)} %get-tuple-element.100) | copy-start | bytes 9220
  12.7 14.8 %copy-start.34 = (f32[3,256]{1,0:T(4,128)}, f32[3,256]{1,0:T(4,128)S(1)}, u32[]{:S(2)}) copy-start(f32[3,256]{1,0:T(4,128)S(1)} %get-tuple-element.101) | copy-start | bytes 9220
  20.4 1.6 copy-start.25
  22.7 5.1 %copy-start.10 = (bf16[1024,256]{0,1:T(8,128)(2,1)S(1)}, bf16[1024,256]{0,1:T(8,128)(2,1)}, u32[]{:S(2)}) copy-start(bf16[1024,256]{0,1:T(8,128)(2,1)} %copy.155) | copy-start | bytes 1572868
  27.7 0.7 copy-start.23
  27.9 4.4 %copy-start.8 = (bf16[32,8,8,128]{3,2,1,0:T(8,128)(2,1)}, bf16[32,8,8,128]{3,2,1,0:T(8,128)(2,1)S(1)}, u32[]{:S(2)}) copy-start(bf16[32,8,8,128]{3,2,1,0:T(8,128)(2,1)S(1)} %copy.211) | copy-start | bytes 1572868
  28.2 1.2 copy-start.2
  28.5 1.0 copy-start.20
  28.5 1.1 copy-start.28
  32.3 2.4 %copy-start.50 = (f32[8]{0:T(128)S(1)}, f32[8]{0:T(128)}, u32[]{:S(2)}) copy-start(f32[8]{0:T(128)} %copy-done.49) | copy-start | bytes 100
  34.6 6.2 %copy-start.39 = (f32[8,8]{1,0:T(8,128)S(1)}, f32[8,8]{1,0:T(8,128)}, u32[]{:S(2)}) copy-start(f32[8,8]{1,0:T(8,128)} %copy.164) | copy-start | bytes 772
  46.7 5.3 %copy-start.17 = (f32[1,16,16,128]{3,2,0,1:T(8,128)S(1)}, f32[1,16,16,128]{3,2,0,1:T(8,128)}, u32[]{:S(2)}) copy-start(f32[1,16,16,128]{3,2,0,1:T(8,128)} %get-tuple-element.81) | copy-start | bytes 393220
  46.7 5.3 %copy-start.18 = (f32[1,16,16,128]{3,2,0,1:T(8,128)S(1)}, f32[1,16,16,128]{3,2,0,1:T(8,128)}, u32[]{:S(2)}) copy-start(f32[1,16,16,128]{3,2,0,1:T(8,128)} %get-tuple-element.82) | copy-start | bytes 393220
  52.0 3.4 %copy-start.3 = (f32[32,8,8,128]{3,2,1,0:T(8,128)S(1)}, f32[32,8,8,128]{3,2,1,0:T(8,128)}, u32[]{:S(2)}) copy-start(f32[32,8,8,128]{3,2,1,0:T(8,128)} %copy-done.2) | copy-start | bytes 3145732
  52.0 3.4 %copy-start.6 = (f32[8,16,16,16]{1,3,0,2:T(8,128)S(1)}, f32[8,16,16,16]{1,3,0,2:T(8,128)}, u32[]{:S(2)}) copy-start(f32[8,16,16,16]{1,3,0,2:T(8,128)} %copy.169) | copy-start | bytes 393220
  52.0 3.4 %copy-start.14 = (f32[8,16,16,16]{1,3,0,2:T(8,128)S(1)}, f32[8,16,16,16]{1,3,0,2:T(8,128)}, u32[]{:S(2)}) copy-start(f32[8,16,16,16]{1,3,0,2:T(8,128)} %copy.165) | copy-start | bytes 393220
  55.4 3.4 %copy-start.37 = (f32[16,16]{1,0:T(8,128)S(1)}, f32[16,16]{1,0:T(8,128)}, u32[]{:S(2)}) copy-start(f32[16,16]{1,0:T(8,128)} %get-tuple-element.63) | copy-start | bytes 3076
  64.7 43.3 %copy-start.26 = (f32[16,256]{1,0:T(8,128)S(1)}, f32[16,256]{1,0:T(8,128)}, u32[]{:S(2)}) copy-start(f32[16,256]{1,0:T(8,128)} %copy-done.25) | copy-start | bytes 49156
  64.7 43.3 %copy-start.41 = (f32[16,16]{1,0:T(8,128)S(1)}, f32[16,16]{1,0:T(8,128)}, u32[]{:S(2)}) copy-start(f32[16,16]{1,0:T(8,128)} %get-tuple-element.95) | copy-start | bytes 3076
  64.7 43.4 %copy-start.42 = (f32[16,16]{1,0:T(8,128)S(1)}, f32[16,16]{1,0:T(8,128)}, u32[]{:S(2)}) copy-start(f32[16,16]{1,0:T(8,128)} %get-tuple-element.96) | copy-start | bytes 3076
  64.7 43.4 %copy-start.48 = (pred[16,16]{1,0:T(8,128)(4,1)S(1)}, pred[16,16]{1,0:T(8,128)(4,1)}, u32[]{:S(2)}) copy-start(pred[16,16]{1,0:T(8,128)(4,1)} %subtract_compare_fusion) | copy-start | bytes 772
  69.5 40.8 %copy-start.31 = (f32[16,256]{1,0:T(8,128)S(1)}, f32[16,256]{1,0:T(8,128)}, u32[]{:S(2)}) copy-start(f32[16,256]{1,0:T(8,128)} %exp.102) | copy-start | bytes 49156
  69.5 40.8 %copy-start.44 = (f32[16]{0:T(128)S(1)}, f32[16]{0:T(128)}, u32[]{:S(2)}) copy-start(f32[16]{0:T(128)} %get-tuple-element.106) | copy-start | bytes 196
  69.5 40.9 %copy-start.45 = (f32[16]{0:T(128)S(1)}, f32[16]{0:T(128)}, u32[]{:S(2)}) copy-start(f32[16]{0:T(128)} %get-tuple-element.107) | copy-start | bytes 196
  69.5 40.9 %copy-start.46 = (pred[16]{0:T(512)(128)(4,1)S(1)}, pred[16]{0:T(512)(128)(4,1)}, u32[]{:S(2)}) copy-start(pred[16]{0:T(512)(128)(4,1)} %get-tuple-element.108) | copy-start | bytes 52
  69.5 40.9 %copy-start.47 = (pred[16]{0:T(512)(128)(4,1)S(1)}, pred[16]{0:T(512)(128)(4,1)}, u32[]{:S(2)}) copy-start(pred[16]{0:T(512)(128)(4,1)} %get-tuple-element.109) | copy-start | bytes 52
  103.0 8.6 %copy-start.38 = (f32[16,16]{0,1:T(8,128)S(1)}, f32[16,16]{0,1:T(8,128)}, u32[]{:S(2)}) copy-start(f32[16,16]{0,1:T(8,128)} %copy.144) | copy-start | bytes 3076
  103.0 10.0 %copy-start.21 = (f32[128,128]{1,0:T(8,128)S(1)}, f32[128,128]{1,0:T(8,128)}, u32[]{:S(2)}) copy-start(f32[128,128]{1,0:T(8,128)} %maximum_convert_fusion) | copy-start | bytes 196612
  106.9 3.5 %copy-start.7 = (f32[16,64,256]{2,1,0:T(8,128)S(1)}, f32[16,64,256]{2,1,0:T(8,128)}, u32[]{:S(2)}) copy-start(f32[16,64,256]{2,1,0:T(8,128)} %slice.150) | copy-start | bytes 3145732
  113.1 4.3 %copy-start.4 = (f32[32,8,8,128]{3,2,1,0:T(8,128)S(1)}, f32[32,8,8,128]{3,2,1,0:T(8,128)}, u32[]{:S(2)}) copy-start(f32[32,8,8,128]{3,2,1,0:T(8,128)} %copy-done.2) | copy-start | bytes 3145732
  113.1 4.3 %copy-start.24 = (pred[128,128]{1,0:T(8,128)(4,1)S(1)}, pred[128,128]{1,0:T(8,128)(4,1)}, u32[]{:S(2)}) copy-start(pred[128,128]{1,0:T(8,128)(4,1)} %fusion.71) | copy-start | bytes 49156
  117.4 2.2 %copy-start.9 = (bf16[32,8,8,128]{3,2,1,0:T(8,128)(2,1)S(1)}, bf16[32,8,8,128]{3,2,1,0:T(8,128)(2,1)}, u32[]{:S(2)}) copy-start(bf16[32,8,8,128]{3,2,1,0:T(8,128)(2,1)} %copy-done.8) | copy-start | bytes 1572868
  132.8 4.2 %copy-start.11 = (f32[16,8,16,128]{3,2,1,0:T(8,128)S(1)}, f32[16,8,16,128]{3,2,1,0:T(8,128)}, u32[]{:S(2)}) copy-start(f32[16,8,16,128]{3,2,1,0:T(8,128)} %fusion.15) | copy-start | bytes 3145732
  132.8 4.2 %copy-start.13 = (f32[8,16,16,16]{1,3,0,2:T(8,128)S(1)}, f32[8,16,16,16]{1,3,0,2:T(8,128)}, u32[]{:S(2)}) copy-start(f32[8,16,16,16]{1,3,0,2:T(8,128)} %copy.177) | copy-start | bytes 393220
  132.8 4.2 %copy-start.51 = (f32[128]{0:T(128)S(1)}, f32[128]{0:T(128)}, u32[]{:S(2)}) copy-start(f32[128]{0:T(128)} %iota_subtract_fusion.2) | copy-start | bytes 1540
  141.9 3.0 %copy-start.12 = (f32[1,1024,256]{1,2,0:T(8,128)S(1)}, f32[1,1024,256]{1,2,0:T(8,128)}, u32[]{:S(2)}) copy-start(f32[1,1024,256]{1,2,0:T(8,128)} %reshape_reshape.12) | copy-start | bytes 3145732
  148.7 4.4 %copy-start.29 = (f32[1,16,16]{1,2,0:T(8,128)S(1)}, f32[1,16,16]{1,2,0:T(8,128)}, u32[]{:S(2)}) copy-start(f32[1,16,16]{1,2,0:T(8,128)} %get-tuple-element.76) | copy-start | bytes 3076
  148.7 4.4 %copy-start.30 = (f32[1,16,16]{1,2,0:T(8,128)S(1)}, f32[1,16,16]{1,2,0:T(8,128)}, u32[]{:S(2)}) copy-start(f32[1,16,16]{1,2,0:T(8,128)} %get-tuple-element.77) | copy-start | bytes 3076
  148.7 38.5 %copy-start = (f32[1,1024,256]{1,2,0:T(8,128)S(1)}, f32[1,1024,256]{1,2,0:T(8,128)}, u32[]{:S(2)}) copy-start(f32[1,1024,256]{1,2,0:T(8,128)} %get-tuple-element.68) | copy-start | bytes 3145732
  148.7 38.5 %copy-start.1 = (f32[1,1024,256]{1,2,0:T(8,128)S(1)}, f32[1,1024,256]{1,2,0:T(8,128)}, u32[]{:S(2)}) copy-start(f32[1,1024,256]{1,2,0:T(8,128)} %get-tuple-element.69) | copy-start | bytes 3145732
  148.7 38.6 %copy-start.5 = (f32[1,1024,256]{1,2,0:T(8,128)S(1)}, f32[1,1024,256]{1,2,0:T(8,128)}, u32[]{:S(2)}) copy-start(f32[1,1024,256]{1,2,0:T(8,128)} %get-tuple-element.72) | copy-start | bytes 3145732
  (5 other events, 3.4 us)

commit v2 on v1

--- a/solution.py
+++ b/solution.py
@@ -187,21 +187,28 @@
 
     z_wide = z_blocks.astype(jnp.float32)
     block_ids = jnp.arange(block_count, dtype=jnp.float32)
-    block_steps = (block_ids[:, None] - 1.0 - block_ids[None, :])[:, :, None, None, None]
+    rate_cols = jnp.repeat(decay_rates.T, members, axis=1)
+    block_steps = (block_ids[:, None] - 1.0 - block_ids[None, :])[:, :, None, None]
     span_weight = jnp.where(
         block_steps >= 0,
-        jnp.exp(-decay_rates.T[None, None, :, :, None] * (block_len * jnp.maximum(block_steps, 0.0))),
+        jnp.exp(-rate_cols[None, None] * (block_len * jnp.maximum(block_steps, 0.0))),
         0.0,
     )
     inside_fwd = jnp.einsum("gts,bsgm->btgm", toeplitz, z_wide, precision=threepass)
-    fresh_fwd = jnp.einsum("kgns,bsgm->kbngm", block_ends, z_wide, precision=threepass)
-    start_states = jnp.sum(span_weight * fresh_fwd[0][None], axis=1)
-    start_lagged = jnp.sum(
+    fresh_fwd = jnp.einsum("kgns,bsgm->kbngm", block_ends, z_wide, precision=threepass).reshape(
+        2, block_count, order_count, channels
+    )
+    start_flat = jnp.sum(span_weight * fresh_fwd[0][None], axis=1)
+    lagged_flat = jnp.sum(
         span_weight * (fresh_fwd[1][None] - block_len * block_steps * fresh_fwd[0][None]), axis=1
     )
-    moments = jnp.einsum("kgnt,btgm->kbngm", block_moments, e_blocks, precision=precise)
-    first_acc = jnp.sum(moments[0] * start_states, axis=(0, 3))
-    lag_acc = jnp.sum(moments[0] * start_lagged - moments[1] * start_states, axis=(0, 3))
+    moments = jnp.einsum("kgnt,btgm->kbngm", block_moments, e_blocks, precision=precise).reshape(
+        2, block_count, order_count, channels
+    )
+    first_acc = jnp.sum(moments[0] * start_flat, axis=0)
+    lag_acc = jnp.sum(moments[0] * lagged_flat - moments[1] * start_flat, axis=0)
+    first_acc = first_acc.reshape(order_count, group_count, members).sum(axis=2)
+    lag_acc = lag_acc.reshape(order_count, group_count, members).sum(axis=2)
     gram_acc = jnp.einsum("btgm,bsgm->gts", e_blocks, z_wide, precision=precise)
     gram_low = jnp.where(lag_index[None] >= 0, gram_acc, 0.0)
     gram_pair = jnp.stack([gram_low, gram_low * lag_value[None]])
@@ -212,21 +219,18 @@
     first_local = first_acc.T + first_in
     lag_local = lag_acc.T - lag_in
     inside_bwd = jnp.einsum("gts,btgm->bsgm", toeplitz, e_blocks, precision=precise)
-    fresh_bwd = jnp.einsum("gnt,btgm->bngm", block_pow, e_blocks, precision=precise)
-    later_states = jnp.sum(jnp.swapaxes(span_weight, 0, 1) * fresh_bwd[None], axis=1)
-    rates_ng = decay_rates.T[None, :, :, None]
-    from_first = jnp.exp(-rates_ng * (block_len * block_ids[:, None, None, None]))
-    from_last = jnp.exp(-rates_ng * (block_len * (block_count - 1.0 - block_ids[:, None, None, None])))
+    fresh_bwd = jnp.einsum("gnt,btgm->bngm", block_pow, e_blocks, precision=precise).reshape(
+        block_count, order_count, channels
+    )
+    later_flat = jnp.sum(jnp.swapaxes(span_weight, 0, 1) * fresh_bwd[None], axis=1)
+    first_ids = block_ids[:, None, None]
+    last_ids = block_count - 1.0 - block_ids[:, None, None]
+    from_first = jnp.exp(-rate_cols[None] * (block_len * first_ids))
+    from_last = jnp.exp(-rate_cols[None] * (block_len * last_ids))
     end_state = jnp.sum(from_last * fresh_fwd[0], axis=0)
-    end_lagged = jnp.sum(
-        from_last
-        * (fresh_fwd[1] - block_len * (block_count - 1.0 - block_ids[:, None, None, None]) * fresh_fwd[0]),
-        axis=0,
-    )
+    end_lagged = jnp.sum(from_last * (fresh_fwd[1] - block_len * last_ids * fresh_fwd[0]), axis=0)
     start_state = jnp.sum(from_first * fresh_bwd, axis=0)
-    second_moment = jnp.sum(
-        from_first * (moments[1] + block_len * block_ids[:, None, None, None] * moments[0]), axis=0
-    )
+    second_moment = jnp.sum(from_first * (moments[1] + block_len * first_ids * moments[0]), axis=0)
     partial_rows = jnp.stack([first_local, lag_local]).reshape(-1, channels)
     state_rows = jnp.stack([end_state, end_lagged, start_state, second_moment]).reshape(
         4 * order_count, channels
@@ -237,7 +241,6 @@
     local_states = local_states.at[state_rows.shape[0] : state_rows.shape[0] + partial_rows.shape[0]].set(
         partial_rows
     )
-    rate_cols = jnp.repeat(decay_rates.T, members, axis=1)
     gathered = gather_along(local_states, "ctx", 0)
     everyone = gathered[:, : state_rows.shape[0]].reshape(ctx_count, 4, order_count, channels)
     device_ids = jnp.arange(ctx_count, dtype=jnp.int32)
@@ -274,10 +277,9 @@
     first_total = local_totals[0] + cross_first
     lag_total = local_totals[1] + cross_lag
 
-    prev_grouped = prev_state.reshape(order_count, group_count, members)
-    next_grouped = next_state.reshape(order_count, group_count, members)
-    start_total = start_states + from_first * prev_grouped[None]
-    later_total = later_states + from_last * next_grouped[None]
+    grouped_shape = (block_count, order_count, group_count, members)
+    start_total = (start_flat + from_first * prev_state[None]).reshape(grouped_shape)
+    later_total = (later_flat + from_last * next_state[None]).reshape(grouped_shape)
     carried_fwd = jnp.einsum("gnt,bngm->btgm", coef_after, start_total, precision=precise)
     inner_sum = (inside_fwd + carried_fwd).reshape(tokens, group_count, members)
     carried_bwd = jnp.einsum("gns,bngm->bsgm", coef_tail, later_total, precision=precise)

time: 195 us -> 200 us (1.026)
  local copies, waits for them, and re-layouts: 54.8 us -> 67.7 us
  other arithmetic: 53.8 us -> 45 us
    slice x0 -> x3, local copies, waits for them, and re-layouts: none -> 6.73 us  [the longest x2 4.15 us: per_device(): start_flat = jnp.sum(span_weight * fresh_fwd[0][None], axis=1)]
    reduce_sum x1 -> x4, local copies, waits for them, and re-layouts: 2.61 us -> 7.86 us  [per_device(): start_flat = jnp.sum(span_weight * fresh_fwd[0][None], axis=1)]
    reduce_sum x2 -> x1, other arithmetic: 6.22 us -> 1.77 us  [per_device(): first_acc = first_acc.reshape(order_count, group_count, members).sum(axis=2)]
    another operation x2, other arithmetic: 5.25 us -> 1.62 us  [per_device(): jnp.stack([cotangent * inner_flat, grad_flat * value_part, grad_flat * ke...]
    reduce_sum x1, other arithmetic: 5.91 us -> 2.7 us  [per_device(): jnp.sum(span_weight * (fresh_fwd[1][None] - block_len * block_steps * fre...]
    unnamed x116 -> x112, local copies, waits for them, and re-layouts: 13.7 us -> 16.5 us
    squeeze x1 -> x0, local copies, waits for them, and re-layouts: 2.57 us -> none  [per_device(): fresh_fwd[1]]
    sub x0 -> x1, local copies, waits for them, and re-layouts: none -> 2.25 us  [per_device(): fresh_fwd[1][None] - block_len * block_steps * fresh_fwd[0][None]]
where the time goes in v2:
time: 200 us; the launch traced here: 199 us
  local copies, waits for them, and re-layouts  67.7 us (34%)
  Pallas kernels  60.4 us (30%)
  other arithmetic  45 us (22%)
  matrix products  19 us (10%)
  starting transfers between devices  4.38 us (2%)
  between operations  2.06 us (1%)
    pallas_call x1, Pallas kernels, gather_along(): pl.pallas_call(functools.partial(gather_kernel, axis, count), out_shape=j...  32.6 us
    pallas_call x1, Pallas kernels, finish_exchange(): pl.pallas_call(functools.partial(finish_kernel, fsdp_count, ctx_count), o...  27.8 us
    unnamed x112, local copies, waits for them, and re-layouts  16.5 us
    reduce_sum x4, local copies, waits for them, and re-layouts, per_device(): start_flat = jnp.sum(span_weight * fresh_fwd[0][None], axis=1)  7.86 us
    reduce_sum x2, local copies, waits for them, and re-layouts, per_device(): jnp.sum(span_weight * (fresh_fwd[1][None] - block_len * block_steps * fre...  4.81 us
    add x1, other arithmetic, short_conv(): summed + taps_table[:, offset, None, :] * row_data[:, start_row:start_row...  4.77 us
    reduce_sum x1, other arithmetic, per_device(): jnp.sum(mode_coefs[:, :, None, None] * pair_pow, axis=1)  4.53 us
    ppermute x1, starting transfers between devices, passed_along(): lax.ppermute(value, axis, [(source, source + steps) for source in range(l...  4.38 us
  transfers between devices with their start and end apart: 1, of which 0 were waited for; matrix products, arithmetic and copies ran while one was open for 8% of the time, Pallas kernels for 0%

profile of v2, /device:TPU:1, one launch (start us, length us, event | category | flops | bytes accessed | tf_op | source)
XLA Modules:
  0.0 198.6 jit_solution(11825138334882458429)
XLA Ops:
  1.6 4.4 %collective-permute-start = (bf16[3,2,256]{1,2,0:T(8,128)(2,1)S(1)}, bf16[3,2,256]{1,2,0:T(8,128)(2,1)S(1)}, u32[]{:S(2)}, u32[]{:S(2)}) collective-permute-start(bf16[3,2,256]{1,2,0:T(8,128)(2,1)S(1)} %copy.129), channel_id=1, source_target_pairs={{0,1},{1,2},{2,3},{3,4},{4,5},{5,6},{6,7},{7,8},{8,9},{9,10},{10,1... | collective-permute-start | bytes 9224 | tf_op jit(solution)/shard_map/ppermute | solution.py:133
  15.1 2.6 %copy.128 = bf16[3,1024,256]{1,2,0:T(8,128)(2,1)} copy(bf16[3,1024,256]{2,1,0:T(8,128)(2,1)} %param.9) | data formatting | bytes 3145728 | tf_op args[0]
  22.2 4.8 %multiply_add_fusion = f32[3,1024,256]{1,2,0:T(8,128)S(1)} fusion(bf16[3,1024,256]{1,2,0:T(8,128)(2,1)} %copy.128, bf16[3,2,256]{1,2,0:T(8,128)(2,1)} %copy-done.22, f32[3,256]{1,0:T(4,128)} %get-tuple-element.104, f32[3,256]{1,0:T(4,128)} %get-tuple-element.105, f32[3,256]{1,0:T(4,128)} %bitcast.212), kind=kLoop, calls=%fused_computation.11 | loop fusion | flops 11010048 | bytes 4730880 | tf_op jit(solution)/shard_map/add | solution.py:141
  28.9 1.3 copy-done
  30.2 1.6 fusion.91
  31.8 2.6 %copy.137 = f32[1,8,16,16,16]{4,3,2,1,0:T(8,128)} copy(f32[1,8,16,16,16]{2,4,0,1,3:T(8,128)} %get-tuple-element.72) | data formatting | bytes 262144 | tf_op jit(solution)/shard_map/slice | solution.py:201
  34.4 2.2 %mul.636 = f32[8,16,256]{2,1,0:T(8,128)} reshape(f32[1,8,16,16,16]{4,3,2,1,0:T(8,128)} %copy.137) | data formatting | bytes 262144 | tf_op jit(solution)/shard_map/mul | solution.py:201
  36.6 2.6 %copy.148 = f32[1,8,16,16,16]{4,3,2,1,0:T(8,128)} copy(f32[1,8,16,16,16]{2,4,0,1,3:T(8,128)} %get-tuple-element.73) | data formatting | bytes 262144 | tf_op jit(solution)/shard_map/slice | solution.py:231
  39.2 2.3 %sub.252 = f32[8,16,256]{2,1,0:T(8,128)} reshape(f32[1,8,16,16,16]{4,3,2,1,0:T(8,128)} %copy.148) | data formatting | bytes 262144 | tf_op jit(solution)/shard_map/sub | solution.py:203
  43.9 2.2 %multiply_reduce_fusion.7 = (f32[16,16,16]{0,2,1:T(8,128)S(1)}, f32[8,16,16,16]{1,3,0,2:T(8,128)}) fusion(f32[8]{0:T(128)S(1)} %copy-done.39, f32[16,16]{0,1:T(8,128)S(1)} %get-tuple-element.93, f32[16,16]{1,0:T(8,128)S(1)} %get-tuple-element.94, f32[8,128,16,16]{1,0,3,2:T(8,128)S(1)} %bitcast.194), kind=kOutput, calls=%fused_computation.53 | convolution fusion | flops 50458624 | bytes 1198112 | tf_op jit(solution)/shard_map/gnt,btgm->bngm/dot_general | solution.py:222
  46.0 2.6 %copy.157 = f32[8,16,16,16]{3,2,1,0:T(8,128)} copy(f32[8,16,16,16]{1,3,0,2:T(8,128)} %get-tuple-element.103) | data formatting | bytes 262144 | tf_op jit(solution)/shard_map/gnt,btgm->bngm/transpose | solution.py:222
  48.6 2.3 %mul.696 = f32[8,16,256]{2,1,0:T(8,128)} reshape(f32[8,16,16,16]{3,2,1,0:T(8,128)} %copy.157) | data formatting | bytes 262144 | tf_op jit(solution)/shard_map/mul | solution.py:225
  50.9 2.7 %multiply_reduce_fusion.4 = (f32[8,16,256]{2,1,0:T(8,128)}, f32[8,16,256]{2,1,0:T(8,128)S(1)}, f32[8,16,256]{2,1,0:T(8,128)}) fusion(f32[8,8]{1,0:T(8,128)} %get-tuple-element.100, f32[8,16,256]{2,1,0:T(8,128)} %sub.252, f32[8,16,256]{2,1,0:T(8,128)} %mul.636, f32[8,8]{1,0:T(8,128)} %get-tuple-element.101, f32[16,256]{1,0:T(8,128)} %copy-done.24, ...), kind=kLoop, calls=%fused_computation.49 | loop fusion | flops 3047424 | bytes 803712 | tf_op jit(solution)/shard_map/reduce_sum | solution.py:202
  53.6 1.3 reduce_sum.230
  54.9 2.6 %copy.145 = f32[1,8,16,16,16]{2,4,0,1,3:T(8,128)} copy(f32[1,8,16,16,16]{4,3,2,1,0:T(8,128)} %reduce_sum.230) | data formatting | bytes 262144 | tf_op jit(solution)/shard_map/reduce_sum | solution.py:201
  57.5 2.2 %reduce_sum.234 = f32[1,8,16,16,16]{4,3,2,1,0:T(8,128)} reshape(f32[8,16,256]{2,1,0:T(8,128)} %get-tuple-element.63) | data formatting | bytes 262144 | tf_op jit(solution)/shard_map/reduce_sum | solution.py:202
  59.7 2.6 %copy.149 = f32[1,8,16,16,16]{2,4,0,1,3:T(8,128)} copy(f32[1,8,16,16,16]{4,3,2,1,0:T(8,128)} %reduce_sum.234) | data formatting | bytes 262144 | tf_op jit(solution)/shard_map/reduce_sum | solution.py:202
  62.3 2.4 %fusion.8 = f32[16,128,128]{2,1,0:T(8,128)S(1)} fusion(f32[8,128,16,16]{1,0,3,2:T(8,128)} %bitcast.195, bf16[8,128,16,16]{1,0,3,2:T(8,128)(2,1)} %bitcast.201, pred[128,128]{1,0:T(8,128)(4,1)} %fusion.75), kind=kOutput, calls=%fused_computation.29 | convolution fusion | flops 402915328 | bytes 2637824 | tf_op jit(solution)/shard_map/btgm,bsgm->gts/dot_general | solution.py:212
  64.9 1.9 fusion.9
  67.6 2.0 %convolution_bitcast_fusion = f32[2,8,16,16,16]{2,4,0,1,3:T(8,128)S(1)} fusion(f32[8,128,16,16,1]{1,0,3,2,4:T(8,128)S(1)} %bitcast.196, f32[1,16,16,128]{3,2,0,1:T(8,128)S(1)} %copy-done.18, f32[1,16,16,128]{3,2,0,1:T(8,128)S(1)} %get-tuple-element.83), kind=kOutput, calls=%fused_computation.17 | convolution fusion | flops 100728832 | bytes 1572864 | tf_op jit(solution)/shard_map/kgnt,btgm->kbngm/dot_general | solution.py:205
  69.6 1.8 multiply_reduce_fusion.5
  72.0 1.4 stack.70
  73.4 1.3 bitcast_subtract_fusion
  74.7 1.4 stack.71
  76.1 1.6 copy.141
  77.6 1.6 copy.142
  82.1 32.6 %shard_map.84 = f32[16,72,256]{2,1,0:T(8,128)} custom-call(f32[72,256]{1,0:T(8,128)} %copy-done.19), custom_call_target="tpu_custom_call" | custom-call | tf_op jit(solution)/shard_map/pallas_call | solution.py:49
  114.7 1.4 slice.154
  116.0 1.5 slice_reduce_fusion
  117.6 2.2 %multiply_reduce_fusion.1 = (f32[16,16,256]{2,1,0:T(8,128)S(1)}, f32[16,16,256]{2,1,0:T(8,128)S(1)}) fusion(f32[16,16]{1,0:T(8,128)S(1)} %copy-done.38, f32[16,16,256]{2,1,0:T(8,128)S(1)} %get-tuple-element.77, f32[16,16,256]{2,1,0:T(8,128)S(1)} %get-tuple-element.76, f32[16,16]{1,0:T(8,128)S(1)} %copy-done.37, f32[16,256]{1,0:T(8,128)S(1)} %copy-done.25, ...), kind=kLoop, calls=%fused_computation.1 | loop fusion | flops 8257536 | bytes 1067264 | tf_op jit(solution)/shard_map/reduce_sum | solution.py:265
  123.0 4.5 %multiply_reduce_fusion = f32[16,128,128]{2,1,0:T(8,128)S(1)} fusion(f32[128,128]{1,0:T(8,128)S(1)} %copy-done.21, f32[16,16]{1,0:T(8,128)S(1)} %get-tuple-element.94, f32[16,16]{1,0:T(8,128)S(1)} %copy.133), kind=kLoop, calls=%fused_computation | loop fusion | flops 12320768 | bytes 1116160 | tf_op jit(solution)/shard_map/reduce_sum | solution.py:183
  127.6 2.3 %fusion.15 = f32[16,8,16,128]{3,2,1,0:T(8,128)} fusion(f32[8,128,16,16]{1,0,3,2:T(8,128)S(1)} %bitcast.197, f32[16,128,128]{2,1,0:T(8,128)S(1)} %multiply_reduce_fusion, pred[128,128]{1,0:T(8,128)(4,1)S(1)} %copy-done.23), kind=kOutput, calls=%fused_computation.36 | convolution fusion | flops 402915328 | bytes 3162112 | tf_op jit(solution)/shard_map/gts,btgm->bsgm/dot_general | solution.py:221
  129.9 1.8 fusion.17
  131.7 1.3 reduce_sum.225
  133.1 1.3 reduce_sum.239
  134.4 2.6 %copy.160 = f32[8,16,16,16]{1,3,0,2:T(8,128)} copy(f32[8,16,16,16]{3,2,1,0:T(8,128)} %reduce_sum.239) | data formatting | bytes 262144 | tf_op jit(solution)/shard_map/reduce_sum | solution.py:225
  137.1 2.8 %fusion.6 = f32[8,128,16,16]{1,3,0,2:T(8,128)S(1)} fusion(f32[16,8,16,128]{3,2,1,0:T(8,128)} %fusion.15, f32[8,16,16,16]{1,3,0,2:T(8,128)} %copy.160, f32[16,16,16]{0,2,1:T(8,128)S(1)} %bitcast.209, f32[8]{0:T(128)S(1)} %copy-done.43, f32[16,16]{0,1:T(8,128)S(1)} %get-tuple-element.93, f32[128]{0:T(128)S(1)} %copy-done.49, f32[16,16]{1,0:T(8,128)S(1)} %copy.133, ...), kind=kOutput, calls=%fused_computation.23 | convolution fusion | flops 50757632 | bytes 2248224 | tf_op jit(solution)/shard_map/gns,bngm->bsgm/dot_general | solution.py:285
  139.8 1.4 copy.161
  141.2 2.4 %reshape_reshape.12 = f32[1,1024,256]{1,2,0:T(8,128)} reshape(f32[8,128,16,16]{1,0,3,2:T(8,128)} %copy.161) | data formatting | bytes 2097152 | tf_op jit(solution)/shard_map/reshape;reshape | solution.py:291
  143.6 3.0 %slice_multiply_fusion.2 = (f32[1,1024,256]{1,2,0:T(8,128)}, f32[1,1024,256]{1,2,0:T(8,128)}) fusion(f32[1,1024,256]{1,2,0:T(8,128)} %reshape_reshape.12, f32[3,1024,256]{1,2,0:T(8,128)S(1)} %multiply_add_fusion), kind=kLoop, calls=%fused_computation.61 | loop fusion | flops 524288 | bytes 5242880 | tf_op jit(solution)/shard_map/mul | solution.py:292
  146.7 2.6 %copy.153 = f32[8,16,16,16]{1,3,0,2:T(8,128)} copy(f32[8,16,16,16]{3,2,1,0:T(8,128)} %reduce_sum.225) | data formatting | bytes 262144 | tf_op jit(solution)/shard_map/reduce_sum | solution.py:201
  149.3 2.9 %fusion.7 = f32[8,128,16,16]{1,3,0,2:T(8,128)S(1)} fusion(f32[16,8,16,128]{3,2,1,0:T(8,128)} %fusion.17, f32[8,16,16,16]{1,3,0,2:T(8,128)} %copy.153, f32[16,16,16]{0,2,1:T(8,128)S(1)} %bitcast.210, f32[8]{0:T(128)S(1)} %copy-done.41, f32[16,16]{0,1:T(8,128)S(1)} %get-tuple-element.93, f32[16,16]{1,0:T(8,128)S(1)} %copy-done.28, f32[16,16]{1,0:T(8,128)S(1)} %copy.133, ...), kind=kOutput, calls=%fused_computation.25 | convolution fusion | flops 50790400 | bytes 2248736 | tf_op jit(solution)/shard_map/gnt,bngm->btgm/dot_general | solution.py:283
  156.3 1.2 broadcast_in_dim.110.tile_ref
  157.6 27.8 %shard_map.85 = (f32[32,8,128]{2,1,0:T(8,128)}, f32[6,256]{1,0:T(8,128)}) custom-call(f32[8,128]{1,0:T(8,128)} %broadcast_in_dim.110.tile_ref, f32[6,256]{1,0:T(8,128)} %reshape.482.rim_ref), custom_call_target="tpu_custom_call" | custom-call | tf_op jit(solution)/shard_map/pallas_call | solution.py:110
  185.4 1.5 slice_reduce_fusion.1
  190.0 1.6 pad_maximum_fusion
  191.6 3.3 %fusion.1 = bf16[3,1024,256]{1,2,0:T(8,128)(2,1)} fusion(f32[3,1026,256]{1,2,0:T(8,128)S(1)} %pad_maximum_fusion, f32[3,256]{1,0:T(4,128)S(1)} %copy-done.33, f32[3,256]{1,0:T(4,128)S(1)} %copy-done.34, f32[3,256]{1,0:T(4,128)S(1)} %bitcast.213, f32[1,1024,256]{1,2,0:T(8,128)S(1)} %copy-done.5, f32[1,1024,256]{1,2,0:T(8,128)S(1)} %copy-done.3, ...), kind=kLoop, calls=%fused_computation.7 | loop fusion | flops 6291456 | bytes 11019264 | tf_op jit(solution)/shard_map/convert_element_type | solution.py:302
  195.0 2.6 %copy.169 = bf16[3,1024,256]{2,1,0:T(8,128)(2,1)} copy(bf16[3,1024,256]{1,2,0:T(8,128)(2,1)} %fusion.1) | data formatting | bytes 3145728
  (172 shorter events, 33.8 us)
Async XLA Ops:
  0.6 17.1 %copy-start.29 = (f32[16,16]{1,0:T(8,128)S(1)}, f32[16,16]{1,0:T(8,128)}, u32[]{:S(2)}) copy-start(f32[16,16]{1,0:T(8,128)} %param.11) | copy-start | bytes 3076
  0.6 18.3 %copy-start.17 = (bf16[1024,256]{1,0:T(8,128)(2,1)S(1)}, bf16[1024,256]{1,0:T(8,128)(2,1)}, u32[]{:S(2)}) copy-start(bf16[1024,256]{1,0:T(8,128)(2,1)} %param.13) | copy-start | bytes 1572868
  0.7 20.2 %copy-start.36 = (f32[16,16]{1,0:T(8,128)S(1)}, f32[16,16]{1,0:T(8,128)}, u32[]{:S(2)}) copy-start(f32[16,16]{1,0:T(8,128)} %param.12) | copy-start | bytes 3076
  1.6 19.9 %collective-permute-start = (bf16[3,2,256]{1,2,0:T(8,128)(2,1)S(1)}, bf16[3,2,256]{1,2,0:T(8,128)(2,1)S(1)}, u32[]{:S(2)}, u32[]{:S(2)}) collective-permute-start(bf16[3,2,256]{1,2,0:T(8,128)(2,1)S(1)} %copy.129), channel_id=1, source_target_pairs={{0,1},{1,2},{2,3},{3,4},{4,5},{5,6},{6,7},{7,8},{8,9},{9,10},{10,1... | collective-permute-start | bytes 9224 | tf_op jit(solution)/shard_map/ppermute | solution.py:133
  13.2 8.3 %copy-start.27 = (f32[16,16]{1,0:T(8,128)}, f32[16,16]{1,0:T(8,128)S(1)}, u32[]{:S(2)}) copy-start(f32[16,16]{1,0:T(8,128)S(1)} %get-tuple-element.92) | copy-start | bytes 3076
  20.3 1.3 copy-start.24
  28.9 1.3 copy-start
  39.2 4.6 %copy-start.39 = (f32[8]{0:T(128)S(1)}, f32[8]{0:T(128)}, u32[]{:S(2)}) copy-start(f32[8]{0:T(128)} %get-tuple-element.109) | copy-start | bytes 100
  42.9 1.0 copy-start.6
  62.3 2.4 %copy-start.20 = (f32[128,128]{1,0:T(8,128)S(1)}, f32[128,128]{1,0:T(8,128)}, u32[]{:S(2)}) copy-start(f32[128,128]{1,0:T(8,128)} %maximum_convert_fusion) | copy-start | bytes 196612
  62.3 2.6 %copy-start.30 = (f32[16,16]{1,0:T(8,128)S(1)}, f32[16,16]{1,0:T(8,128)}, u32[]{:S(2)}) copy-start(f32[16,16]{1,0:T(8,128)} %param.11) | copy-start | bytes 3076
  64.7 2.8 %copy-start.7 = (f32[32,8,8,128]{3,2,1,0:T(8,128)S(1)}, f32[32,8,8,128]{3,2,1,0:T(8,128)}, u32[]{:S(2)}) copy-start(f32[32,8,8,128]{3,2,1,0:T(8,128)} %copy-done.6) | copy-start | bytes 3145732
  64.7 2.8 %copy-start.18 = (f32[1,16,16,128]{3,2,0,1:T(8,128)S(1)}, f32[1,16,16,128]{3,2,0,1:T(8,128)}, u32[]{:S(2)}) copy-start(f32[1,16,16,128]{3,2,0,1:T(8,128)} %get-tuple-element.84) | copy-start | bytes 393220
  64.8 4.8 %copy-start.1 = (f32[2,8,16,16,16]{2,4,0,1,3:T(8,128)S(1)}, f32[2,8,16,16,16]{2,4,0,1,3:T(8,128)}, u32[]{:S(2)}) copy-start(f32[2,8,16,16,16]{2,4,0,1,3:T(8,128)} %copy-done) | copy-start | bytes 786436
  64.8 4.8 %copy-start.14 = (f32[1,8,16,16,16]{2,4,0,1,3:T(8,128)S(1)}, f32[1,8,16,16,16]{2,4,0,1,3:T(8,128)}, u32[]{:S(2)}) copy-start(f32[1,8,16,16,16]{2,4,0,1,3:T(8,128)} %copy.145) | copy-start | bytes 393220
  64.8 4.8 %copy-start.15 = (f32[1,8,16,16,16]{2,4,0,1,3:T(8,128)S(1)}, f32[1,8,16,16,16]{2,4,0,1,3:T(8,128)}, u32[]{:S(2)}) copy-start(f32[1,8,16,16,16]{2,4,0,1,3:T(8,128)} %copy.149) | copy-start | bytes 393220
  64.9 4.8 %copy-start.40 = (f32[8]{0:T(128)S(1)}, f32[8]{0:T(128)}, u32[]{:S(2)}) copy-start(f32[8]{0:T(128)} %get-tuple-element.109) | copy-start | bytes 100
  64.9 4.8 %copy-start.42 = (f32[8]{0:T(128)S(1)}, f32[8]{0:T(128)}, u32[]{:S(2)}) copy-start(f32[8]{0:T(128)} %get-tuple-element.108) | copy-start | bytes 100
  79.9 37.7 %copy-start.25 = (f32[16,256]{1,0:T(8,128)S(1)}, f32[16,256]{1,0:T(8,128)}, u32[]{:S(2)}) copy-start(f32[16,256]{1,0:T(8,128)} %copy-done.24) | copy-start | bytes 49156
  79.9 37.7 %copy-start.37 = (f32[16,16]{1,0:T(8,128)S(1)}, f32[16,16]{1,0:T(8,128)}, u32[]{:S(2)}) copy-start(f32[16,16]{1,0:T(8,128)} %get-tuple-element.95) | copy-start | bytes 3076
  79.9 37.7 %copy-start.38 = (f32[16,16]{1,0:T(8,128)S(1)}, f32[16,16]{1,0:T(8,128)}, u32[]{:S(2)}) copy-start(f32[16,16]{1,0:T(8,128)} %get-tuple-element.96) | copy-start | bytes 3076
  79.9 37.7 %copy-start.48 = (pred[16,16]{1,0:T(8,128)(4,1)S(1)}, pred[16,16]{1,0:T(8,128)(4,1)}, u32[]{:S(2)}) copy-start(pred[16,16]{1,0:T(8,128)(4,1)} %subtract_compare_fusion) | copy-start | bytes 772
  82.1 37.8 %copy-start.32 = (f32[16,256]{1,0:T(8,128)S(1)}, f32[16,256]{1,0:T(8,128)}, u32[]{:S(2)}) copy-start(f32[16,256]{1,0:T(8,128)} %exp.108) | copy-start | bytes 49156
  82.1 37.8 %copy-start.44 = (f32[16]{0:T(128)S(1)}, f32[16]{0:T(128)}, u32[]{:S(2)}) copy-start(f32[16]{0:T(128)} %get-tuple-element.110) | copy-start | bytes 196
  82.1 37.8 %copy-start.45 = (f32[16]{0:T(128)S(1)}, f32[16]{0:T(128)}, u32[]{:S(2)}) copy-start(f32[16]{0:T(128)} %get-tuple-element.111) | copy-start | bytes 196
  82.1 37.8 %copy-start.46 = (pred[16]{0:T(512)(128)(4,1)S(1)}, pred[16]{0:T(512)(128)(4,1)}, u32[]{:S(2)}) copy-start(pred[16]{0:T(512)(128)(4,1)} %get-tuple-element.112) | copy-start | bytes 52
  82.1 37.8 %copy-start.47 = (pred[16]{0:T(512)(128)(4,1)S(1)}, pred[16]{0:T(512)(128)(4,1)}, u32[]{:S(2)}) copy-start(pred[16]{0:T(512)(128)(4,1)} %get-tuple-element.113) | copy-start | bytes 52
  114.7 8.4 %copy-start.21 = (f32[128,128]{1,0:T(8,128)S(1)}, f32[128,128]{1,0:T(8,128)}, u32[]{:S(2)}) copy-start(f32[128,128]{1,0:T(8,128)} %maximum_convert_fusion) | copy-start | bytes 196612
  123.0 4.5 %copy-start.8 = (f32[32,8,8,128]{3,2,1,0:T(8,128)S(1)}, f32[32,8,8,128]{3,2,1,0:T(8,128)}, u32[]{:S(2)}) copy-start(f32[32,8,8,128]{3,2,1,0:T(8,128)} %copy-done.6) | copy-start | bytes 3145732
  123.0 4.6 %copy-start.23 = (pred[128,128]{1,0:T(8,128)(4,1)S(1)}, pred[128,128]{1,0:T(8,128)(4,1)}, u32[]{:S(2)}) copy-start(pred[128,128]{1,0:T(8,128)(4,1)} %fusion.75) | copy-start | bytes 49156
  127.6 2.3 %copy-start.12 = (bf16[32,8,8,128]{3,2,1,0:T(8,128)(2,1)S(1)}, bf16[32,8,8,128]{3,2,1,0:T(8,128)(2,1)}, u32[]{:S(2)}) copy-start(bf16[32,8,8,128]{3,2,1,0:T(8,128)(2,1)} %copy-done.11) | copy-start | bytes 1572868
  127.6 5.4 %copy-start.31 = (f32[16,256]{1,0:T(8,128)S(1)}, f32[16,256]{1,0:T(8,128)}, u32[]{:S(2)}) copy-start(f32[16,256]{1,0:T(8,128)} %get-tuple-element.55) | copy-start | bytes 49156
  127.6 5.5 %copy-start.26 = (f32[8,16,256]{2,1,0:T(8,128)S(1)}, f32[8,16,256]{2,1,0:T(8,128)}, u32[]{:S(2)}) copy-start(f32[8,16,256]{2,1,0:T(8,128)} %get-tuple-element.65) | copy-start | bytes 393220
  129.9 7.2 %copy-start.43 = (f32[8]{0:T(128)S(1)}, f32[8]{0:T(128)}, u32[]{:S(2)}) copy-start(f32[8]{0:T(128)} %get-tuple-element.108) | copy-start | bytes 100
  129.9 7.2 %copy-start.49 = (f32[128]{0:T(128)S(1)}, f32[128]{0:T(128)}, u32[]{:S(2)}) copy-start(f32[128]{0:T(128)} %iota_subtract_fusion.3) | copy-start | bytes 1540
  143.6 5.8 %copy-start.28 = (f32[16,16]{1,0:T(8,128)S(1)}, f32[16,16]{1,0:T(8,128)}, u32[]{:S(2)}) copy-start(f32[16,16]{1,0:T(8,128)} %copy-done.27) | copy-start | bytes 3076
  143.6 5.8 %copy-start.41 = (f32[8]{0:T(128)S(1)}, f32[8]{0:T(128)}, u32[]{:S(2)}) copy-start(f32[8]{0:T(128)} %get-tuple-element.109) | copy-start | bytes 100
  149.3 3.3 %copy-start.13 = (bf16[1024,256]{0,1:T(8,128)(2,1)S(1)}, bf16[1024,256]{0,1:T(8,128)(2,1)}, u32[]{:S(2)}) copy-start(bf16[1024,256]{0,1:T(8,128)(2,1)} %copy.138) | copy-start | bytes 1572868
  152.3 1.6 copy-start.2
  152.3 1.6 copy-start.4
  153.9 1.0 copy-start.9
  153.9 36.0 %copy-start.3 = (f32[1,1024,256]{1,2,0:T(8,128)S(1)}, f32[1,1024,256]{1,2,0:T(8,128)}, u32[]{:S(2)}) copy-start(f32[1,1024,256]{1,2,0:T(8,128)} %get-tuple-element.70) | copy-start | bytes 3145732
  153.9 36.0 %copy-start.5 = (f32[1,1024,256]{1,2,0:T(8,128)S(1)}, f32[1,1024,256]{1,2,0:T(8,128)}, u32[]{:S(2)}) copy-start(f32[1,1024,256]{1,2,0:T(8,128)} %get-tuple-element.71) | copy-start | bytes 3145732
  189.9 1.7 copy-start.10
  189.9 1.7 copy-start.33
  189.9 1.7 copy-start.34
  189.9 1.7 copy-start.35
  194.9 2.6 %copy-start.16 = (bf16[1024,256]{0,1:T(8,128)(2,1)S(1)}, bf16[1024,256]{0,1:T(8,128)(2,1)}, u32[]{:S(2)}) copy-start(bf16[1024,256]{0,1:T(8,128)(2,1)} %get-tuple-element.75) | copy-start | bytes 1572868
  (3 other events, 2.1 us)

commit v3 on v2

--- a/solution.py
+++ b/solution.py
@@ -194,6 +194,9 @@
         jnp.exp(-rate_cols[None, None] * (block_len * jnp.maximum(block_steps, 0.0))),
         0.0,
     )
+    span_weight, span_back = lax.optimization_barrier(
+        (span_weight, jnp.swapaxes(span_weight, 0, 1))
+    )
     inside_fwd = jnp.einsum("gts,bsgm->btgm", toeplitz, z_wide, precision=threepass)
     fresh_fwd = jnp.einsum("kgns,bsgm->kbngm", block_ends, z_wide, precision=threepass).reshape(
         2, block_count, order_count, channels
@@ -222,11 +225,15 @@
     fresh_bwd = jnp.einsum("gnt,btgm->bngm", block_pow, e_blocks, precision=precise).reshape(
         block_count, order_count, channels
     )
-    later_flat = jnp.sum(jnp.swapaxes(span_weight, 0, 1) * fresh_bwd[None], axis=1)
+    later_flat = jnp.sum(span_back * fresh_bwd[None], axis=1)
     first_ids = block_ids[:, None, None]
     last_ids = block_count - 1.0 - block_ids[:, None, None]
-    from_first = jnp.exp(-rate_cols[None] * (block_len * first_ids))
-    from_last = jnp.exp(-rate_cols[None] * (block_len * last_ids))
+    from_first, from_last = lax.optimization_barrier(
+        (
+            jnp.exp(-rate_cols[None] * (block_len * first_ids)),
+            jnp.exp(-rate_cols[None] * (block_len * last_ids)),
+        )
+    )
     end_state = jnp.sum(from_last * fresh_fwd[0], axis=0)
     end_lagged = jnp.sum(from_last * (fresh_fwd[1] - block_len * last_ids * fresh_fwd[0]), axis=0)
     start_state = jnp.sum(from_first * fresh_bwd, axis=0)

time: 200 us -> 209 us (1.045)
  other arithmetic: 45 us -> 49.5 us
  local copies, waits for them, and re-layouts: 67.7 us -> 71.8 us
    squeeze x0 -> x3, local copies, waits for them, and re-layouts: none -> 6.79 us  [the longest x1 2.27 us: per_device(): fresh_fwd[1] - block_len * last_ids * fresh_fwd[0]]
    slice x0 -> x2, local copies, waits for them, and re-layouts: none -> 5.38 us  [the longest x1 2.81 us: per_device(): moments[0]]
    reshape x0 -> x3, local copies, waits for them, and re-layouts: none -> 4.34 us  [the longest x1 1.61 us: per_device(): jnp.einsum('gnt,btgm->bngm', block_pow, e_blocks, precision=precise)]
    reduce_sum x4 -> x2, local copies, waits for them, and re-layouts: 7.86 us -> 3.91 us  [per_device(): start_flat = jnp.sum(span_weight * fresh_fwd[0][None], axis=1)]
    reduce_sum x2 -> x0, local copies, waits for them, and re-layouts: 3.94 us -> none  [per_device(): jnp.sum(jnp.swapaxes(span_weight, 0, 1) * fresh_bwd[None], axis=1)]
    another operation x4 -> x0, local copies, waits for them, and re-layouts: 3.89 us -> none  [per_device(): jnp.stack([end_state, end_lagged, start_state, second_moment])]
    unnamed x112 -> x116, local copies, waits for them, and re-layouts: 16.5 us -> 12.8 us
    squeeze x2, local copies, waits for them, and re-layouts: 0.15 us -> 2.71 us  [per_device(): lag_total = local_totals[1] + cross_lag]
where the time goes in v3:
time: 209 us; the launch traced here: 207 us
  local copies, waits for them, and re-layouts  71.8 us (34%)
  Pallas kernels  60.3 us (29%)
  other arithmetic  49.5 us (24%)
  matrix products  19 us (9%)
  starting transfers between devices  4.38 us (2%)
  between operations  2.12 us (1%)
    pallas_call x1, Pallas kernels, gather_along(): pl.pallas_call(functools.partial(gather_kernel, axis, count), out_shape=j...  32.5 us
    pallas_call x1, Pallas kernels, finish_exchange(): pl.pallas_call(functools.partial(finish_kernel, fsdp_count, ctx_count), o...  27.8 us
    unnamed x116, local copies, waits for them, and re-layouts  12.8 us
    reduce_sum x1, other arithmetic, per_device(): jnp.sum(mode_coefs[:, :, None, None] * pair_pow, axis=1)  5.25 us
    add x1, other arithmetic, short_conv(): summed + taps_table[:, offset, None, :] * row_data[:, start_row:start_row...  4.91 us
    reduce_sum x2, local copies, waits for them, and re-layouts, per_device(): jnp.sum(span_weight * (fresh_fwd[1][None] - block_len * block_steps * fre...  4.84 us
    ppermute x1, starting transfers between devices, passed_along(): lax.ppermute(value, axis, [(source, source + steps) for source in range(l...  4.38 us
  transfers between devices with their start and end apart: 1, of which 0 were waited for; matrix products, arithmetic and copies ran while one was open for 8% of the time, Pallas kernels for 0%

profile of v3, /device:TPU:1, one launch (start us, length us, event | category | flops | bytes accessed | tf_op | source)
XLA Modules:
  0.0 207.0 jit_solution(15958948379196333905)
XLA Ops:
  1.7 4.4 %collective-permute-start = (bf16[3,2,256]{1,2,0:T(8,128)(2,1)S(1)}, bf16[3,2,256]{1,2,0:T(8,128)(2,1)S(1)}, u32[]{:S(2)}, u32[]{:S(2)}) collective-permute-start(bf16[3,2,256]{1,2,0:T(8,128)(2,1)S(1)} %copy.92), channel_id=1, source_target_pairs={{0,1},{1,2},{2,3},{3,4},{4,5},{5,6},{6,7},{7,8},{8,9},{9,10},{10,1... | collective-permute-start | bytes 9224 | tf_op jit(solution)/shard_map/ppermute | solution.py:133
  13.8 1.7 exponential_select_fusion.1
  17.0 1.7 copy.91
  22.9 4.9 %multiply_add_fusion = f32[3,1024,256]{1,2,0:T(8,128)S(1)} fusion(bf16[3,1024,256]{1,2,0:T(8,128)(2,1)} %copy.91, bf16[3,2,256]{1,2,0:T(8,128)(2,1)} %copy-done.27, f32[3,256]{1,0:T(4,128)} %get-tuple-element.112, f32[3,256]{1,0:T(4,128)} %get-tuple-element.113, f32[3,256]{1,0:T(4,128)} %bitcast.210), kind=kLoop, calls=%fused_computation.11 | loop fusion | flops 11010048 | bytes 4730880 | tf_op jit(solution)/shard_map/add | solution.py:141
  29.7 1.6 fusion.81
  31.3 2.6 %copy.100 = f32[1,8,16,16,16]{4,3,2,1,0:T(8,128)} copy(f32[1,8,16,16,16]{2,4,0,1,3:T(8,128)} %get-tuple-element.76) | data formatting | bytes 262144 | tf_op jit(solution)/shard_map/slice | solution.py:204
  33.9 1.6 mul.593
  35.5 2.6 %copy.101 = f32[1,8,16,16,16]{4,3,2,1,0:T(8,128)} copy(f32[1,8,16,16,16]{2,4,0,1,3:T(8,128)} %get-tuple-element.77) | data formatting | bytes 262144 | tf_op jit(solution)/shard_map/slice | solution.py:238
  38.1 2.3 %squeeze.49 = f32[8,16,256]{2,1,0:T(8,128)} reshape(f32[1,8,16,16,16]{4,3,2,1,0:T(8,128)} %copy.101) | data formatting | bytes 262144 | tf_op jit(solution)/shard_map/squeeze | solution.py:238
  40.4 2.2 %multiply_reduce_fusion.4 = (f32[8,16,256]{2,1,0:T(8,128)}, f32[8,16,256]{2,1,0:T(8,128)S(1)}) fusion(f32[8,8,16,256]{3,2,1,0:T(8,128)} %get-tuple-element.34, f32[8,8]{1,0:T(8,128)} %get-tuple-element.105, f32[8,16,256]{2,1,0:T(8,128)} %squeeze.49, f32[8,16,256]{2,1,0:T(8,128)S(1)} %mul.593), kind=kLoop, calls=%fused_computation.45 | loop fusion | flops 1507328 | bytes 1573120 | tf_op jit(solution)/shard_map/reduce_sum | solution.py:205
  43.9 2.6 %copy.108 = f32[1,8,16,16,16]{2,4,0,1,3:T(8,128)} copy(f32[1,8,16,16,16]{4,3,2,1,0:T(8,128)} %reduce_sum.225) | data formatting | bytes 262144 | tf_op jit(solution)/shard_map/reduce_sum | solution.py:204
  46.5 2.2 %reduce_sum.229 = f32[1,8,16,16,16]{4,3,2,1,0:T(8,128)} reshape(f32[8,16,256]{2,1,0:T(8,128)} %get-tuple-element.56) | data formatting | bytes 262144 | tf_op jit(solution)/shard_map/reduce_sum | solution.py:205
  48.7 2.6 %copy.111 = f32[1,8,16,16,16]{2,4,0,1,3:T(8,128)} copy(f32[1,8,16,16,16]{4,3,2,1,0:T(8,128)} %reduce_sum.229) | data formatting | bytes 262144 | tf_op jit(solution)/shard_map/reduce_sum | solution.py:205
  52.8 2.1 %convolution_bitcast_fusion.3 = f32[8,16,16,16]{1,3,0,2:T(8,128)} fusion(f32[8,128,16,16]{1,0,3,2:T(8,128)S(1)} %bitcast.194, f32[16,16]{1,0:T(8,128)S(1)} %copy-done.23), kind=kOutput, calls=%fused_computation.26 | convolution fusion | flops 50364416 | bytes 1180672 | tf_op jit(solution)/shard_map/gnt,btgm->bngm/dot_general | solution.py:225
  56.1 1.9 fusion.9
  58.8 2.0 convolution_bitcast_fusion
  60.8 1.7 multiply_reduce_fusion.5
  63.9 2.6 %copy.106 = f32[1,8,16,16,16]{4,3,2,1,0:T(8,128)} copy(f32[1,8,16,16,16]{2,4,0,1,3:T(8,128)} %get-tuple-element.75) | data formatting | bytes 262144 | tf_op jit(solution)/shard_map/slice | solution.py:240
  66.4 2.3 %squeeze.50 = f32[8,16,256]{2,1,0:T(8,128)} reshape(f32[1,8,16,16,16]{4,3,2,1,0:T(8,128)} %copy.106) | data formatting | bytes 262144 | tf_op jit(solution)/shard_map/squeeze | solution.py:240
  68.7 2.8 %copy.107 = f32[1,8,16,16,16]{4,3,2,1,0:T(8,128)} copy(f32[1,8,16,16,16]{2,4,0,1,3:T(8,128)} %get-tuple-element.74) | data formatting | bytes 262144 | tf_op jit(solution)/shard_map/slice | solution.py:240
  71.5 2.3 %squeeze.51 = f32[8,16,256]{2,1,0:T(8,128)} reshape(f32[1,8,16,16,16]{4,3,2,1,0:T(8,128)} %copy.107) | data formatting | bytes 262144 | tf_op jit(solution)/shard_map/squeeze | solution.py:240
  73.8 2.6 %copy.104 = f32[8,16,16,16]{3,2,1,0:T(8,128)} copy(f32[8,16,16,16]{1,3,0,2:T(8,128)} %convolution_bitcast_fusion.3) | data formatting | bytes 262144 | tf_op jit(solution)/shard_map/gnt,btgm->bngm/transpose | solution.py:225
  76.4 1.6 reshape.442
  82.1 32.5 %shard_map.84 = f32[16,72,256]{2,1,0:T(8,128)} custom-call(f32[72,256]{1,0:T(8,128)} %maximum_dynamic-update-slice_fusion.x_ref), custom_call_target="tpu_custom_call" | custom-call | tf_op jit(solution)/shard_map/pallas_call | solution.py:49
  115.9 1.5 slice_reduce_fusion
  117.5 2.2 %multiply_reduce_fusion.1 = (f32[16,16,256]{2,1,0:T(8,128)S(1)}, f32[16,16,256]{2,1,0:T(8,128)S(1)}) fusion(f32[16,16]{1,0:T(8,128)S(1)} %copy-done.44, f32[16,16,256]{2,1,0:T(8,128)S(1)} %get-tuple-element.81, f32[16,16,256]{2,1,0:T(8,128)S(1)} %get-tuple-element.80, f32[16,16]{1,0:T(8,128)S(1)} %copy-done.43, f32[16,256]{1,0:T(8,128)S(1)} %neg.46, ...), kind=kLoop, calls=%fused_computation.1 | loop fusion | flops 8257536 | bytes 1067264 | tf_op jit(solution)/shard_map/reduce_sum | solution.py:272
  120.6 1.5 reshape.447
  123.1 1.5 reshape.448
  125.6 1.4 slice_reduce_fusion.3
  127.0 1.3 squeeze.56
  128.3 1.4 copy.121
  129.7 1.3 squeeze.57
  131.0 1.4 copy.123
  132.4 1.4 multiply_bitcast_fusion.1
  134.5 5.3 %multiply_reduce_fusion = f32[16,128,128]{2,1,0:T(8,128)S(1)} fusion(f32[128,128]{1,0:T(8,128)} %maximum_convert_fusion, f32[16,16]{1,0:T(8,128)} %copy-done.22, f32[16,16]{1,0:T(8,128)S(1)} %copy.96), kind=kLoop, calls=%fused_computation | loop fusion | flops 12320768 | bytes 1116160 | tf_op jit(solution)/shard_map/reduce_sum | solution.py:183
  139.8 2.2 %fusion.15 = f32[16,8,16,128]{3,2,1,0:T(8,128)} fusion(f32[8,128,16,16]{1,0,3,2:T(8,128)S(1)} %bitcast.197, f32[16,128,128]{2,1,0:T(8,128)S(1)} %multiply_reduce_fusion, pred[128,128]{1,0:T(8,128)(4,1)S(1)} %copy-done.29), kind=kOutput, calls=%fused_computation.36 | convolution fusion | flops 402915328 | bytes 3162112 | tf_op jit(solution)/shard_map/gts,btgm->bsgm/dot_general | solution.py:224
  142.1 1.8 fusion.17
  144.0 1.4 reshape.446
  145.4 3.5 %fusion.6 = f32[8,128,16,16]{1,3,0,2:T(8,128)S(1)} fusion(f32[16,8,16,128]{3,2,1,0:T(8,128)} %fusion.15, f32[8,16,16,16]{3,2,1,0:T(8,128)} %reshape.446, f32[128]{0:T(128)} %iota_subtract_fusion.3, f32[16,16]{1,0:T(8,128)S(1)} %copy.96, f32[16,16]{1,0:T(8,128)S(1)} %copy-done.25), kind=kOutput, calls=%fused_computation.23 | convolution fusion | flops 50659328 | bytes 2230784 | tf_op jit(solution)/shard_map/gns,bngm->bsgm/dot_general | solution.py:292
  150.3 2.4 %reshape_reshape.12 = f32[1,1024,256]{1,2,0:T(8,128)} reshape(f32[8,128,16,16]{1,0,3,2:T(8,128)} %copy.120) | data formatting | bytes 2097152 | tf_op jit(solution)/shard_map/reshape;reshape | solution.py:298
  152.7 3.0 %slice_multiply_fusion.2 = (f32[1,1024,256]{1,2,0:T(8,128)}, f32[1,1024,256]{1,2,0:T(8,128)}) fusion(f32[1,1024,256]{1,2,0:T(8,128)} %reshape_reshape.12, f32[3,1024,256]{1,2,0:T(8,128)S(1)} %multiply_add_fusion), kind=kLoop, calls=%fused_computation.52 | loop fusion | flops 524288 | bytes 5242880 | tf_op jit(solution)/shard_map/mul | solution.py:299
  155.7 1.4 reshape.445
  157.1 3.6 %fusion.7 = f32[8,128,16,16]{1,3,0,2:T(8,128)S(1)} fusion(f32[16,8,16,128]{3,2,1,0:T(8,128)} %fusion.17, f32[8,16,16,16]{3,2,1,0:T(8,128)} %reshape.445, f32[16,16]{1,0:T(8,128)} %copy-done.30, f32[16,16]{1,0:T(8,128)S(1)} %copy.96, f32[16,16]{1,0:T(8,128)S(1)} %copy-done.25), kind=kOutput, calls=%fused_computation.25 | convolution fusion | flops 50692096 | bytes 2231296 | tf_op jit(solution)/shard_map/gnt,bngm->btgm/dot_general | solution.py:290
  166.0 27.8 %shard_map.85 = (f32[32,8,128]{2,1,0:T(8,128)}, f32[6,256]{1,0:T(8,128)}) custom-call(f32[8,128]{1,0:T(8,128)} %broadcast_in_dim.110.tile_ref, f32[6,256]{1,0:T(8,128)} %reshape.449.rim_ref), custom_call_target="tpu_custom_call" | custom-call | tf_op jit(solution)/shard_map/pallas_call | solution.py:110
  193.9 1.5 slice_reduce_fusion.1
  198.4 1.6 pad_maximum_fusion
  200.1 3.3 %fusion.1 = bf16[3,1024,256]{1,2,0:T(8,128)(2,1)} fusion(f32[3,1026,256]{1,2,0:T(8,128)S(1)} %pad_maximum_fusion, f32[3,256]{1,0:T(4,128)S(1)} %copy-done.38, f32[3,256]{1,0:T(4,128)S(1)} %copy-done.39, f32[3,256]{1,0:T(4,128)S(1)} %bitcast.211, f32[1,1024,256]{1,2,0:T(8,128)S(1)} %copy-done.3, f32[1,1024,256]{1,2,0:T(8,128)S(1)} %copy-done.1, ...), kind=kLoop, calls=%fused_computation.7 | loop fusion | flops 6291456 | bytes 11019264 | tf_op jit(solution)/shard_map/convert_element_type | solution.py:309
  203.4 2.6 %copy.128 = bf16[3,1024,256]{2,1,0:T(8,128)(2,1)} copy(bf16[3,1024,256]{1,2,0:T(8,128)(2,1)} %fusion.1) | data formatting | bytes 3145728
  (179 shorter events, 41.4 us)
Async XLA Ops:
  0.6 16.3 %copy-start.16 = (bf16[3,1024,256]{2,1,0:T(8,128)(2,1)S(1)}, bf16[3,1024,256]{2,1,0:T(8,128)(2,1)}, u32[]{:S(2)}) copy-start(bf16[3,1024,256]{2,1,0:T(8,128)(2,1)} %param.9) | copy-start | bytes 4718596
  1.7 20.6 %collective-permute-start = (bf16[3,2,256]{1,2,0:T(8,128)(2,1)S(1)}, bf16[3,2,256]{1,2,0:T(8,128)(2,1)S(1)}, u32[]{:S(2)}, u32[]{:S(2)}) collective-permute-start(bf16[3,2,256]{1,2,0:T(8,128)(2,1)S(1)} %copy.92), channel_id=1, source_target_pairs={{0,1},{1,2},{2,3},{3,4},{4,5},{5,6},{6,7},{7,8},{8,9},{9,10},{10,1... | collective-permute-start | bytes 9224 | tf_op jit(solution)/shard_map/ppermute | solution.py:133
  8.1 7.4 %copy-start.45 = (f32[8]{0:T(128)}, f32[8]{0:T(128)S(1)}, u32[]{:S(2)}) copy-start(f32[8]{0:T(128)S(1)} %get-tuple-element.111) | copy-start | bytes 100
  8.1 7.4 %copy-start.46 = (f32[8]{0:T(128)}, f32[8]{0:T(128)S(1)}, u32[]{:S(2)}) copy-start(f32[8]{0:T(128)S(1)} %get-tuple-element.110) | copy-start | bytes 100
  12.2 6.5 %copy-start.22 = (f32[16,16]{1,0:T(8,128)}, f32[16,16]{1,0:T(8,128)S(1)}, u32[]{:S(2)}) copy-start(f32[16,16]{1,0:T(8,128)S(1)} %get-tuple-element.102) | copy-start | bytes 3076
  12.2 6.5 %copy-start.30 = (f32[16,16]{1,0:T(8,128)}, f32[16,16]{1,0:T(8,128)S(1)}, u32[]{:S(2)}) copy-start(f32[16,16]{1,0:T(8,128)S(1)} %get-tuple-element.100) | copy-start | bytes 3076
  12.3 7.0 %copy-start.31 = (f32[16,16]{1,0:T(8,128)S(1)}, f32[16,16]{1,0:T(8,128)}, u32[]{:S(2)}) copy-start(f32[16,16]{1,0:T(8,128)} %param.11) | copy-start | bytes 3076
  12.4 8.2 %copy-start.19 = (bf16[1024,256]{1,0:T(8,128)(2,1)S(1)}, bf16[1024,256]{1,0:T(8,128)(2,1)}, u32[]{:S(2)}) copy-start(bf16[1024,256]{1,0:T(8,128)(2,1)} %param.13) | copy-start | bytes 1572868
  13.8 7.7 %copy-start.42 = (f32[16,16]{1,0:T(8,128)S(1)}, f32[16,16]{1,0:T(8,128)}, u32[]{:S(2)}) copy-start(f32[16,16]{1,0:T(8,128)} %param.12) | copy-start | bytes 3076
  35.5 11.0 %copy-start.17 = (f32[8,16,256]{2,1,0:T(8,128)}, f32[8,16,256]{2,1,0:T(8,128)S(1)}, u32[]{:S(2)}) copy-start(f32[8,16,256]{2,1,0:T(8,128)S(1)} %mul.593) | copy-start | bytes 393220
  48.7 4.1 %copy-start.23 = (f32[16,16]{1,0:T(8,128)S(1)}, f32[16,16]{1,0:T(8,128)}, u32[]{:S(2)}) copy-start(f32[16,16]{1,0:T(8,128)} %copy-done.22) | copy-start | bytes 3076
  51.3 3.6 %copy-start.9 = (bf16[32,8,8,128]{3,2,1,0:T(8,128)(2,1)S(1)}, bf16[32,8,8,128]{3,2,1,0:T(8,128)(2,1)}, u32[]{:S(2)}) copy-start(bf16[32,8,8,128]{3,2,1,0:T(8,128)(2,1)} %copy-done.8) | copy-start | bytes 1572868
  51.3 3.6 %copy-start.28 = (pred[128,128]{1,0:T(8,128)(4,1)S(1)}, pred[128,128]{1,0:T(8,128)(4,1)}, u32[]{:S(2)}) copy-start(pred[128,128]{1,0:T(8,128)(4,1)} %fusion.65) | copy-start | bytes 49156
  52.8 6.0 %copy-start.4 = (f32[32,8,8,128]{3,2,1,0:T(8,128)}, f32[32,8,8,128]{3,2,1,0:T(8,128)S(1)}, u32[]{:S(2)}) copy-start(f32[32,8,8,128]{3,2,1,0:T(8,128)S(1)} %copy.153) | copy-start | bytes 3145732
  55.9 2.0 copy-start.24
  56.0 2.8 %copy-start.20 = (f32[1,16,16,128]{3,2,0,1:T(8,128)S(1)}, f32[1,16,16,128]{3,2,0,1:T(8,128)}, u32[]{:S(2)}) copy-start(f32[1,16,16,128]{3,2,0,1:T(8,128)} %get-tuple-element.87) | copy-start | bytes 393220
  56.0 2.8 %copy-start.21 = (f32[1,16,16,128]{3,2,0,1:T(8,128)S(1)}, f32[1,16,16,128]{3,2,0,1:T(8,128)}, u32[]{:S(2)}) copy-start(f32[1,16,16,128]{3,2,0,1:T(8,128)} %get-tuple-element.88) | copy-start | bytes 393220
  56.1 4.7 %copy-start.13 = (f32[1,8,16,16,16]{2,4,0,1,3:T(8,128)S(1)}, f32[1,8,16,16,16]{2,4,0,1,3:T(8,128)}, u32[]{:S(2)}) copy-start(f32[1,8,16,16,16]{2,4,0,1,3:T(8,128)} %copy.108) | copy-start | bytes 393220
  56.1 4.7 %copy-start.14 = (f32[1,8,16,16,16]{2,4,0,1,3:T(8,128)S(1)}, f32[1,8,16,16,16]{2,4,0,1,3:T(8,128)}, u32[]{:S(2)}) copy-start(f32[1,8,16,16,16]{2,4,0,1,3:T(8,128)} %copy.111) | copy-start | bytes 393220
  60.8 2.4 %copy-start.41 = (f32[16,16]{1,0:T(8,128)S(1)}, f32[16,16]{1,0:T(8,128)}, u32[]{:S(2)}) copy-start(f32[16,16]{1,0:T(8,128)} %get-tuple-element.65) | copy-start | bytes 3076
  114.5 3.0 %copy-start.43 = (f32[16,16]{1,0:T(8,128)S(1)}, f32[16,16]{1,0:T(8,128)}, u32[]{:S(2)}) copy-start(f32[16,16]{1,0:T(8,128)} %get-tuple-element.103) | copy-start | bytes 3076
  114.5 3.0 %copy-start.44 = (f32[16,16]{1,0:T(8,128)S(1)}, f32[16,16]{1,0:T(8,128)}, u32[]{:S(2)}) copy-start(f32[16,16]{1,0:T(8,128)} %get-tuple-element.104) | copy-start | bytes 3076
  114.5 3.0 %copy-start.51 = (pred[16,16]{1,0:T(8,128)(4,1)S(1)}, pred[16,16]{1,0:T(8,128)(4,1)}, u32[]{:S(2)}) copy-start(pred[16,16]{1,0:T(8,128)(4,1)} %subtract_compare_fusion) | copy-start | bytes 772
  114.6 5.2 %copy-start.37 = (f32[16,256]{1,0:T(8,128)S(1)}, f32[16,256]{1,0:T(8,128)}, u32[]{:S(2)}) copy-start(f32[16,256]{1,0:T(8,128)} %exp.84) | copy-start | bytes 49156
  114.6 5.2 %copy-start.47 = (f32[16]{0:T(128)S(1)}, f32[16]{0:T(128)}, u32[]{:S(2)}) copy-start(f32[16]{0:T(128)} %get-tuple-element.116) | copy-start | bytes 196
  114.6 5.2 %copy-start.48 = (f32[16]{0:T(128)S(1)}, f32[16]{0:T(128)}, u32[]{:S(2)}) copy-start(f32[16]{0:T(128)} %get-tuple-element.117) | copy-start | bytes 196
  114.6 5.2 %copy-start.49 = (pred[16]{0:T(512)(128)(4,1)S(1)}, pred[16]{0:T(512)(128)(4,1)}, u32[]{:S(2)}) copy-start(pred[16]{0:T(512)(128)(4,1)} %get-tuple-element.118) | copy-start | bytes 52
  114.6 5.2 %copy-start.50 = (pred[16]{0:T(512)(128)(4,1)S(1)}, pred[16]{0:T(512)(128)(4,1)}, u32[]{:S(2)}) copy-start(pred[16]{0:T(512)(128)(4,1)} %get-tuple-element.119) | copy-start | bytes 52
  134.5 5.3 %copy-start.5 = (f32[32,8,8,128]{3,2,1,0:T(8,128)S(1)}, f32[32,8,8,128]{3,2,1,0:T(8,128)}, u32[]{:S(2)}) copy-start(f32[32,8,8,128]{3,2,1,0:T(8,128)} %copy-done.4) | copy-start | bytes 3145732
  134.5 5.3 %copy-start.29 = (pred[128,128]{1,0:T(8,128)(4,1)S(1)}, pred[128,128]{1,0:T(8,128)(4,1)}, u32[]{:S(2)}) copy-start(pred[128,128]{1,0:T(8,128)(4,1)} %fusion.65) | copy-start | bytes 49156
  139.8 2.3 %copy-start.10 = (bf16[32,8,8,128]{3,2,1,0:T(8,128)(2,1)S(1)}, bf16[32,8,8,128]{3,2,1,0:T(8,128)(2,1)}, u32[]{:S(2)}) copy-start(bf16[32,8,8,128]{3,2,1,0:T(8,128)(2,1)} %copy-done.8) | copy-start | bytes 1572868
  139.8 4.1 %copy-start.12 = (f32[8,8,16,256]{3,2,1,0:T(8,128)S(1)}, f32[8,8,16,256]{3,2,1,0:T(8,128)}, u32[]{:S(2)}) copy-start(f32[8,8,16,256]{3,2,1,0:T(8,128)} %get-tuple-element.37) | copy-start | bytes 3145732
  139.8 4.2 %copy-start.18 = (f32[8,16,256]{2,1,0:T(8,128)S(1)}, f32[8,16,256]{2,1,0:T(8,128)}, u32[]{:S(2)}) copy-start(f32[8,16,256]{2,1,0:T(8,128)} %get-tuple-element.36) | copy-start | bytes 393220
  139.8 4.2 %copy-start.36 = (f32[16,256]{1,0:T(8,128)S(1)}, f32[16,256]{1,0:T(8,128)}, u32[]{:S(2)}) copy-start(f32[16,256]{1,0:T(8,128)} %get-tuple-element.58) | copy-start | bytes 49156
  142.1 3.4 %copy-start.25 = (f32[16,16]{1,0:T(8,128)S(1)}, f32[16,16]{1,0:T(8,128)}, u32[]{:S(2)}) copy-start(f32[16,16]{1,0:T(8,128)} %copy-done.22) | copy-start | bytes 3076
  152.7 3.0 %copy-start.35 = (f32[16,256]{1,0:T(8,128)S(1)}, f32[16,256]{1,0:T(8,128)}, u32[]{:S(2)}) copy-start(f32[16,256]{1,0:T(8,128)} %get-tuple-element.59) | copy-start | bytes 49156
  157.1 4.0 %copy-start.11 = (bf16[1024,256]{0,1:T(8,128)(2,1)S(1)}, bf16[1024,256]{0,1:T(8,128)(2,1)}, u32[]{:S(2)}) copy-start(bf16[1024,256]{0,1:T(8,128)(2,1)} %copy.102) | copy-start | bytes 1572868
  160.7 1.6 copy-start
  160.7 1.6 copy-start.2
  162.3 1.8 copy-start.33
  162.3 1.8 copy-start.34
  162.3 36.0 %copy-start.1 = (f32[1,1024,256]{1,2,0:T(8,128)S(1)}, f32[1,1024,256]{1,2,0:T(8,128)}, u32[]{:S(2)}) copy-start(f32[1,1024,256]{1,2,0:T(8,128)} %get-tuple-element.72) | copy-start | bytes 3145732
  162.3 36.0 %copy-start.3 = (f32[1,1024,256]{1,2,0:T(8,128)S(1)}, f32[1,1024,256]{1,2,0:T(8,128)}, u32[]{:S(2)}) copy-start(f32[1,1024,256]{1,2,0:T(8,128)} %get-tuple-element.73) | copy-start | bytes 3145732
  198.4 1.7 copy-start.7
  198.4 1.7 copy-start.38
  198.4 1.7 copy-start.39
  198.4 1.7 copy-start.40
  203.4 2.6 %copy-start.15 = (bf16[1024,256]{0,1:T(8,128)(2,1)S(1)}, bf16[1024,256]{0,1:T(8,128)(2,1)}, u32[]{:S(2)}) copy-start(bf16[1024,256]{0,1:T(8,128)(2,1)} %get-tuple-element.79) | copy-start | bytes 1572868
  (5 other events, 4.7 us)

commit v4 on v1

--- a/solution.py
+++ b/solution.py
@@ -178,9 +178,11 @@
         - jnp.arange(block_len, dtype=jnp.int32)[None, :]
     )
     lag_value = jnp.maximum(lag_index, 0).astype(jnp.float32)
-    pair_pow = jnp.exp(-decay_rates[:, :, None, None] * lag_value[None, None])
+    rise_pow = jnp.exp(rate_axis * lag_axis)
     toeplitz = jnp.where(
-        lag_index[None] >= 0, jnp.sum(mode_coefs[:, :, None, None] * pair_pow, axis=1), 0.0
+        lag_index[None] >= 0,
+        jnp.einsum("gnt,gns->gts", mode_coefs[:, :, None] * block_pow, rise_pow, precision=precise),
+        0.0,
     )
     z_blocks = grouped_z.reshape(block_count, block_len, group_count, members)
     e_blocks = grouped_e.reshape(block_count, block_len, group_count, members)
@@ -205,7 +207,6 @@
     gram_acc = jnp.einsum("btgm,bsgm->gts", e_blocks, z_wide, precision=precise)
     gram_low = jnp.where(lag_index[None] >= 0, gram_acc, 0.0)
     gram_pair = jnp.stack([gram_low, gram_low * lag_value[None]])
-    rise_pow = jnp.exp(rate_axis * lag_axis)
     gram_rise = jnp.einsum("kgts,gns->kgnt", gram_pair, rise_pow, precision=precise)
     first_in = jnp.sum(block_pow * gram_rise[0], axis=2)
     lag_in = jnp.sum(block_pow * gram_rise[1], axis=2)

time: 195 us -> 198 us (1.015)
  matrix products: 18.5 us -> 22.5 us
  other arithmetic: 53.8 us -> 51.2 us
    reduce_sum x1 -> x0, other arithmetic: 4.31 us -> none  [per_device(): jnp.sum(mode_coefs[:, :, None, None] * pair_pow, axis=1)]
    dot_general x0 -> x1, matrix products: none -> 2.72 us  [per_device(): jnp.einsum('gnt,gns->gts', mode_coefs[:, :, None] * block_pow, rise_pow,...]
    unnamed x116 -> x94, local copies, waits for them, and re-layouts: 13.7 us -> 13.6 us
where the time goes in v4:
time: 198 us; the launch traced here: 196 us
  Pallas kernels  60.3 us (30%)
  local copies, waits for them, and re-layouts  56.1 us (28%)
  other arithmetic  51.2 us (26%)
  matrix products  22.5 us (11%)
  starting transfers between devices  4.38 us (2%)
    pallas_call x1, Pallas kernels, gather_along(): pl.pallas_call(functools.partial(gather_kernel, axis, count), out_shape=j...  32.4 us
    pallas_call x1, Pallas kernels, finish_exchange(): pl.pallas_call(functools.partial(finish_kernel, fsdp_count, ctx_count), o...  27.8 us
    unnamed x94, local copies, waits for them, and re-layouts  13.6 us
    reduce_sum x1, other arithmetic, per_device(): jnp.sum(span_weight * (fresh_fwd[1][None] - block_len * block_steps * fre...  5.9 us
    another operation x2, other arithmetic, per_device(): jnp.stack([cotangent * inner_flat, grad_flat * value_part, grad_flat * ke...  5.25 us
    reduce_sum x1, other arithmetic, per_device(): jnp.sum(jnp.swapaxes(span_weight, 0, 1) * fresh_bwd[None], axis=1)  5.17 us
    add x1, other arithmetic, short_conv(): summed + taps_table[:, offset, None, :] * row_data[:, start_row:start_row...  4.8 us
    ppermute x1, starting transfers between devices, passed_along(): lax.ppermute(value, axis, [(source, source + steps) for source in range(l...  4.38 us
  transfers between devices with their start and end apart: 1, of which 0 were waited for; matrix products, arithmetic and copies ran while one was open for 8% of the time, Pallas kernels for 0%

profile of v4, /device:TPU:1, one launch (start us, length us, event | category | flops | bytes accessed | tf_op | source)
XLA Modules:
  0.0 196.3 jit_solution(14612471402373339364)
XLA Ops:
  1.7 4.4 %collective-permute-start = (bf16[3,2,256]{1,2,0:T(8,128)(2,1)S(1)}, bf16[3,2,256]{1,2,0:T(8,128)(2,1)S(1)}, u32[]{:S(2)}, u32[]{:S(2)}) collective-permute-start(bf16[3,2,256]{1,2,0:T(8,128)(2,1)S(1)} %copy.141), channel_id=1, source_target_pairs={{0,1},{1,2},{2,3},{3,4},{4,5},{5,6},{6,7},{7,8},{8,9},{9,10},{10,1... | collective-permute-start | bytes 9224 | tf_op jit(solution)/shard_map/ppermute | solution.py:133
  11.7 1.0 select_bitcast_fusion
  12.8 1.0 exponential_select_fusion.1
  15.3 1.4 copy.143
  16.6 1.7 copy.140
  22.8 4.8 %multiply_add_fusion = f32[3,1024,256]{1,2,0:T(8,128)S(1)} fusion(bf16[3,1024,256]{1,2,0:T(8,128)(2,1)} %copy.140, bf16[3,2,256]{1,2,0:T(8,128)(2,1)} %copy-done.20, f32[3,256]{1,0:T(4,128)S(1)} %get-tuple-element.100, f32[3,256]{1,0:T(4,128)S(1)} %get-tuple-element.101, f32[3,256]{1,0:T(4,128)} %bitcast.235), kind=kLoop, calls=%fused_computation.13 | loop fusion | flops 11010048 | bytes 4730880 | tf_op jit(solution)/shard_map/add | solution.py:141
  29.6 1.9 fusion.10
  33.1 1.6 slice_bitcast_fusion.3
  34.7 1.1 multiply_reduce_fusion.9
  35.8 2.6 %copy.152 = f32[8,16,16,16]{3,2,1,0:T(8,128)} copy(f32[8,16,16,16]{1,3,0,2:T(8,128)} %get-tuple-element.70) | data formatting | bytes 262144 | tf_op jit(solution)/shard_map/mul | solution.py:200
  38.3 2.6 %copy.162 = f32[8,16,16,16]{3,2,1,0:T(8,128)} copy(f32[8,16,16,16]{1,3,0,2:T(8,128)} %get-tuple-element.71) | data formatting | bytes 262144 | tf_op jit(solution)/shard_map/squeeze | solution.py:224
  40.9 5.9 %multiply_reduce_fusion.1 = (f32[8,16,16,16]{3,2,1,0:T(8,128)}, f32[8,16,16,16]{3,2,1,0:T(8,128)}) fusion(f32[8,8]{1,0:T(8,128)S(1)} %copy-done.35, f32[8,16,16,16]{3,2,1,0:T(8,128)} %copy.162, f32[8,16,16,16]{3,2,1,0:T(8,128)} %copy.152, f32[8,8,16,16]{3,2,1,0:T(8,128)} %exponential_select_fusion.1), kind=kLoop, calls=%fused_computation.1 | loop fusion | flops 1507328 | bytes 590080 | tf_op jit(solution)/shard_map/reduce_sum | solution.py:201
  46.8 2.7 %copy.164 = f32[8,16,16,16]{1,3,0,2:T(8,128)} copy(f32[8,16,16,16]{3,2,1,0:T(8,128)} %get-tuple-element.53) | data formatting | bytes 262144 | tf_op jit(solution)/shard_map/reduce_sum | solution.py:201
  49.5 2.6 %copy.168 = f32[8,16,16,16]{1,3,0,2:T(8,128)} copy(f32[8,16,16,16]{3,2,1,0:T(8,128)} %get-tuple-element.54) | data formatting | bytes 262144 | tf_op jit(solution)/shard_map/reduce_sum | solution.py:200
  52.1 3.4 %convolution_bitcast_fusion = f32[2,8,16,16,16]{2,4,1,3,0:T(8,128)S(1)} fusion(f32[8,128,16,16]{1,0,3,2:T(8,128)} %bitcast.219, f32[1,16,16,128]{3,2,0,1:T(8,128)S(1)} %copy-done.17, f32[1,16,16,128]{3,2,0,1:T(8,128)S(1)} %copy-done.16), kind=kOutput, calls=%fused_computation.19 | convolution fusion | flops 100728832 | bytes 1572864 | tf_op jit(solution)/shard_map/kgnt,btgm->kbngm/dot_general | solution.py:204
  55.6 3.4 %multiply_reduce_fusion.5 = (f32[16,16]{0,1:T(8,128)S(1)}, f32[16,16]{0,1:T(8,128)S(1)}, f32[16,16,16]{0,2,1:T(8,128)S(1)}, f32[16,16,16]{0,2,1:T(8,128)S(1)}, f32[8,16,16,16]{1,3,0,2:T(8,128)}) fusion(f32[8,16,16,16]{1,3,0,2:T(8,128)S(1)} %copy-done.5, f32[2,8,16,16,16]{2,4,1,3,0:T(8,128)S(1)} %convolution_bitcast_fusion, ...), kind=kOutput, calls=%fused_computation.51 | convolution fusion | flops 50748928 | bytes 1748000 | tf_op jit(solution)/shard_map/gnt,btgm->bngm/dot_general | solution.py:216
  59.6 1.4 stack.70
  61.0 1.3 bitcast_subtract_fusion
  63.0 1.8 pad_maximum_fusion.4
  64.9 2.1 %copy.158 = f32[4,16,16,16]{3,2,1,0:T(8,128)} copy(f32[4,16,16,16]{1,3,2,0:T(8,128)} %pad_maximum_fusion.4) | data formatting | bytes 131072 | tf_op jit(solution)/shard_map/stack | solution.py:232
  66.9 1.3 reshape.428
  69.5 32.4 %shard_map.84 = f32[16,72,256]{2,1,0:T(8,128)} custom-call(f32[72,256]{1,0:T(8,128)} %copy-done.18), custom_call_target="tpu_custom_call" | custom-call | tf_op jit(solution)/shard_map/pallas_call | solution.py:49
  102.9 2.3 %slice.150 = f32[16,64,256]{2,1,0:T(8,128)} slice(f32[16,72,256]{2,1,0:T(8,128)} %shard_map.84), slice={[0:16], [0:64], [0:256]} | slice | bytes 2097152 | tf_op jit(solution)/shard_map/slice | solution.py:243
  106.7 1.2 slice_bitcast_fusion.8
  107.9 3.1 %multiply_reduce_fusion.3 = (f32[16,16,256]{2,1,0:T(8,128)S(1)}, f32[16,16,256]{2,1,0:T(8,128)S(1)}) fusion(f32[16,16]{1,0:T(8,128)} %get-tuple-element.96, f32[16,16,256]{2,1,0:T(8,128)S(1)} %get-tuple-element.75, f32[16,16,256]{2,1,0:T(8,128)S(1)} %get-tuple-element.74, f32[16,16]{1,0:T(8,128)} %get-tuple-element.95, f32[16,256]{1,0:T(8,128)} %copy-done.21, ...), kind=kLoop, calls=%fused_computation.3 | loop fusion | flops 8257536 | bytes 1067264 | tf_op jit(solution)/shard_map/reduce_sum | solution.py:263
  111.0 1.6 multiply_reduce_fusion.11
  114.5 1.4 multiply_bitcast_fusion.1
  115.9 2.7 %fusion.8 = f32[16,128,128,1]{2,1,3,0:T(8,128)S(1)} fusion(pred[128,128]{1,0:T(8,128)(4,1)} %fusion.65, f32[16,16]{1,0:T(8,128)} %param.11, f32[16,16]{1,0:T(8,128)S(1)} %get-tuple-element.94, f32[16,16]{1,0:T(8,128)S(1)} %copy.145), kind=kOutput, calls=%fused_computation.30 | convolution fusion | flops 50692096 | bytes 1068032 | tf_op jit(solution)/shard_map/gnt,gns->gts/dot_general | solution.py:184
  118.7 3.5 %fusion.21 = f32[16,8,16,128]{3,2,1,0:T(8,128)} fusion(f32[16,128,128,1]{2,1,3,0:T(8,128)S(1)} %fusion.8, f32[8,128,16,16]{1,0,3,2:T(8,128)} %bitcast.220), kind=kOutput, calls=%fused_computation.59 | convolution fusion | flops 402653184 | bytes 3145728 | tf_op jit(solution)/shard_map/gts,btgm->bsgm/dot_general | solution.py:215
  122.1 1.9 fusion.27
  124.0 2.6 %copy.172 = f32[8,16,16,16]{3,2,1,0:T(8,128)} copy(f32[8,16,16,16]{1,3,0,2:T(8,128)} %get-tuple-element.99) | data formatting | bytes 262144 | tf_op jit(solution)/shard_map/gnt,btgm->bngm/transpose | solution.py:216
  126.6 5.2 %multiply_reduce_fusion = f32[8,16,16,16]{3,2,1,0:T(8,128)} fusion(f32[8,16,16,16]{3,2,1,0:T(8,128)} %copy.172, f32[8,8,16,16]{3,2,1,0:T(8,128)} %select_bitcast_fusion), kind=kLoop, calls=%fused_computation | loop fusion | flops 491520 | bytes 327680 | tf_op jit(solution)/shard_map/reduce_sum | solution.py:217
  131.8 2.6 %copy.175 = f32[8,16,16,16]{1,3,0,2:T(8,128)} copy(f32[8,16,16,16]{3,2,1,0:T(8,128)} %multiply_reduce_fusion) | data formatting | bytes 262144 | tf_op jit(solution)/shard_map/reduce_sum | solution.py:217
  135.3 2.9 %fusion.7 = f32[8,128,16,16]{1,3,0,2:T(8,128)S(1)} fusion(f32[16,8,16,128]{3,2,1,0:T(8,128)} %fusion.27, f32[8,16,16,16]{1,3,0,2:T(8,128)} %copy.168, f32[16,16,16]{0,2,1:T(8,128)S(1)} %bitcast.230, f32[8,16,16]{1,0,2:T(8,128)S(1)} %get-tuple-element.89, f32[16,16]{1,0:T(8,128)} %copy-done.23, f32[16,16]{1,0:T(8,128)S(1)} %get-tuple-element.94, ...), kind=kOutput, calls=%fused_computation.27 | convolution fusion | flops 50757632 | bytes 2255872 | tf_op jit(solution)/shard_map/gnt,bngm->btgm/dot_general | solution.py:282
  138.2 1.3 copy.169
  139.5 1.2 fusion.6
  140.7 1.3 copy.176
  142.0 2.4 %reshape_reshape.12 = f32[1,1024,256]{1,2,0:T(8,128)} reshape(f32[8,128,16,16]{1,0,3,2:T(8,128)} %copy.176) | data formatting | bytes 2097152 | tf_op jit(solution)/shard_map/reshape;reshape | solution.py:290
  144.4 3.0 %fusion.14 = (f32[1,1024,256]{1,2,0:T(8,128)}, bf16[1024,256]{0,1:T(8,128)(2,1)}) fusion(bf16[1024,256]{0,1:T(8,128)(2,1)} %copy.154, f32[32,8,8,128]{3,2,1,0:T(8,128)} %bitcast.228, f32[3,1024,256]{1,2,0:T(8,128)S(1)} %multiply_add_fusion), kind=kLoop, calls=%fused_computation.36 | loop fusion | flops 1048576 | bytes 4194304 | tf_op jit(solution)/shard_map/stack | solution.py:291
  147.4 1.7 slice_multiply_fusion.2
  149.2 2.0 %copy.183 = bf16[1024,256]{1,0:T(8,128)(2,1)} copy(bf16[1024,256]{0,1:T(8,128)(2,1)} %get-tuple-element.73) | data formatting | bytes 1048576
  151.2 2.2 %pad_maximum_fusion.1 = f32[3,1024,256]{1,2,0:T(8,128)S(1)} fusion(f32[1,1024,256]{1,2,0:T(8,128)} %get-tuple-element.69, f32[1,1024,256]{1,2,0:T(8,128)} %get-tuple-element.68, f32[1,1024,256]{1,2,0:T(8,128)} %get-tuple-element.72), kind=kLoop, calls=%fused_computation.12 | loop fusion | flops 1572864 | bytes 6291456 | tf_op jit(solution)/shard_map/stack | solution.py:291
  154.3 1.3 reshape.432.rim_ref
  156.2 1.2 broadcast_in_dim.114.tile_ref
  157.4 27.8 %shard_map.85 = (f32[32,8,128]{2,1,0:T(8,128)}, f32[6,256]{1,0:T(8,128)}) custom-call(f32[8,128]{1,0:T(8,128)} %broadcast_in_dim.114.tile_ref, f32[6,256]{1,0:T(8,128)} %reshape.432.rim_ref), custom_call_target="tpu_custom_call" | custom-call | tf_op jit(solution)/shard_map/pallas_call | solution.py:110
  185.2 1.5 slice_reduce_fusion.1
  190.5 3.3 %fusion.1 = bf16[3,1024,256]{1,2,0:T(8,128)(2,1)} fusion(f32[3,1026,256]{1,2,0:T(8,128)S(1)} %pad_maximum_fusion, f32[3,256]{1,0:T(4,128)S(1)} %copy-done.29, f32[3,256]{1,0:T(4,128)S(1)} %copy-done.31, f32[3,256]{1,0:T(4,128)S(1)} %bitcast.236, f32[1,1024,256]{1,2,0:T(8,128)S(1)} %copy-done.1, f32[1,1024,256]{1,2,0:T(8,128)S(1)} %copy-done, ...), kind=kLoop, calls=%fused_computation.9 | loop fusion | flops 6291456 | bytes 11019264 | tf_op jit(solution)/shard_map/convert_element_type | solution.py:301
  193.8 2.6 %copy.184 = bf16[3,1024,256]{2,1,0:T(8,128)(2,1)} copy(bf16[3,1024,256]{1,2,0:T(8,128)(2,1)} %fusion.1) | data formatting | bytes 3145728
  (151 shorter events, 28.4 us)
Async XLA Ops:
  0.6 16.0 %copy-start.14 = (bf16[3,1024,256]{2,1,0:T(8,128)(2,1)S(1)}, bf16[3,1024,256]{2,1,0:T(8,128)(2,1)}, u32[]{:S(2)}) copy-start(bf16[3,1024,256]{2,1,0:T(8,128)(2,1)} %param.9) | copy-start | bytes 4718596
  0.6 18.4 %copy-start.36 = (f32[16,16]{1,0:T(8,128)S(1)}, f32[16,16]{1,0:T(8,128)}, u32[]{:S(2)}) copy-start(f32[16,16]{1,0:T(8,128)} %param.12) | copy-start | bytes 3076
  0.7 20.5 %copy-start.15 = (bf16[1024,256]{1,0:T(8,128)(2,1)S(1)}, bf16[1024,256]{1,0:T(8,128)(2,1)}, u32[]{:S(2)}) copy-start(bf16[1024,256]{1,0:T(8,128)(2,1)} %param.13) | copy-start | bytes 1572868
  1.7 20.4 %collective-permute-start = (bf16[3,2,256]{1,2,0:T(8,128)(2,1)S(1)}, bf16[3,2,256]{1,2,0:T(8,128)(2,1)S(1)}, u32[]{:S(2)}, u32[]{:S(2)}) collective-permute-start(bf16[3,2,256]{1,2,0:T(8,128)(2,1)S(1)} %copy.141), channel_id=1, source_target_pairs={{0,1},{1,2},{2,3},{3,4},{4,5},{5,6},{6,7},{7,8},{8,9},{9,10},{10,1... | collective-permute-start | bytes 9224 | tf_op jit(solution)/shard_map/ppermute | solution.py:133
  7.3 12.4 %copy-start.37 = (f32[8]{0:T(128)}, f32[8]{0:T(128)S(1)}, u32[]{:S(2)}) copy-start(f32[8]{0:T(128)S(1)} %get-tuple-element.105) | copy-start | bytes 100
  7.3 12.4 %copy-start.38 = (f32[8]{0:T(128)}, f32[8]{0:T(128)S(1)}, u32[]{:S(2)}) copy-start(f32[8]{0:T(128)S(1)} %get-tuple-element.104) | copy-start | bytes 100
  11.6 8.1 %copy-start.23 = (f32[16,16]{1,0:T(8,128)}, f32[16,16]{1,0:T(8,128)S(1)}, u32[]{:S(2)}) copy-start(f32[16,16]{1,0:T(8,128)S(1)} %get-tuple-element.92) | copy-start | bytes 3076
  12.7 14.9 %copy-start.28 = (f32[3,256]{1,0:T(4,128)}, f32[3,256]{1,0:T(4,128)S(1)}, u32[]{:S(2)}) copy-start(f32[3,256]{1,0:T(4,128)S(1)} %get-tuple-element.100) | copy-start | bytes 9220
  12.7 14.9 %copy-start.30 = (f32[3,256]{1,0:T(4,128)}, f32[3,256]{1,0:T(4,128)S(1)}, u32[]{:S(2)}) copy-start(f32[3,256]{1,0:T(4,128)S(1)} %get-tuple-element.101) | copy-start | bytes 9220
  20.5 1.6 copy-start.21
  22.1 0.7 copy-start.20
  22.8 5.1 %copy-start.9 = (bf16[1024,256]{0,1:T(8,128)(2,1)S(1)}, bf16[1024,256]{0,1:T(8,128)(2,1)}, u32[]{:S(2)}) copy-start(bf16[1024,256]{0,1:T(8,128)(2,1)} %copy.154) | copy-start | bytes 1572868
  27.8 0.7 copy-start.27
  27.9 4.4 %copy-start.7 = (bf16[32,8,8,128]{3,2,1,0:T(8,128)(2,1)}, bf16[32,8,8,128]{3,2,1,0:T(8,128)(2,1)S(1)}, u32[]{:S(2)}) copy-start(bf16[32,8,8,128]{3,2,1,0:T(8,128)(2,1)S(1)} %copy.209) | copy-start | bytes 1572868
  28.3 1.2 copy-start.2
  28.5 1.0 copy-start.19
  28.5 1.1 copy-start.22
  32.3 2.4 %copy-start.39 = (f32[8]{0:T(128)S(1)}, f32[8]{0:T(128)}, u32[]{:S(2)}) copy-start(f32[8]{0:T(128)} %copy-done.38) | copy-start | bytes 100
  34.7 6.2 %copy-start.35 = (f32[8,8]{1,0:T(8,128)S(1)}, f32[8,8]{1,0:T(8,128)}, u32[]{:S(2)}) copy-start(f32[8,8]{1,0:T(8,128)} %copy.163) | copy-start | bytes 772
  46.8 5.3 %copy-start.16 = (f32[1,16,16,128]{3,2,0,1:T(8,128)S(1)}, f32[1,16,16,128]{3,2,0,1:T(8,128)}, u32[]{:S(2)}) copy-start(f32[1,16,16,128]{3,2,0,1:T(8,128)} %get-tuple-element.81) | copy-start | bytes 393220
  46.8 5.3 %copy-start.17 = (f32[1,16,16,128]{3,2,0,1:T(8,128)S(1)}, f32[1,16,16,128]{3,2,0,1:T(8,128)}, u32[]{:S(2)}) copy-start(f32[1,16,16,128]{3,2,0,1:T(8,128)} %get-tuple-element.82) | copy-start | bytes 393220
  52.1 3.4 %copy-start.3 = (f32[32,8,8,128]{3,2,1,0:T(8,128)S(1)}, f32[32,8,8,128]{3,2,1,0:T(8,128)}, u32[]{:S(2)}) copy-start(f32[32,8,8,128]{3,2,1,0:T(8,128)} %copy-done.2) | copy-start | bytes 3145732
  52.1 3.4 %copy-start.5 = (f32[8,16,16,16]{1,3,0,2:T(8,128)S(1)}, f32[8,16,16,16]{1,3,0,2:T(8,128)}, u32[]{:S(2)}) copy-start(f32[8,16,16,16]{1,3,0,2:T(8,128)} %copy.168) | copy-start | bytes 393220
  52.1 3.4 %copy-start.13 = (f32[8,16,16,16]{1,3,0,2:T(8,128)S(1)}, f32[8,16,16,16]{1,3,0,2:T(8,128)}, u32[]{:S(2)}) copy-start(f32[8,16,16,16]{1,3,0,2:T(8,128)} %copy.164) | copy-start | bytes 393220
  55.5 3.5 %copy-start.33 = (f32[16,16]{1,0:T(8,128)S(1)}, f32[16,16]{1,0:T(8,128)}, u32[]{:S(2)}) copy-start(f32[16,16]{1,0:T(8,128)} %get-tuple-element.63) | copy-start | bytes 3076
  68.9 0.6 copy-start.18
  102.9 11.6 %copy-start.34 = (f32[16,16]{0,1:T(8,128)S(1)}, f32[16,16]{0,1:T(8,128)}, u32[]{:S(2)}) copy-start(f32[16,16]{0,1:T(8,128)} %copy.143) | copy-start | bytes 3076
  106.7 4.3 %copy-start.6 = (f32[16,64,256]{2,1,0:T(8,128)S(1)}, f32[16,64,256]{2,1,0:T(8,128)}, u32[]{:S(2)}) copy-start(f32[16,64,256]{2,1,0:T(8,128)} %slice.150) | copy-start | bytes 3145732
  115.9 6.2 %copy-start.8 = (bf16[32,8,8,128]{3,2,1,0:T(8,128)(2,1)S(1)}, bf16[32,8,8,128]{3,2,1,0:T(8,128)(2,1)}, u32[]{:S(2)}) copy-start(bf16[32,8,8,128]{3,2,1,0:T(8,128)(2,1)} %copy-done.7) | copy-start | bytes 1572868
  124.0 10.4 %copy-start.26 = (f32[16,256]{1,0:T(8,128)S(1)}, f32[16,256]{1,0:T(8,128)}, u32[]{:S(2)}) copy-start(f32[16,256]{1,0:T(8,128)} %get-tuple-element.57) | copy-start | bytes 49156
  135.3 4.2 %copy-start.10 = (f32[16,8,16,128]{3,2,1,0:T(8,128)S(1)}, f32[16,8,16,128]{3,2,1,0:T(8,128)}, u32[]{:S(2)}) copy-start(f32[16,8,16,128]{3,2,1,0:T(8,128)} %fusion.21) | copy-start | bytes 3145732
  135.3 4.2 %copy-start.12 = (f32[8,16,16,16]{1,3,0,2:T(8,128)S(1)}, f32[8,16,16,16]{1,3,0,2:T(8,128)}, u32[]{:S(2)}) copy-start(f32[8,16,16,16]{1,3,0,2:T(8,128)} %copy.175) | copy-start | bytes 393220
  135.3 4.2 %copy-start.40 = (f32[128]{0:T(128)S(1)}, f32[128]{0:T(128)}, u32[]{:S(2)}) copy-start(f32[128]{0:T(128)} %iota_subtract_fusion.2) | copy-start | bytes 1540
  144.4 3.0 %copy-start.11 = (f32[1,1024,256]{1,2,0:T(8,128)S(1)}, f32[1,1024,256]{1,2,0:T(8,128)}, u32[]{:S(2)}) copy-start(f32[1,1024,256]{1,2,0:T(8,128)} %reshape_reshape.12) | copy-start | bytes 3145732
  151.2 4.4 %copy-start.24 = (f32[1,16,16]{1,2,0:T(8,128)S(1)}, f32[1,16,16]{1,2,0:T(8,128)}, u32[]{:S(2)}) copy-start(f32[1,16,16]{1,2,0:T(8,128)} %get-tuple-element.76) | copy-start | bytes 3076
  151.2 4.4 %copy-start.25 = (f32[1,16,16]{1,2,0:T(8,128)S(1)}, f32[1,16,16]{1,2,0:T(8,128)}, u32[]{:S(2)}) copy-start(f32[1,16,16]{1,2,0:T(8,128)} %get-tuple-element.77) | copy-start | bytes 3076
  151.2 38.5 %copy-start = (f32[1,1024,256]{1,2,0:T(8,128)S(1)}, f32[1,1024,256]{1,2,0:T(8,128)}, u32[]{:S(2)}) copy-start(f32[1,1024,256]{1,2,0:T(8,128)} %get-tuple-element.68) | copy-start | bytes 3145732
  151.2 38.6 %copy-start.1 = (f32[1,1024,256]{1,2,0:T(8,128)S(1)}, f32[1,1024,256]{1,2,0:T(8,128)}, u32[]{:S(2)}) copy-start(f32[1,1024,256]{1,2,0:T(8,128)} %get-tuple-element.69) | copy-start | bytes 3145732
  151.2 38.6 %copy-start.4 = (f32[1,1024,256]{1,2,0:T(8,128)S(1)}, f32[1,1024,256]{1,2,0:T(8,128)}, u32[]{:S(2)}) copy-start(f32[1,1024,256]{1,2,0:T(8,128)} %get-tuple-element.72) | copy-start | bytes 3145732
  189.8 0.7 copy-start.29
  189.8 0.7 copy-start.31
  189.8 0.7 copy-start.32

commit v5 on v1

--- a/solution.py
+++ b/solution.py
@@ -61,7 +61,8 @@
 
 
 def finish_kernel(
-    fsdp_count, ctx_count, tile_ref, rim_ref, tiles_out, rim_out, tiles_held, rim_held,
+    fsdp_count, ctx_count, tile_ref, rim_ref, cot_ref, inner_ref, grad_ref, value_ref, key_ref,
+    taps_ref, tiles_out, grads_out, tiles_held, rim_held, adj_buf,
     send_sem, recv_sem, rim_send_sem, rim_recv_sem,
 ):
     f_me = lax.axis_index("fsdp")
@@ -96,35 +97,62 @@
         )
         copy.start()
         copies.append(copy)
+    tokens = cot_ref.shape[0]
+    rim_rows = rim_ref.shape[0] // 3
+    shifts = taps_ref.shape[1]
+    adj_buf[0, :tokens] = cot_ref[...].astype(jnp.float32) * inner_ref[...]
+    adj_buf[1, :tokens] = grad_ref[...] * value_ref[...]
+    adj_buf[2, :tokens] = grad_ref[...] * key_ref[...]
+    early = tokens - 16
+
+    def conv_rows(start, count):
+        for part in range(3):
+            total = jnp.zeros((count, adj_buf.shape[2]), jnp.float32)
+            for offset in range(shifts):
+                total = total + taps_ref[part, offset][None, :] * adj_buf[
+                    part, start + offset : start + offset + count
+                ]
+            grads_out[part, start : start + count] = total.astype(grads_out.dtype)
+
+    conv_rows(0, early)
     for copy in copies:
         copy.wait()
     rim_copy.wait()
+    keep = jnp.where(c_me == ctx_count - 1, 0.0, 1.0)
+    for part in range(3):
+        adj_buf[part, tokens : tokens + rim_rows] = (
+            rim_held[part * rim_rows : (part + 1) * rim_rows] * keep
+        )
+    conv_rows(early, tokens - early)
     tiles_held[f_me] = tile_ref[...]
     tiles_out[...] = tiles_held[...]
-    rim_out[...] = rim_held[...]
-
-
-def finish_exchange(tile, rim):
+
+
+def finish_exchange(tile, rim, cot, inner, grad, value, key, taps):
     fsdp_count = lax.axis_size("fsdp")
     ctx_count = lax.axis_size("ctx")
+    tokens, channels = cot.shape
+    rim_rows = rim.shape[0] // 3
+    pad_rows = -(-(tokens + rim_rows) // 8) * 8
     return pl.pallas_call(
         functools.partial(finish_kernel, fsdp_count, ctx_count),
         out_shape=(
             jax.ShapeDtypeStruct((fsdp_count,) + tile.shape, tile.dtype),
-            jax.ShapeDtypeStruct(rim.shape, rim.dtype),
+            jax.ShapeDtypeStruct((3, tokens, channels), jnp.bfloat16),
         ),
-        in_specs=[pl.BlockSpec(memory_space=pltpu.VMEM)] * 2,
+        in_specs=[pl.BlockSpec(memory_space=pltpu.VMEM)] * 8,
         out_specs=(pl.BlockSpec(memory_space=pltpu.VMEM), pl.BlockSpec(memory_space=pltpu.VMEM)),
         scratch_shapes=[
             pltpu.VMEM((fsdp_count,) + tile.shape, tile.dtype),
             pltpu.VMEM(rim.shape, rim.dtype),
+            pltpu.VMEM((3, pad_rows, channels), jnp.float32),
             pltpu.SemaphoreType.DMA((fsdp_count - 1,)),
             pltpu.SemaphoreType.DMA((fsdp_count - 1,)),
             pltpu.SemaphoreType.DMA(()),
             pltpu.SemaphoreType.DMA(()),
         ],
         compiler_params=pltpu.CompilerParams(collective_id=1, has_side_effects=True),
-    )(tile, rim)
+    )(tile, rim, cot, inner, grad, value, key, taps)
 
 
 def passed_along(value, axis, steps):
@@ -287,17 +315,22 @@
     inner_flat = inner_sum.reshape(tokens, channels)
     mixer_output = (query_part * inner_flat).astype(jnp.bfloat16)
     grad_flat = product_grad.reshape(tokens, channels)
-    feature_adj = jnp.stack([cotangent * inner_flat, grad_flat * value_part, grad_flat * key_part])
+    rim_adj = jnp.stack(
+        [
+            cotangent[:rim_rows] * inner_flat[:rim_rows],
+            grad_flat[:rim_rows] * value_part[:rim_rows],
+            grad_flat[:rim_rows] * key_part[:rim_rows],
+        ]
+    )
     filter_local = jnp.stack([gain_part, rate_part])
     entry_count = 2 * group_count * order_count * lax.axis_size("fsdp")
     summed = filter_local
     square_tile = jnp.full((8, 128), jnp.sum(summed * summed), jnp.float32)
-    rim_send = feature_adj[:, :rim_rows, :].reshape(3 * rim_rows, channels)
-    square_tiles, rim_got = finish_exchange(square_tile, rim_send)
+    rim_send = rim_adj.reshape(3 * rim_rows, channels)
+    square_tiles, feature_grads = finish_exchange(
+        square_tile, rim_send, cotangent, inner_flat, grad_flat, value_part, key_part, short_taps
+    )
     squares = jnp.sum(square_tiles[:, 0, 0])
-    later_rows = jnp.where(ctx_index == ctx_count - 1, 0.0, rim_got).reshape(3, rim_rows, channels)
-    appended = jnp.concatenate([feature_adj, later_rows], axis=1)
-    feature_grads = short_conv(short_taps, appended, tokens, rim_rows, False).astype(jnp.bfloat16)
     factor = jnp.minimum(1.0, lax.rsqrt(squares / entry_count + 1e-06))
     clipped = summed * factor
     return (mixer_output, feature_grads, clipped[0], clipped[1])

time: 195 us -> 166 us (0.85)
  local copies, waits for them, and re-layouts: 54.8 us -> 39.9 us
  other arithmetic: 53.8 us -> 41.1 us
  matrix products: 18.5 us -> 14.5 us
  Pallas kernels: 60.4 us -> 62.7 us
    add x1, other arithmetic: 4.79 us -> 1.03 us  [short_conv(): summed + taps_table[:, offset, None, :] * row_data[:, start_row:start_row...]
    another operation x2 -> x3, other arithmetic: 5.25 us -> 1.51 us  [per_device(): jnp.stack([cotangent[:rim_rows] * inner_flat[:rim_rows], grad_flat[:rim_r...]
    pallas_call x1, Pallas kernels: 27.8 us -> 30.1 us  [finish_exchange(): pl.pallas_call(functools.partial(finish_kernel, fsdp_count, ctx_count), o...]
    another operation x1, local copies, waits for them, and re-layouts: 2.4 us -> 0.33 us  [per_device(): grad_flat = product_grad.reshape(tokens, channels)]
    unnamed x116 -> x79, local copies, waits for them, and re-layouts: 13.7 us -> 11.9 us
where the time goes in v5:
time: 166 us; the launch traced here: 165 us
  Pallas kernels  62.7 us (38%)
  other arithmetic  41.1 us (25%)
  local copies, waits for them, and re-layouts  39.9 us (24%)
  matrix products  14.5 us (9%)
  starting transfers between devices  4.36 us (3%)
  between operations  2.03 us (1%)
    pallas_call x1, Pallas kernels, gather_along(): pl.pallas_call(functools.partial(gather_kernel, axis, count), out_shape=j...  32.6 us
    pallas_call x1, Pallas kernels, finish_exchange(): pl.pallas_call(functools.partial(finish_kernel, fsdp_count, ctx_count), o...  30.1 us
    unnamed x79, local copies, waits for them, and re-layouts  11.9 us
    reduce_sum x1, other arithmetic, per_device(): jnp.sum(span_weight * (fresh_fwd[1][None] - block_len * block_steps * fre...  5.78 us
    reduce_sum x1, other arithmetic, per_device(): jnp.sum(jnp.swapaxes(span_weight, 0, 1) * fresh_bwd[None], axis=1)  4.77 us
    reduce_sum x1, other arithmetic, per_device(): jnp.sum(mode_coefs[:, :, None, None] * pair_pow, axis=1)  4.53 us
    ppermute x1, starting transfers between devices, passed_along(): lax.ppermute(value, axis, [(source, source + steps) for source in range(l...  4.36 us
    dot_general x1, matrix products, per_device(): jnp.einsum('gnt,btgm->bngm', block_pow, e_blocks, precision=precise)  3.38 us
  transfers between devices with their start and end apart: 1, of which 0 were waited for; matrix products, arithmetic and copies ran while one was open for 8% of the time, Pallas kernels for 0%

profile of v5, /device:TPU:1, one launch (start us, length us, event | category | flops | bytes accessed | tf_op | source)
XLA Modules:
  0.0 164.6 jit_solution(6084244238549075745)
XLA Ops:
  0.6 0.8 slice.149
  1.5 4.4 %collective-permute-start = (bf16[3,2,256]{2,1,0:T(2,128)(2,1)S(1)}, bf16[3,2,256]{2,1,0:T(2,128)(2,1)S(1)}, u32[]{:S(2)}, u32[]{:S(2)}) collective-permute-start(bf16[3,2,256]{2,1,0:T(2,128)(2,1)S(1)} %slice.149), channel_id=1, source_target_pairs={{0,1},{1,2},{2,3},{3,4},{4,5},{5,6},{6,7},{7,8},{8,9},{9,10},{10,1... | collective-permute-start | bytes 9224 | tf_op jit(solution)/shard_map/ppermute | solution.py:161
  9.7 0.8 fusion.83
  11.5 1.0 select_bitcast_fusion
  12.5 1.0 exponential_select_fusion.1
  13.6 0.8 exponential_multiply_fusion
  15.0 1.4 copy.141
  17.9 1.4 copy.142
  19.2 1.0 multiply_add_fusion
  20.3 1.7 %copy-done = f32[3,1024,256]{2,1,0:T(8,128)} copy-done((f32[3,1024,256]{2,1,0:T(8,128)}, f32[3,1024,256]{2,1,0:T(8,128)S(1)}, u32[]{:S(2)}) %copy-start) | copy-done | bytes 3145752
  21.9 1.5 slice_bitcast_fusion.6
  23.8 0.8 copy-done.4
  25.4 1.6 slice_bitcast_fusion.3
  27.0 1.7 %copy.150 = f32[8,16,16,16]{3,2,1,0:T(8,128)S(1)} copy(f32[8,16,16,16]{1,3,0,2:T(8,128)} %get-tuple-element.65) | data formatting | bytes 262144 | tf_op jit(solution)/shard_map/mul | solution.py:226
  28.7 2.6 %copy.160 = f32[8,16,16,16]{3,2,1,0:T(8,128)} copy(f32[8,16,16,16]{1,3,0,2:T(8,128)} %get-tuple-element.66) | data formatting | bytes 262144 | tf_op jit(solution)/shard_map/squeeze | solution.py:251
  31.4 5.8 %multiply_reduce_fusion.2 = (f32[8,16,16,16]{3,2,1,0:T(8,128)}, f32[8,16,16,16]{3,2,1,0:T(8,128)}) fusion(f32[8,8]{1,0:T(8,128)S(1)} %copy-done.22, f32[8,16,16,16]{3,2,1,0:T(8,128)} %copy.160, f32[8,16,16,16]{3,2,1,0:T(8,128)S(1)} %copy.150, f32[8,8,16,16]{3,2,1,0:T(8,128)} %exponential_select_fusion.1), kind=kLoop, calls=%fused_computation.2 | loop fusion | flops 1507328 | bytes 590080 | tf_op jit(solution)/shard_map/reduce_sum | solution.py:227
  37.1 2.7 %copy.166 = f32[8,16,16,16]{1,3,0,2:T(8,128)} copy(f32[8,16,16,16]{3,2,1,0:T(8,128)} %get-tuple-element.46) | data formatting | bytes 262144 | tf_op jit(solution)/shard_map/reduce_sum | solution.py:226
  39.8 2.6 %copy.162 = f32[8,16,16,16]{1,3,0,2:T(8,128)} copy(f32[8,16,16,16]{3,2,1,0:T(8,128)} %get-tuple-element.45) | data formatting | bytes 262144 | tf_op jit(solution)/shard_map/reduce_sum | solution.py:227
  42.4 1.5 convert_multiply_fusion
  43.9 1.3 copy.152
  45.3 1.4 copy.210
  46.7 2.1 %fusion.5 = f32[16,128,128]{2,1,0:T(8,128)S(1)} fusion(f32[8,128,16,16]{1,0,3,2:T(8,128)S(1)} %bitcast.238, bf16[8,128,16,16]{1,0,3,2:T(8,128)(2,1)} %bitcast.245, pred[128,128]{1,0:T(8,128)(4,1)S(1)} %copy-done.14), kind=kOutput, calls=%fused_computation.23 | convolution fusion | flops 402915328 | bytes 2637824 | tf_op jit(solution)/shard_map/btgm,bsgm->gts/dot_general | solution.py:233
  48.9 1.9 %fusion.6 = f32[2,16,16,128]{3,2,0,1:T(8,128)S(1)} fusion(f32[16,16]{1,0:T(8,128)S(1)} %copy-done.18, f32[1,16,128,128]{3,2,1,0:T(8,128)S(1)} %multiply_bitcast_fusion, f32[1,16,128,128]{3,2,1,0:T(8,128)S(1)} %bitcast.248), kind=kOutput, calls=%fused_computation.24 | convolution fusion | flops 101220352 | bytes 2360320 | tf_op jit(solution)/shard_map/kgts,gns->kgnt/dot_general | solution.py:237
  50.8 0.8 fusion.43
  51.6 2.0 %convolution_bitcast_fusion = f32[2,8,16,16,16]{2,4,1,3,0:T(8,128)S(1)} fusion(f32[8,128,16,16]{1,0,3,2:T(8,128)S(1)} %bitcast.239, f32[1,16,16,128]{3,2,0,1:T(8,128)S(1)} %copy-done.10, f32[1,16,16,128]{3,2,0,1:T(8,128)S(1)} %copy-done.9), kind=kOutput, calls=%fused_computation.11 | convolution fusion | flops 100728832 | bytes 1572864 | tf_op jit(solution)/shard_map/kgnt,btgm->kbngm/dot_general | solution.py:230
  53.7 3.4 %multiply_reduce_fusion.6 = (f32[16,16]{0,1:T(8,128)S(1)}, f32[16,16]{0,1:T(8,128)}, f32[16,16,16]{0,2,1:T(8,128)S(1)}, f32[16,16,16]{0,2,1:T(8,128)S(1)}, f32[8,16,16,16]{1,3,0,2:T(8,128)}) fusion(f32[8,16,16,16]{1,3,0,2:T(8,128)S(1)} %copy-done.2, f32[2,8,16,16,16]{2,4,1,3,0:T(8,128)S(1)} %convolution_bitcast_fusion, f32[8,16,16,16]{1,3,0,2:T(8,128)S(1)} %copy-done.7, ...), kind=kOutput, calls=%fused_computation.44 | convolution fusion | flops 50748928 | bytes 1748000 | tf_op jit(solution)/shard_map/gnt,btgm->bngm/dot_general | solution.py:243
  57.6 1.4 stack.74
  59.0 1.3 bitcast_subtract_fusion
  60.3 1.3 stack.75
  61.7 1.0 multiply_reduce_fusion.10
  64.6 32.6 %shard_map.84 = f32[16,72,256]{2,1,0:T(8,128)} custom-call(f32[72,256]{1,0:T(8,128)} %copy-done.11), custom_call_target="tpu_custom_call" | custom-call | tf_op jit(solution)/shard_map/pallas_call | solution.py:49
  97.2 1.4 slice.162
  98.6 0.9 slice_reduce_fusion
  99.6 2.2 %multiply_reduce_fusion.4 = (f32[16,16,256]{2,1,0:T(8,128)S(1)}, f32[16,16,256]{2,1,0:T(8,128)S(1)}) fusion(f32[16,16]{1,0:T(8,128)S(1)} %copy-done.24, f32[16,16,256]{2,1,0:T(8,128)S(1)} %get-tuple-element.68, f32[16,16,256]{2,1,0:T(8,128)S(1)} %get-tuple-element.67, f32[16,16]{1,0:T(8,128)S(1)} %copy-done.23, f32[16,256]{1,0:T(8,128)S(1)} %copy-done.17, ...), kind=kLoop, calls=%fused_computation.4 | loop fusion | flops 8257536 | bytes 1067264 | tf_op jit(solution)/shard_map/reduce_sum | solution.py:290
  103.0 4.5 %multiply_reduce_fusion = f32[16,128,128]{2,1,0:T(8,128)S(1)} fusion(f32[128,128]{1,0:T(8,128)S(1)} %copy-done.13, f32[16,16]{1,0:T(8,128)S(1)} %get-tuple-element.87, f32[16,16]{1,0:T(8,128)S(1)} %copy.143), kind=kLoop, calls=%fused_computation | loop fusion | flops 12320768 | bytes 1116160 | tf_op jit(solution)/shard_map/reduce_sum | solution.py:211
  107.5 1.2 fusion.9
  108.8 0.8 fusion.11
  109.7 1.2 fusion.4
  112.6 2.1 %multiply_convert_fusion = bf16[1024,256]{1,0:T(8,128)(2,1)} fusion(f32[1024,256]{1,0:T(8,128)S(1)} %copy.169.inner_ref, f32[3,1024,256]{2,1,0:T(8,128)} %copy-done), kind=kLoop, calls=%fused_computation.39 | loop fusion | flops 524288 | bytes 2621440 | tf_op jit(solution)/shard_map/convert_element_type | solution.py:316
  114.8 1.7 %copy.178 = f32[8,16,16,16]{3,2,1,0:T(8,128)S(1)} copy(f32[8,16,16,16]{1,3,0,2:T(8,128)} %get-tuple-element.92) | data formatting | bytes 262144 | tf_op jit(solution)/shard_map/gnt,btgm->bngm/transpose | solution.py:243
  116.5 4.8 %multiply_reduce_fusion.1 = f32[8,16,16,16]{3,2,1,0:T(8,128)} fusion(f32[8,16,16,16]{3,2,1,0:T(8,128)S(1)} %copy.178, f32[8,8,16,16]{3,2,1,0:T(8,128)} %select_bitcast_fusion), kind=kLoop, calls=%fused_computation.1 | loop fusion | flops 491520 | bytes 327680 | tf_op jit(solution)/shard_map/reduce_sum | solution.py:244
  121.3 1.7 %copy.180 = f32[8,16,16,16]{1,3,0,2:T(8,128)S(1)} copy(f32[8,16,16,16]{3,2,1,0:T(8,128)} %multiply_reduce_fusion.1) | data formatting | bytes 262144 | tf_op jit(solution)/shard_map/reduce_sum | solution.py:244
  122.9 1.2 fusion.3
  125.0 0.8 fusion.77
  127.0 1.2 broadcast_in_dim.108.tile_ref
  128.2 30.1 %shard_map.85 = (f32[32,8,128]{2,1,0:T(8,128)}, bf16[3,1024,256]{2,1,0:T(8,128)(2,1)}) custom-call(f32[8,128]{1,0:T(8,128)} %broadcast_in_dim.108.tile_ref, f32[6,256]{1,0:T(8,128)} %reshape.446.rim_ref, bf16[1024,256]{1,0:T(8,128)(2,1)} %cot_ref.1, f32[1024,256]{1,0:T(8,128)} %copy-done.1, f32[1024,256]{1,0:T(8,128)} %copy-done.6, ...), custom_call_target="tpu_custom_call" | custom-call | tf_op jit(solution)/shard_map/pallas_call | solution.py:137
  158.3 1.5 slice_reduce_fusion.1
  161.9 2.7 %copy.243 = bf16[3,1024,256]{2,1,0:T(8,128)(2,1)} copy(bf16[3,1024,256]{2,1,0:T(8,128)(2,1)} %get-tuple-element.108) | data formatting | bytes 3145728
  (132 shorter events, 17.0 us)
Async XLA Ops:
  0.6 18.6 %copy-start.8 = (bf16[3,1024,256]{2,1,0:T(8,128)(2,1)S(1)}, bf16[3,1024,256]{2,1,0:T(8,128)(2,1)}, u32[]{:S(2)}) copy-start(bf16[3,1024,256]{2,1,0:T(8,128)(2,1)} %param.9) | copy-start | bytes 4718596
  1.5 17.8 %collective-permute-start = (bf16[3,2,256]{2,1,0:T(2,128)(2,1)S(1)}, bf16[3,2,256]{2,1,0:T(2,128)(2,1)S(1)}, u32[]{:S(2)}, u32[]{:S(2)}) collective-permute-start(bf16[3,2,256]{2,1,0:T(2,128)(2,1)S(1)} %slice.149), channel_id=1, source_target_pairs={{0,1},{1,2},{2,3},{3,4},{4,5},{5,6},{6,7},{7,8},{8,9},{9,10},{10,1... | collective-permute-start | bytes 9224 | tf_op jit(solution)/shard_map/ppermute | solution.py:161
  5.9 10.4 %copy-start.25 = (f32[8]{0:T(128)}, f32[8]{0:T(128)S(1)}, u32[]{:S(2)}) copy-start(f32[8]{0:T(128)S(1)} %get-tuple-element.98) | copy-start | bytes 100
  5.9 10.4 %copy-start.32 = (f32[8]{0:T(128)}, f32[8]{0:T(128)S(1)}, u32[]{:S(2)}) copy-start(f32[8]{0:T(128)S(1)} %get-tuple-element.97) | copy-start | bytes 100
  17.2 6.2 %copy-start.16 = (f32[16,256]{1,0:T(8,128)}, f32[16,256]{1,0:T(8,128)S(1)}, u32[]{:S(2)}) copy-start(f32[16,256]{1,0:T(8,128)S(1)} %neg.50) | copy-start | bytes 49156
  20.3 1.7 %copy-start = (f32[3,1024,256]{2,1,0:T(8,128)}, f32[3,1024,256]{2,1,0:T(8,128)S(1)}, u32[]{:S(2)}) copy-start(f32[3,1024,256]{2,1,0:T(8,128)S(1)} %multiply_add_fusion) | copy-start | bytes 9437188
  23.8 0.8 copy-start.4
  27.0 4.3 %copy-start.22 = (f32[8,8]{1,0:T(8,128)S(1)}, f32[8,8]{1,0:T(8,128)}, u32[]{:S(2)}) copy-start(f32[8,8]{1,0:T(8,128)} %copy.161) | copy-start | bytes 772
  42.4 4.3 %copy-start.14 = (pred[128,128]{1,0:T(8,128)(4,1)S(1)}, pred[128,128]{1,0:T(8,128)(4,1)}, u32[]{:S(2)}) copy-start(pred[128,128]{1,0:T(8,128)(4,1)} %fusion.64) | copy-start | bytes 49156
  46.7 2.1 %copy-start.12 = (f32[128,128]{1,0:T(8,128)S(1)}, f32[128,128]{1,0:T(8,128)}, u32[]{:S(2)}) copy-start(f32[128,128]{1,0:T(8,128)} %maximum_convert_fusion) | copy-start | bytes 196612
  46.7 2.2 %copy-start.18 = (f32[16,16]{1,0:T(8,128)S(1)}, f32[16,16]{1,0:T(8,128)}, u32[]{:S(2)}) copy-start(f32[16,16]{1,0:T(8,128)} %param.11) | copy-start | bytes 3076
  48.8 2.8 %copy-start.9 = (f32[1,16,16,128]{3,2,0,1:T(8,128)S(1)}, f32[1,16,16,128]{3,2,0,1:T(8,128)}, u32[]{:S(2)}) copy-start(f32[1,16,16,128]{3,2,0,1:T(8,128)} %get-tuple-element.74) | copy-start | bytes 393220
  48.8 2.8 %copy-start.10 = (f32[1,16,16,128]{3,2,0,1:T(8,128)S(1)}, f32[1,16,16,128]{3,2,0,1:T(8,128)}, u32[]{:S(2)}) copy-start(f32[1,16,16,128]{3,2,0,1:T(8,128)} %get-tuple-element.75) | copy-start | bytes 393220
  48.9 4.8 %copy-start.2 = (f32[8,16,16,16]{1,3,0,2:T(8,128)S(1)}, f32[8,16,16,16]{1,3,0,2:T(8,128)}, u32[]{:S(2)}) copy-start(f32[8,16,16,16]{1,3,0,2:T(8,128)} %copy.166) | copy-start | bytes 393220
  48.9 4.8 %copy-start.7 = (f32[8,16,16,16]{1,3,0,2:T(8,128)S(1)}, f32[8,16,16,16]{1,3,0,2:T(8,128)}, u32[]{:S(2)}) copy-start(f32[8,16,16,16]{1,3,0,2:T(8,128)} %copy.162) | copy-start | bytes 393220
  48.9 4.8 %copy-start.26 = (f32[8]{0:T(128)S(1)}, f32[8]{0:T(128)}, u32[]{:S(2)}) copy-start(f32[8]{0:T(128)} %copy-done.25) | copy-start | bytes 100
  62.7 36.9 %copy-start.17 = (f32[16,256]{1,0:T(8,128)S(1)}, f32[16,256]{1,0:T(8,128)}, u32[]{:S(2)}) copy-start(f32[16,256]{1,0:T(8,128)} %copy-done.16) | copy-start | bytes 49156
  62.7 36.9 %copy-start.23 = (f32[16,16]{1,0:T(8,128)S(1)}, f32[16,16]{1,0:T(8,128)}, u32[]{:S(2)}) copy-start(f32[16,16]{1,0:T(8,128)} %get-tuple-element.88) | copy-start | bytes 3076
  62.7 36.9 %copy-start.24 = (f32[16,16]{1,0:T(8,128)S(1)}, f32[16,16]{1,0:T(8,128)}, u32[]{:S(2)}) copy-start(f32[16,16]{1,0:T(8,128)} %get-tuple-element.89) | copy-start | bytes 3076
  62.7 36.9 %copy-start.31 = (pred[16,16]{1,0:T(8,128)(4,1)S(1)}, pred[16,16]{1,0:T(8,128)(4,1)}, u32[]{:S(2)}) copy-start(pred[16,16]{1,0:T(8,128)(4,1)} %subtract_compare_fusion) | copy-start | bytes 772
  63.9 0.6 copy-start.11
  64.6 37.3 %copy-start.19 = (f32[16,256]{1,0:T(8,128)S(1)}, f32[16,256]{1,0:T(8,128)}, u32[]{:S(2)}) copy-start(f32[16,256]{1,0:T(8,128)} %exp.99) | copy-start | bytes 49156
  64.6 37.3 %copy-start.27 = (f32[16]{0:T(128)S(1)}, f32[16]{0:T(128)}, u32[]{:S(2)}) copy-start(f32[16]{0:T(128)} %get-tuple-element.99) | copy-start | bytes 196
  64.6 37.3 %copy-start.28 = (f32[16]{0:T(128)S(1)}, f32[16]{0:T(128)}, u32[]{:S(2)}) copy-start(f32[16]{0:T(128)} %get-tuple-element.100) | copy-start | bytes 196
  64.6 37.3 %copy-start.29 = (pred[16]{0:T(512)(128)(4,1)S(1)}, pred[16]{0:T(512)(128)(4,1)}, u32[]{:S(2)}) copy-start(pred[16]{0:T(512)(128)(4,1)} %get-tuple-element.101) | copy-start | bytes 52
  64.6 37.3 %copy-start.30 = (pred[16]{0:T(512)(128)(4,1)S(1)}, pred[16]{0:T(512)(128)(4,1)}, u32[]{:S(2)}) copy-start(pred[16]{0:T(512)(128)(4,1)} %get-tuple-element.102) | copy-start | bytes 52
  97.2 5.7 %copy-start.20 = (f32[16,16]{0,1:T(8,128)S(1)}, f32[16,16]{0,1:T(8,128)}, u32[]{:S(2)}) copy-start(f32[16,16]{0,1:T(8,128)} %copy.141) | copy-start | bytes 3076
  97.2 5.6 %copy-start.21 = (f32[16,16]{0,1:T(8,128)S(1)}, f32[16,16]{0,1:T(8,128)}, u32[]{:S(2)}) copy-start(f32[16,16]{0,1:T(8,128)} %copy.142) | copy-start | bytes 3076
  97.2 5.7 %copy-start.13 = (f32[128,128]{1,0:T(8,128)S(1)}, f32[128,128]{1,0:T(8,128)}, u32[]{:S(2)}) copy-start(f32[128,128]{1,0:T(8,128)} %maximum_convert_fusion) | copy-start | bytes 196612
  103.0 4.5 %copy-start.15 = (pred[128,128]{1,0:T(8,128)(4,1)S(1)}, pred[128,128]{1,0:T(8,128)(4,1)}, u32[]{:S(2)}) copy-start(pred[128,128]{1,0:T(8,128)(4,1)} %fusion.64) | copy-start | bytes 49156
  107.5 1.3 copy-start.5
  107.5 2.2 %copy-start.3 = (f32[8,16,16,16]{1,3,0,2:T(8,128)S(1)}, f32[8,16,16,16]{1,3,0,2:T(8,128)}, u32[]{:S(2)}) copy-start(f32[8,16,16,16]{1,3,0,2:T(8,128)} %copy.166) | copy-start | bytes 393220
  111.8 9.4 %copy-start.1 = (f32[1024,256]{1,0:T(8,128)}, f32[1024,256]{1,0:T(8,128)S(1)}, u32[]{:S(2)}) copy-start(f32[1024,256]{1,0:T(8,128)S(1)} %copy.169.inner_ref) | copy-start | bytes 3145732
  114.8 8.1 %copy-start.33 = (f32[128]{0:T(128)S(1)}, f32[128]{0:T(128)}, u32[]{:S(2)}) copy-start(f32[128]{0:T(128)} %iota_subtract_fusion.2) | copy-start | bytes 1540
  125.0 3.2 %copy-start.6 = (f32[1024,256]{1,0:T(8,128)}, f32[1024,256]{1,0:T(8,128)S(1)}, u32[]{:S(2)}) copy-start(f32[1024,256]{1,0:T(8,128)S(1)} %copy.182.grad_ref) | copy-start | bytes 3145732

commit v6 on v5

--- a/solution.py
+++ b/solution.py
@@ -62,7 +62,7 @@
 
 def finish_kernel(
     fsdp_count, ctx_count, tile_ref, rim_ref, cot_ref, inner_ref, grad_ref, value_ref, key_ref,
-    taps_ref, tiles_out, grads_out, tiles_held, rim_held, adj_buf,
+    taps_ref, query_ref, tiles_out, grads_out, mixed_out, tiles_held, rim_held, adj_buf,
     send_sem, recv_sem, rim_send_sem, rim_recv_sem,
 ):
     f_me = lax.axis_index("fsdp")
@@ -100,6 +100,7 @@
     tokens = cot_ref.shape[0]
     rim_rows = rim_ref.shape[0] // 3
     shifts = taps_ref.shape[1]
+    mixed_out[...] = (query_ref[...] * inner_ref[...]).astype(mixed_out.dtype)
     adj_buf[0, :tokens] = cot_ref[...].astype(jnp.float32) * inner_ref[...]
     adj_buf[1, :tokens] = grad_ref[...] * value_ref[...]
     adj_buf[2, :tokens] = grad_ref[...] * key_ref[...]
@@ -125,10 +126,13 @@
         )
     conv_rows(early, tokens - early)
     tiles_held[f_me] = tile_ref[...]
-    tiles_out[...] = tiles_held[...]
-
-
-def finish_exchange(tile, rim, cot, inner, grad, value, key, taps):
+    total = tiles_held[0]
+    for slot in range(1, fsdp_count):
+        total = total + tiles_held[slot]
+    tiles_out[...] = total
+
+
+def finish_exchange(tile, rim, cot, inner, grad, value, key, taps, query):
     fsdp_count = lax.axis_size("fsdp")
     ctx_count = lax.axis_size("ctx")
     tokens, channels = cot.shape
@@ -137,11 +141,12 @@
     return pl.pallas_call(
         functools.partial(finish_kernel, fsdp_count, ctx_count),
         out_shape=(
-            jax.ShapeDtypeStruct((fsdp_count,) + tile.shape, tile.dtype),
+            jax.ShapeDtypeStruct(tile.shape, tile.dtype),
             jax.ShapeDtypeStruct((3, tokens, channels), jnp.bfloat16),
+            jax.ShapeDtypeStruct((tokens, channels), jnp.bfloat16),
         ),
-        in_specs=[pl.BlockSpec(memory_space=pltpu.VMEM)] * 8,
-        out_specs=(pl.BlockSpec(memory_space=pltpu.VMEM), pl.BlockSpec(memory_space=pltpu.VMEM)),
+        in_specs=[pl.BlockSpec(memory_space=pltpu.VMEM)] * 9,
+        out_specs=(pl.BlockSpec(memory_space=pltpu.VMEM),) * 3,
         scratch_shapes=[
             pltpu.VMEM((fsdp_count,) + tile.shape, tile.dtype),
             pltpu.VMEM(rim.shape, rim.dtype),
@@ -152,7 +157,7 @@
             pltpu.SemaphoreType.DMA(()),
         ],
         compiler_params=pltpu.CompilerParams(collective_id=1, has_side_effects=True),
-    )(tile, rim, cot, inner, grad, value, key, taps)
+    )(tile, rim, cot, inner, grad, value, key, taps, query)
 
 
 def passed_along(value, axis, steps):
@@ -313,7 +318,6 @@
     gain_part = jnp.sqrt(2.0 * decay_rates) * first_total
     rate_part = mode_coefs * (0.5 * first_total + decay_rates * lag_total)
     inner_flat = inner_sum.reshape(tokens, channels)
-    mixer_output = (query_part * inner_flat).astype(jnp.bfloat16)
     grad_flat = product_grad.reshape(tokens, channels)
     rim_adj = jnp.stack(
         [
@@ -327,10 +331,11 @@
     summed = filter_local
     square_tile = jnp.full((8, 128), jnp.sum(summed * summed), jnp.float32)
     rim_send = rim_adj.reshape(3 * rim_rows, channels)
-    square_tiles, feature_grads = finish_exchange(
-        square_tile, rim_send, cotangent, inner_flat, grad_flat, value_part, key_part, short_taps
-    )
-    squares = jnp.sum(square_tiles[:, 0, 0])
+    square_total, feature_grads, mixer_output = finish_exchange(
+        square_tile, rim_send, cotangent, inner_flat, grad_flat, value_part, key_part, short_taps,
+        query_part,
+    )
+    squares = square_total[0, 0]
     factor = jnp.minimum(1.0, lax.rsqrt(squares / entry_count + 1e-06))
     clipped = summed * factor
     return (mixer_output, feature_grads, clipped[0], clipped[1])

time: 166 us -> 167 us (level)
  other arithmetic: 41.1 us -> 37.9 us
  matrix products: 14.5 us -> 16.8 us
  local copies, waits for them, and re-layouts: 39.9 us -> 42 us
    squeeze x1 -> x2, local copies, waits for them, and re-layouts: 0.03 us -> 3.33 us  [per_device(): end_state = jnp.sum(from_last * fresh_fwd[0], axis=0)]
    mul x2 -> x1, local copies, waits for them, and re-layouts: 3.33 us -> 0.03 us  [per_device(): all_prev = jnp.sum(pair_weight * everyone[None, :, 0], axis=1)]
    convert_element_type x1 -> x0, other arithmetic: 2.12 us -> none  [per_device(): mixer_output = (query_part * inner_flat).astype(jnp.bfloat16)]
    unnamed x79 -> x80, local copies, waits for them, and re-layouts: 11.9 us -> 12.8 us
where the time goes in v6:
time: 167 us; the launch traced here: 166 us
  Pallas kernels  63.1 us (38%)
  local copies, waits for them, and re-layouts  42 us (25%)
  other arithmetic  37.9 us (23%)
  matrix products  16.8 us (10%)
  starting transfers between devices  4.36 us (3%)
  between operations  2.02 us (1%)
    pallas_call x1, Pallas kernels, gather_along(): pl.pallas_call(functools.partial(gather_kernel, axis, count), out_shape=j...  32.6 us
    pallas_call x1, Pallas kernels, finish_exchange(): pl.pallas_call(functools.partial(finish_kernel, fsdp_count, ctx_count), o...  30.5 us
    unnamed x80, local copies, waits for them, and re-layouts  12.8 us
    reduce_sum x1, other arithmetic, per_device(): jnp.sum(span_weight * (fresh_fwd[1][None] - block_len * block_steps * fre...  5.76 us
    reduce_sum x1, other arithmetic, per_device(): jnp.sum(jnp.swapaxes(span_weight, 0, 1) * fresh_bwd[None], axis=1)  4.77 us
    reduce_sum x1, other arithmetic, per_device(): jnp.sum(mode_coefs[:, :, None, None] * pair_pow, axis=1)  4.53 us
    ppermute x1, starting transfers between devices, passed_along(): lax.ppermute(value, axis, [(source, source + steps) for source in range(l...  4.36 us
    dot_general x1, matrix products, per_device(): jnp.einsum('gnt,btgm->bngm', block_pow, e_blocks, precision=precise)  3.38 us
  transfers between devices with their start and end apart: 1, of which 0 were waited for; matrix products, arithmetic and copies ran while one was open for 8% of the time, Pallas kernels for 0%

profile of v6, /device:TPU:1, one launch (start us, length us, event | category | flops | bytes accessed | tf_op | source)
XLA Modules:
  0.0 166.2 jit_solution(11729827061413875480)
XLA Ops:
  0.6 0.8 slice.149
  1.5 4.4 %collective-permute-start = (bf16[3,2,256]{2,1,0:T(2,128)(2,1)S(1)}, bf16[3,2,256]{2,1,0:T(2,128)(2,1)S(1)}, u32[]{:S(2)}, u32[]{:S(2)}) collective-permute-start(bf16[3,2,256]{2,1,0:T(2,128)(2,1)S(1)} %slice.149), channel_id=1, source_target_pairs={{0,1},{1,2},{2,3},{3,4},{4,5},{5,6},{6,7},{7,8},{8,9},{9,10},{10,1... | collective-permute-start | bytes 9224 | tf_op jit(solution)/shard_map/ppermute | solution.py:166
  9.7 0.8 fusion.83
  11.5 1.0 select_bitcast_fusion
  12.5 1.0 exponential_select_fusion.1
  13.6 0.8 exponential_multiply_fusion
  15.1 1.4 copy.137
  17.9 1.4 copy.161
  19.3 1.0 multiply_add_fusion
  20.4 2.0 %slice_bitcast_fusion.2 = (f32[1024,256]{1,0:T(8,128)}, f32[1024,256]{1,0:T(8,128)}, bf16[1,1024,256]{2,1,0:T(8,128)(2,1)S(1)}, f32[1024,256]{1,0:T(8,128)}) fusion(f32[3,1024,256]{2,1,0:T(8,128)S(1)} %multiply_add_fusion), kind=kLoop, calls=%fused_computation.29 | loop fusion | flops 524288 | bytes 6815744 | tf_op jit(solution)/shard_map/squeeze | solution.py:193
  23.4 0.8 copy-done.3
  24.2 0.8 convolution_bitcast_fusion.1
  25.0 1.6 slice_bitcast_fusion.4
  26.6 1.7 %copy.149 = f32[8,16,16,16]{3,2,1,0:T(8,128)S(1)} copy(f32[8,16,16,16]{1,3,0,2:T(8,128)} %get-tuple-element.68) | data formatting | bytes 262144 | tf_op jit(solution)/shard_map/squeeze | solution.py:253
  28.3 2.6 %copy.153 = f32[8,16,16,16]{3,2,1,0:T(8,128)} copy(f32[8,16,16,16]{1,3,0,2:T(8,128)} %get-tuple-element.69) | data formatting | bytes 262144 | tf_op jit(solution)/shard_map/squeeze | solution.py:256
  30.9 5.8 %multiply_reduce_fusion.2 = (f32[8,16,16,16]{3,2,1,0:T(8,128)}, f32[8,16,16,16]{3,2,1,0:T(8,128)}) fusion(f32[8,8]{1,0:T(8,128)S(1)} %copy-done.22, f32[8,16,16,16]{3,2,1,0:T(8,128)} %copy.153, f32[8,16,16,16]{3,2,1,0:T(8,128)S(1)} %copy.149, f32[8,8,16,16]{3,2,1,0:T(8,128)} %exponential_select_fusion.1), kind=kLoop, calls=%fused_computation.2 | loop fusion | flops 1507328 | bytes 590080 | tf_op jit(solution)/shard_map/reduce_sum | solution.py:232
  36.7 2.6 %copy.150 = f32[8,16,16,16]{1,3,0,2:T(8,128)} copy(f32[8,16,16,16]{3,2,1,0:T(8,128)} %get-tuple-element.48) | data formatting | bytes 262144 | tf_op jit(solution)/shard_map/reduce_sum | solution.py:231
  39.3 2.6 %copy.155 = f32[8,16,16,16]{1,3,0,2:T(8,128)} copy(f32[8,16,16,16]{3,2,1,0:T(8,128)} %get-tuple-element.47) | data formatting | bytes 262144 | tf_op jit(solution)/shard_map/reduce_sum | solution.py:232
  42.0 1.5 convert_multiply_fusion
  43.5 1.3 copy.141
  44.8 1.4 copy.206
  46.3 2.1 %fusion.5 = f32[16,128,128]{2,1,0:T(8,128)S(1)} fusion(f32[8,128,16,16]{1,0,3,2:T(8,128)S(1)} %bitcast.237, bf16[8,128,16,16]{1,0,3,2:T(8,128)(2,1)} %bitcast.244, pred[128,128]{1,0:T(8,128)(4,1)S(1)} %copy-done.14), kind=kOutput, calls=%fused_computation.23 | convolution fusion | flops 402915328 | bytes 2637824 | tf_op jit(solution)/shard_map/btgm,bsgm->gts/dot_general | solution.py:238
  48.5 1.9 %fusion.6 = f32[2,16,16,128]{3,2,0,1:T(8,128)S(1)} fusion(f32[16,16]{1,0:T(8,128)S(1)} %copy-done.18, f32[1,16,128,128]{3,2,1,0:T(8,128)S(1)} %multiply_bitcast_fusion, f32[1,16,128,128]{3,2,1,0:T(8,128)S(1)} %bitcast.247), kind=kOutput, calls=%fused_computation.24 | convolution fusion | flops 101220352 | bytes 2360320 | tf_op jit(solution)/shard_map/kgts,gns->kgnt/dot_general | solution.py:242
  50.3 0.8 fusion.43
  51.2 2.0 %convolution_bitcast_fusion = f32[2,8,16,16,16]{2,4,1,3,0:T(8,128)S(1)} fusion(f32[8,128,16,16]{1,0,3,2:T(8,128)S(1)} %bitcast.238, f32[1,16,16,128]{3,2,0,1:T(8,128)S(1)} %copy-done.10, f32[1,16,16,128]{3,2,0,1:T(8,128)S(1)} %copy-done.9), kind=kOutput, calls=%fused_computation.11 | convolution fusion | flops 100728832 | bytes 1572864 | tf_op jit(solution)/shard_map/kgnt,btgm->kbngm/dot_general | solution.py:235
  53.2 3.4 %multiply_reduce_fusion.6 = (f32[16,16]{0,1:T(8,128)S(1)}, f32[16,16]{0,1:T(8,128)}, f32[16,16,16]{0,2,1:T(8,128)S(1)}, f32[16,16,16]{0,2,1:T(8,128)S(1)}, f32[8,16,16,16]{1,3,0,2:T(8,128)}) fusion(f32[8,16,16,16]{1,3,0,2:T(8,128)S(1)} %copy-done.1, f32[2,8,16,16,16]{2,4,1,3,0:T(8,128)S(1)} %convolution_bitcast_fusion, f32[8,16,16,16]{1,3,0,2:T(8,128)S(1)} %copy-done.7, ...), kind=kOutput, calls=%fused_computation.43 | convolution fusion | flops 50748928 | bytes 1748000 | tf_op jit(solution)/shard_map/gnt,btgm->bngm/dot_general | solution.py:248
  57.2 1.4 stack.74
  58.6 1.3 bitcast_subtract_fusion
  59.9 1.3 stack.75
  61.2 0.9 multiply_reduce_fusion.10
  64.1 32.6 %shard_map.84 = f32[16,72,256]{2,1,0:T(8,128)} custom-call(f32[72,256]{1,0:T(8,128)} %copy-done.11), custom_call_target="tpu_custom_call" | custom-call | tf_op jit(solution)/shard_map/pallas_call | solution.py:49
  96.8 1.4 slice.164
  98.1 0.9 slice_reduce_fusion
  99.1 2.2 %multiply_reduce_fusion.4 = (f32[16,16,256]{2,1,0:T(8,128)S(1)}, f32[16,16,256]{2,1,0:T(8,128)S(1)}) fusion(f32[16,16]{1,0:T(8,128)S(1)} %copy-done.24, f32[16,16,256]{2,1,0:T(8,128)S(1)} %get-tuple-element.71, f32[16,16,256]{2,1,0:T(8,128)S(1)} %get-tuple-element.70, f32[16,16]{1,0:T(8,128)S(1)} %copy-done.23, f32[16,256]{1,0:T(8,128)S(1)} %copy-done.17, ...), kind=kLoop, calls=%fused_computation.4 | loop fusion | flops 8257536 | bytes 1067264 | tf_op jit(solution)/shard_map/reduce_sum | solution.py:295
  102.5 4.5 %multiply_reduce_fusion = f32[16,128,128]{2,1,0:T(8,128)S(1)} fusion(f32[128,128]{1,0:T(8,128)S(1)} %copy-done.13, f32[16,16]{1,0:T(8,128)S(1)} %get-tuple-element.90, f32[16,16]{1,0:T(8,128)S(1)} %copy.165), kind=kLoop, calls=%fused_computation | loop fusion | flops 12320768 | bytes 1116160 | tf_op jit(solution)/shard_map/reduce_sum | solution.py:216
  107.1 1.8 %fusion.11 = f32[16,8,16,128]{3,2,1,0:T(8,128)} fusion(f32[16,128,128]{2,1,0:T(8,128)S(1)} %multiply_reduce_fusion, bf16[8,128,16,16]{1,0,3,2:T(8,128)(2,1)S(1)} %bitcast.245, pred[128,128]{1,0:T(8,128)(4,1)S(1)} %copy-done.15), kind=kOutput, calls=%fused_computation.34 | convolution fusion | flops 201588736 | bytes 2637824 | tf_op jit(solution)/shard_map/gts,bsgm->btgm/dot_general | solution.py:229
  108.9 1.2 fusion.9
  110.3 2.4 %fusion.4 = f32[8,128,16,16]{1,3,0,2:T(8,128)S(1)} fusion(f32[16,8,16,128]{3,2,1,0:T(8,128)} %fusion.11, f32[8,16,16,16]{1,3,0,2:T(8,128)S(1)} %copy-done.2, f32[16,16,16]{0,2,1:T(8,128)S(1)} %bitcast.254, f32[8,16,16]{1,0,2:T(8,128)S(1)} %get-tuple-element.85, f32[16,16]{1,0:T(8,128)S(1)} %get-tuple-element.88, f32[16,16]{1,0:T(8,128)S(1)} %copy.165, ...), kind=kOutput, calls=%fused_computation.21 | convolution fusion | flops 50757632 | bytes 2255872 | tf_op jit(solution)/shard_map/gnt,bngm->btgm/dot_general | solution.py:314
  114.4 1.7 %copy.174 = f32[8,16,16,16]{3,2,1,0:T(8,128)S(1)} copy(f32[8,16,16,16]{1,3,0,2:T(8,128)} %get-tuple-element.95) | data formatting | bytes 262144 | tf_op jit(solution)/shard_map/gnt,btgm->bngm/transpose | solution.py:248
  116.1 4.8 %multiply_reduce_fusion.1 = f32[8,16,16,16]{3,2,1,0:T(8,128)} fusion(f32[8,16,16,16]{3,2,1,0:T(8,128)S(1)} %copy.174, f32[8,8,16,16]{3,2,1,0:T(8,128)} %select_bitcast_fusion), kind=kLoop, calls=%fused_computation.1 | loop fusion | flops 491520 | bytes 327680 | tf_op jit(solution)/shard_map/reduce_sum | solution.py:249
  120.9 1.7 copy.176
  122.6 1.2 fusion.3
  124.6 0.8 fusion.77
  126.6 1.2 broadcast_in_dim.106.tile_ref
  127.9 30.5 %shard_map.85 = (f32[8,128]{1,0:T(8,128)}, bf16[3,1024,256]{2,1,0:T(8,128)(2,1)}, bf16[1024,256]{1,0:T(8,128)(2,1)}) custom-call(f32[8,128]{1,0:T(8,128)} %broadcast_in_dim.106.tile_ref, f32[6,256]{1,0:T(8,128)} %reshape.453.rim_ref, bf16[1024,256]{1,0:T(8,128)(2,1)} %cot_ref.1, f32[1024,256]{1,0:T(8,128)} %copy-done.5, f32[1024,256]{1,0:T(8,128)} %copy-done.6, ...), custom_call_target="tpu_custom_call" | custom-call | tf_op jit(solution)/shard_map/pallas_call | solution.py:141
  158.4 1.2 slice.177
  161.6 1.9 %copy.240 = bf16[1024,256]{1,0:T(8,128)(2,1)} copy(bf16[1024,256]{1,0:T(8,128)(2,1)} %get-tuple-element.110) | data formatting | bytes 1048576
  163.5 2.7 %copy.241 = bf16[3,1024,256]{2,1,0:T(8,128)(2,1)} copy(bf16[3,1024,256]{2,1,0:T(8,128)(2,1)} %get-tuple-element.111) | data formatting | bytes 3145728
  (132 shorter events, 16.9 us)
Async XLA Ops:
  0.6 18.7 %copy-start.8 = (bf16[3,1024,256]{2,1,0:T(8,128)(2,1)S(1)}, bf16[3,1024,256]{2,1,0:T(8,128)(2,1)}, u32[]{:S(2)}) copy-start(bf16[3,1024,256]{2,1,0:T(8,128)(2,1)} %param.9) | copy-start | bytes 4718596
  1.5 17.8 %collective-permute-start = (bf16[3,2,256]{2,1,0:T(2,128)(2,1)S(1)}, bf16[3,2,256]{2,1,0:T(2,128)(2,1)S(1)}, u32[]{:S(2)}, u32[]{:S(2)}) collective-permute-start(bf16[3,2,256]{2,1,0:T(2,128)(2,1)S(1)} %slice.149), channel_id=1, source_target_pairs={{0,1},{1,2},{2,3},{3,4},{4,5},{5,6},{6,7},{7,8},{8,9},{9,10},{10,1... | collective-permute-start | bytes 9224 | tf_op jit(solution)/shard_map/ppermute | solution.py:166
  5.9 10.5 %copy-start.25 = (f32[8]{0:T(128)}, f32[8]{0:T(128)S(1)}, u32[]{:S(2)}) copy-start(f32[8]{0:T(128)S(1)} %get-tuple-element.100) | copy-start | bytes 100
  5.9 10.5 %copy-start.32 = (f32[8]{0:T(128)}, f32[8]{0:T(128)S(1)}, u32[]{:S(2)}) copy-start(f32[8]{0:T(128)S(1)} %get-tuple-element.101) | copy-start | bytes 100
  17.3 5.0 %copy-start.16 = (f32[16,256]{1,0:T(8,128)}, f32[16,256]{1,0:T(8,128)S(1)}, u32[]{:S(2)}) copy-start(f32[16,256]{1,0:T(8,128)S(1)} %neg.50) | copy-start | bytes 49156
  20.3 2.7 %copy-start = (f32[3,1024,256]{2,1,0:T(8,128)}, f32[3,1024,256]{2,1,0:T(8,128)S(1)}, u32[]{:S(2)}) copy-start(f32[3,1024,256]{2,1,0:T(8,128)S(1)} %multiply_add_fusion) | copy-start | bytes 9437188
  23.4 0.8 copy-start.3
  26.6 4.3 %copy-start.22 = (f32[8,8]{1,0:T(8,128)S(1)}, f32[8,8]{1,0:T(8,128)}, u32[]{:S(2)}) copy-start(f32[8,8]{1,0:T(8,128)} %copy.154) | copy-start | bytes 772
  42.0 4.3 %copy-start.14 = (pred[128,128]{1,0:T(8,128)(4,1)S(1)}, pred[128,128]{1,0:T(8,128)(4,1)}, u32[]{:S(2)}) copy-start(pred[128,128]{1,0:T(8,128)(4,1)} %fusion.60) | copy-start | bytes 49156
  46.2 2.1 %copy-start.12 = (f32[128,128]{1,0:T(8,128)S(1)}, f32[128,128]{1,0:T(8,128)}, u32[]{:S(2)}) copy-start(f32[128,128]{1,0:T(8,128)} %maximum_convert_fusion) | copy-start | bytes 196612
  46.3 2.2 %copy-start.18 = (f32[16,16]{1,0:T(8,128)S(1)}, f32[16,16]{1,0:T(8,128)}, u32[]{:S(2)}) copy-start(f32[16,16]{1,0:T(8,128)} %param.11) | copy-start | bytes 3076
  48.4 2.8 %copy-start.9 = (f32[1,16,16,128]{3,2,0,1:T(8,128)S(1)}, f32[1,16,16,128]{3,2,0,1:T(8,128)}, u32[]{:S(2)}) copy-start(f32[1,16,16,128]{3,2,0,1:T(8,128)} %get-tuple-element.77) | copy-start | bytes 393220
  48.4 2.8 %copy-start.10 = (f32[1,16,16,128]{3,2,0,1:T(8,128)S(1)}, f32[1,16,16,128]{3,2,0,1:T(8,128)}, u32[]{:S(2)}) copy-start(f32[1,16,16,128]{3,2,0,1:T(8,128)} %get-tuple-element.78) | copy-start | bytes 393220
  48.5 4.8 %copy-start.1 = (f32[8,16,16,16]{1,3,0,2:T(8,128)S(1)}, f32[8,16,16,16]{1,3,0,2:T(8,128)}, u32[]{:S(2)}) copy-start(f32[8,16,16,16]{1,3,0,2:T(8,128)} %copy.150) | copy-start | bytes 393220
  48.5 4.8 %copy-start.7 = (f32[8,16,16,16]{1,3,0,2:T(8,128)S(1)}, f32[8,16,16,16]{1,3,0,2:T(8,128)}, u32[]{:S(2)}) copy-start(f32[8,16,16,16]{1,3,0,2:T(8,128)} %copy.155) | copy-start | bytes 393220
  48.5 4.8 %copy-start.26 = (f32[8]{0:T(128)S(1)}, f32[8]{0:T(128)}, u32[]{:S(2)}) copy-start(f32[8]{0:T(128)} %copy-done.25) | copy-start | bytes 100
  62.2 36.9 %copy-start.17 = (f32[16,256]{1,0:T(8,128)S(1)}, f32[16,256]{1,0:T(8,128)}, u32[]{:S(2)}) copy-start(f32[16,256]{1,0:T(8,128)} %copy-done.16) | copy-start | bytes 49156
  62.2 36.9 %copy-start.23 = (f32[16,16]{1,0:T(8,128)S(1)}, f32[16,16]{1,0:T(8,128)}, u32[]{:S(2)}) copy-start(f32[16,16]{1,0:T(8,128)} %get-tuple-element.91) | copy-start | bytes 3076
  62.2 36.9 %copy-start.24 = (f32[16,16]{1,0:T(8,128)S(1)}, f32[16,16]{1,0:T(8,128)}, u32[]{:S(2)}) copy-start(f32[16,16]{1,0:T(8,128)} %get-tuple-element.92) | copy-start | bytes 3076
  62.2 36.9 %copy-start.31 = (pred[16,16]{1,0:T(8,128)(4,1)S(1)}, pred[16,16]{1,0:T(8,128)(4,1)}, u32[]{:S(2)}) copy-start(pred[16,16]{1,0:T(8,128)(4,1)} %subtract_compare_fusion) | copy-start | bytes 772
  63.5 0.6 copy-start.11
  64.1 37.3 %copy-start.19 = (f32[16,256]{1,0:T(8,128)S(1)}, f32[16,256]{1,0:T(8,128)}, u32[]{:S(2)}) copy-start(f32[16,256]{1,0:T(8,128)} %exp.97) | copy-start | bytes 49156
  64.1 37.3 %copy-start.27 = (f32[16]{0:T(128)S(1)}, f32[16]{0:T(128)}, u32[]{:S(2)}) copy-start(f32[16]{0:T(128)} %get-tuple-element.102) | copy-start | bytes 196
  64.1 37.3 %copy-start.28 = (f32[16]{0:T(128)S(1)}, f32[16]{0:T(128)}, u32[]{:S(2)}) copy-start(f32[16]{0:T(128)} %get-tuple-element.103) | copy-start | bytes 196
  64.1 37.3 %copy-start.29 = (pred[16]{0:T(512)(128)(4,1)S(1)}, pred[16]{0:T(512)(128)(4,1)}, u32[]{:S(2)}) copy-start(pred[16]{0:T(512)(128)(4,1)} %get-tuple-element.104) | copy-start | bytes 52
  64.1 37.3 %copy-start.30 = (pred[16]{0:T(512)(128)(4,1)S(1)}, pred[16]{0:T(512)(128)(4,1)}, u32[]{:S(2)}) copy-start(pred[16]{0:T(512)(128)(4,1)} %get-tuple-element.105) | copy-start | bytes 52
  96.7 5.7 %copy-start.20 = (f32[16,16]{0,1:T(8,128)S(1)}, f32[16,16]{0,1:T(8,128)}, u32[]{:S(2)}) copy-start(f32[16,16]{0,1:T(8,128)} %copy.137) | copy-start | bytes 3076
  96.8 5.7 %copy-start.21 = (f32[16,16]{0,1:T(8,128)S(1)}, f32[16,16]{0,1:T(8,128)}, u32[]{:S(2)}) copy-start(f32[16,16]{0,1:T(8,128)} %copy.161) | copy-start | bytes 3076
  96.8 5.7 %copy-start.13 = (f32[128,128]{1,0:T(8,128)S(1)}, f32[128,128]{1,0:T(8,128)}, u32[]{:S(2)}) copy-start(f32[128,128]{1,0:T(8,128)} %maximum_convert_fusion) | copy-start | bytes 196612
  102.5 4.5 %copy-start.4 = (bf16[32,8,8,128]{3,2,1,0:T(8,128)(2,1)S(1)}, bf16[32,8,8,128]{3,2,1,0:T(8,128)(2,1)}, u32[]{:S(2)}) copy-start(bf16[32,8,8,128]{3,2,1,0:T(8,128)(2,1)} %copy-done.3) | copy-start | bytes 1572868
  102.5 4.6 %copy-start.15 = (pred[128,128]{1,0:T(8,128)(4,1)S(1)}, pred[128,128]{1,0:T(8,128)(4,1)}, u32[]{:S(2)}) copy-start(pred[128,128]{1,0:T(8,128)(4,1)} %fusion.60) | copy-start | bytes 49156
  107.1 3.2 %copy-start.2 = (f32[8,16,16,16]{1,3,0,2:T(8,128)S(1)}, f32[8,16,16,16]{1,3,0,2:T(8,128)}, u32[]{:S(2)}) copy-start(f32[8,16,16,16]{1,3,0,2:T(8,128)} %copy.150) | copy-start | bytes 393220
  113.6 8.9 %copy-start.5 = (f32[1024,256]{1,0:T(8,128)}, f32[1024,256]{1,0:T(8,128)S(1)}, u32[]{:S(2)}) copy-start(f32[1024,256]{1,0:T(8,128)S(1)} %copy.171.inner_ref) | copy-start | bytes 3145732
  114.4 8.1 %copy-start.33 = (f32[128]{0:T(128)S(1)}, f32[128]{0:T(128)}, u32[]{:S(2)}) copy-start(f32[128]{0:T(128)} %iota_subtract_fusion.2) | copy-start | bytes 1540
  124.6 3.3 %copy-start.6 = (f32[1024,256]{1,0:T(8,128)}, f32[1024,256]{1,0:T(8,128)S(1)}, u32[]{:S(2)}) copy-start(f32[1024,256]{1,0:T(8,128)S(1)} %copy.178.grad_ref) | copy-start | bytes 3145732

commit v7 on v5

--- a/solution.py
+++ b/solution.py
@@ -12,7 +12,7 @@
 threepass = lax.Precision.HIGH
 
 
-def gather_kernel(axis, count, x_ref, o_ref, held, send_sem, recv_sem):
+def gather_kernel(axis, count, x_ref, rate_ref, coef_ref, o_ref, toe_ref, held, send_sem, recv_sem):
     me = lax.axis_index(axis)
 
     def device(peer):
@@ -38,26 +38,47 @@
         )
         copy.start()
         copies.append(copy)
+    span = toe_ref.shape[1]
+    lag = lax.broadcasted_iota(jnp.int32, (span, span), 0) - lax.broadcasted_iota(
+        jnp.int32, (span, span), 1
+    )
+    lag_value = jnp.maximum(lag, 0).astype(jnp.float32)
+
+    def one_group(group, carry):
+        total = jnp.zeros((span, span), jnp.float32)
+        for mode in range(rate_ref.shape[1]):
+            total = total + coef_ref[group, mode] * jnp.exp(-rate_ref[group, mode] * lag_value)
+        toe_ref[group] = jnp.where(lag >= 0, total, 0.0)
+        return carry
+
+    lax.fori_loop(0, toe_ref.shape[0], one_group, 0)
     for copy in copies:
         copy.wait()
     held[me] = x_ref[...]
     o_ref[...] = held[...]
 
 
-def gather_along(value, axis, collective_id):
+def gather_along(value, axis, collective_id, rates, coefs, span):
     count = lax.axis_size(axis)
     return pl.pallas_call(
         functools.partial(gather_kernel, axis, count),
-        out_shape=jax.ShapeDtypeStruct((count,) + value.shape, value.dtype),
-        in_specs=[pl.BlockSpec(memory_space=pltpu.VMEM)],
-        out_specs=pl.BlockSpec(memory_space=pltpu.VMEM),
+        out_shape=(
+            jax.ShapeDtypeStruct((count,) + value.shape, value.dtype),
+            jax.ShapeDtypeStruct((rates.shape[0], span, span), jnp.float32),
+        ),
+        in_specs=[
+            pl.BlockSpec(memory_space=pltpu.VMEM),
+            pl.BlockSpec(memory_space=pltpu.SMEM),
+            pl.BlockSpec(memory_space=pltpu.SMEM),
+        ],
+        out_specs=(pl.BlockSpec(memory_space=pltpu.VMEM), pl.BlockSpec(memory_space=pltpu.VMEM)),
         scratch_shapes=[
             pltpu.VMEM((count,) + value.shape, value.dtype),
             pltpu.SemaphoreType.DMA((count - 1,)),
             pltpu.SemaphoreType.DMA((count - 1,)),
         ],
         compiler_params=pltpu.CompilerParams(collective_id=collective_id, has_side_effects=True),
-    )(value)
+    )(value, rates, coefs)
 
 
 def finish_kernel(
@@ -206,10 +227,6 @@
         - jnp.arange(block_len, dtype=jnp.int32)[None, :]
     )
     lag_value = jnp.maximum(lag_index, 0).astype(jnp.float32)
-    pair_pow = jnp.exp(-decay_rates[:, :, None, None] * lag_value[None, None])
-    toeplitz = jnp.where(
-        lag_index[None] >= 0, jnp.sum(mode_coefs[:, :, None, None] * pair_pow, axis=1), 0.0
-    )
     z_blocks = grouped_z.reshape(block_count, block_len, group_count, members)
     e_blocks = grouped_e.reshape(block_count, block_len, group_count, members)
 
@@ -221,7 +238,6 @@
         jnp.exp(-decay_rates.T[None, None, :, :, None] * (block_len * jnp.maximum(block_steps, 0.0))),
         0.0,
     )
-    inside_fwd = jnp.einsum("gts,bsgm->btgm", toeplitz, z_wide, precision=threepass)
     fresh_fwd = jnp.einsum("kgns,bsgm->kbngm", block_ends, z_wide, precision=threepass)
     start_states = jnp.sum(span_weight * fresh_fwd[0][None], axis=1)
     start_lagged = jnp.sum(
@@ -239,7 +255,6 @@
     lag_in = jnp.sum(block_pow * gram_rise[1], axis=2)
     first_local = first_acc.T + first_in
     lag_local = lag_acc.T - lag_in
-    inside_bwd = jnp.einsum("gts,btgm->bsgm", toeplitz, e_blocks, precision=precise)
     fresh_bwd = jnp.einsum("gnt,btgm->bngm", block_pow, e_blocks, precision=precise)
     later_states = jnp.sum(jnp.swapaxes(span_weight, 0, 1) * fresh_bwd[None], axis=1)
     rates_ng = decay_rates.T[None, :, :, None]
@@ -266,7 +281,9 @@
         partial_rows
     )
     rate_cols = jnp.repeat(decay_rates.T, members, axis=1)
-    gathered = gather_along(local_states, "ctx", 0)
+    gathered, toeplitz = gather_along(local_states, "ctx", 0, decay_rates, mode_coefs, block_len)
+    inside_fwd = jnp.einsum("gts,bsgm->btgm", toeplitz, z_wide, precision=threepass)
+    inside_bwd = jnp.einsum("gts,btgm->bsgm", toeplitz, e_blocks, precision=precise)
     everyone = gathered[:, : state_rows.shape[0]].reshape(ctx_count, 4, order_count, channels)
     device_ids = jnp.arange(ctx_count, dtype=jnp.int32)
     ahead_steps = (ctx_index - 1 - device_ids).astype(jnp.float32)[:, None, None]

time: 166 us -> 159 us (0.958)
  local copies, waits for them, and re-layouts: 39.9 us -> 34.7 us
  other arithmetic: 41.1 us -> 37 us
  matrix products: 14.5 us -> 17 us
    reduce_sum x1 -> x0, other arithmetic: 4.53 us -> none  [per_device(): jnp.sum(mode_coefs[:, :, None, None] * pair_pow, axis=1)]
    unnamed x79 -> x89, local copies, waits for them, and re-layouts: 11.9 us -> 7.84 us
    mul x3 -> x0, local copies, waits for them, and re-layouts: 3.4 us -> none  [the longest x2 3.33 us: per_device(): start_states = jnp.sum(span_weight * fresh_fwd[0][None], axis=1)]
    squeeze x0 -> x2, local copies, waits for them, and re-layouts: none -> 3.31 us  [per_device(): end_state = jnp.sum(from_last * fresh_fwd[0], axis=0)]
  transfers between devices with their start and end apart: 1 -> 1, of which waited for: 0 -> 0; matrix products, arithmetic and copies ran while one was open for 8% -> 7% of each run, Pallas kernels for 0% -> 0%
where the time goes in v7:
time: 159 us; the launch traced here: 158 us
  Pallas kernels  63 us (40%)
  other arithmetic  37 us (23%)
  local copies, waits for them, and re-layouts  34.7 us (22%)
  matrix products  17 us (11%)
  starting transfers between devices  4.36 us (3%)
  between operations  2.11 us (1%)
    pallas_call x1, Pallas kernels, gather_along(): pl.pallas_call(functools.partial(gather_kernel, axis, count), out_shape=(...  33 us
    pallas_call x1, Pallas kernels, finish_exchange(): pl.pallas_call(functools.partial(finish_kernel, fsdp_count, ctx_count), o...  30 us
    unnamed x89, local copies, waits for them, and re-layouts  7.84 us
    reduce_sum x1, other arithmetic, per_device(): jnp.sum(span_weight * (fresh_fwd[1][None] - block_len * block_steps * fre...  5.78 us
    reduce_sum x1, other arithmetic, per_device(): jnp.sum(jnp.swapaxes(span_weight, 0, 1) * fresh_bwd[None], axis=1)  5.03 us
    ppermute x1, starting transfers between devices, passed_along(): lax.ppermute(value, axis, [(source, source + steps) for source in range(l...  4.36 us
    squeeze x2, local copies, waits for them, and re-layouts, per_device(): end_state = jnp.sum(from_last * fresh_fwd[0], axis=0)  3.31 us
  transfers between devices with their start and end apart: 1, of which 0 were waited for; matrix products, arithmetic and copies ran while one was open for 7% of the time, Pallas kernels for 0%

profile of v7, /device:TPU:1, one launch (start us, length us, event | category | flops | bytes accessed | tf_op | source)
XLA Modules:
  0.0 158.2 jit_solution(13757774086928011915)
XLA Ops:
  0.6 0.8 slice.149
  1.5 4.4 %collective-permute-start = (bf16[3,2,256]{2,1,0:T(2,128)(2,1)S(1)}, bf16[3,2,256]{2,1,0:T(2,128)(2,1)S(1)}, u32[]{:S(2)}, u32[]{:S(2)}) collective-permute-start(bf16[3,2,256]{2,1,0:T(2,128)(2,1)S(1)} %slice.149), channel_id=1, source_target_pairs={{0,1},{1,2},{2,3},{3,4},{4,5},{5,6},{6,7},{7,8},{8,9},{9,10},{10,1... | collective-permute-start | bytes 9224 | tf_op jit(solution)/shard_map/ppermute | solution.py:182
  9.7 0.8 fusion.75
  10.6 1.3 fusion.65
  12.1 1.0 select_bitcast_fusion
  13.2 1.0 exponential_select_fusion.1
  14.2 0.8 exponential_multiply_fusion
  16.6 1.0 multiply_add_fusion
  17.6 1.7 %copy-done = f32[3,1024,256]{2,1,0:T(8,128)} copy-done((f32[3,1024,256]{2,1,0:T(8,128)}, f32[3,1024,256]{2,1,0:T(8,128)S(1)}, u32[]{:S(2)}) %copy-start) | copy-done | bytes 3145752
  19.2 1.5 slice_bitcast_fusion.6
  21.1 0.8 copy-done.4
  21.9 0.8 convolution_bitcast_fusion.1
  22.7 1.6 %slice_bitcast_fusion.3 = (f32[8,16,16,16]{1,3,0,2:T(8,128)}, f32[8,16,16,16]{1,3,0,2:T(8,128)}) fusion(f32[2,8,16,16,16]{2,4,0,1,3:T(8,128)S(1)} %convolution_bitcast_fusion.1), kind=kLoop, calls=%fused_computation.29 | loop fusion | bytes 524288 | tf_op jit(solution)/shard_map/squeeze | solution.py:263
  24.3 1.7 %copy.106 = f32[8,16,16,16]{3,2,1,0:T(8,128)S(1)} copy(f32[8,16,16,16]{1,3,0,2:T(8,128)} %get-tuple-element.61) | data formatting | bytes 262144 | tf_op jit(solution)/shard_map/squeeze | solution.py:263
  26.0 2.6 %copy.110 = f32[8,16,16,16]{3,2,1,0:T(8,128)} copy(f32[8,16,16,16]{1,3,0,2:T(8,128)} %get-tuple-element.62) | data formatting | bytes 262144 | tf_op jit(solution)/shard_map/squeeze | solution.py:266
  28.7 5.8 %multiply_reduce_fusion.1 = (f32[8,16,16,16]{3,2,1,0:T(8,128)}, f32[8,16,16,16]{3,2,1,0:T(8,128)}) fusion(f32[8,8]{1,0:T(8,128)S(1)} %copy.111, f32[8,16,16,16]{3,2,1,0:T(8,128)} %copy.110, f32[8,16,16,16]{3,2,1,0:T(8,128)S(1)} %copy.106, f32[8,8,16,16]{3,2,1,0:T(8,128)} %exponential_select_fusion.1), kind=kLoop, calls=%fused_computation.1 | loop fusion | flops 1507328 | bytes 590080 | tf_op jit(solution)/shard_map/reduce_sum | solution.py:243
  34.4 2.7 %copy.107 = f32[8,16,16,16]{1,3,0,2:T(8,128)} copy(f32[8,16,16,16]{3,2,1,0:T(8,128)} %get-tuple-element.42) | data formatting | bytes 262144 | tf_op jit(solution)/shard_map/reduce_sum | solution.py:242
  37.1 2.6 %copy.112 = f32[8,16,16,16]{1,3,0,2:T(8,128)} copy(f32[8,16,16,16]{3,2,1,0:T(8,128)} %get-tuple-element.41) | data formatting | bytes 262144 | tf_op jit(solution)/shard_map/reduce_sum | solution.py:243
  39.7 1.5 convert_multiply_fusion
  41.2 1.3 copy.98
  42.5 1.4 copy.158
  44.0 2.1 %fusion.5 = f32[16,128,128]{2,1,0:T(8,128)S(1)} fusion(f32[8,128,16,16]{1,0,3,2:T(8,128)S(1)} %bitcast.238, bf16[8,128,16,16]{1,0,3,2:T(8,128)(2,1)} %bitcast.245, pred[128,128]{1,0:T(8,128)(4,1)S(1)} %copy-done.27), kind=kOutput, calls=%fused_computation.22 | convolution fusion | flops 402915328 | bytes 2637824 | tf_op jit(solution)/shard_map/btgm,bsgm->gts/dot_general | solution.py:249
  46.2 1.9 %fusion.6 = f32[2,16,16,128]{3,2,0,1:T(8,128)S(1)} fusion(f32[16,16]{1,0:T(8,128)S(1)} %copy-done.19, f32[1,16,128,128]{3,2,1,0:T(8,128)S(1)} %multiply_bitcast_fusion, f32[1,16,128,128]{3,2,1,0:T(8,128)S(1)} %bitcast.247), kind=kOutput, calls=%fused_computation.23 | convolution fusion | flops 101220352 | bytes 2360320 | tf_op jit(solution)/shard_map/kgts,gns->kgnt/dot_general | solution.py:253
  48.1 0.8 fusion.37
  48.9 2.0 %convolution_bitcast_fusion = f32[2,8,16,16,16]{2,4,1,3,0:T(8,128)S(1)} fusion(f32[8,128,16,16]{1,0,3,2:T(8,128)S(1)} %bitcast.239, f32[1,16,16,128]{3,2,0,1:T(8,128)S(1)} %copy-done.13, f32[1,16,16,128]{3,2,0,1:T(8,128)S(1)} %copy-done.12), kind=kOutput, calls=%fused_computation.10 | convolution fusion | flops 100728832 | bytes 1572864 | tf_op jit(solution)/shard_map/kgnt,btgm->kbngm/dot_general | solution.py:246
  51.0 2.8 %multiply_reduce_fusion.5 = (f32[16,16]{0,1:T(8,128)S(1)}, f32[16,16]{0,1:T(8,128)S(1)}, f32[16,16,16]{0,2,1:T(8,128)S(1)}, f32[16,16,16]{0,2,1:T(8,128)S(1)}, f32[8,16,16,16]{1,3,0,2:T(8,128)}) fusion(f32[8,16,16,16]{1,3,0,2:T(8,128)S(1)} %copy-done.2, f32[2,8,16,16,16]{2,4,1,3,0:T(8,128)S(1)} %convolution_bitcast_fusion, ...), kind=kOutput, calls=%fused_computation.43 | convolution fusion | flops 50748928 | bytes 1748000 | tf_op jit(solution)/shard_map/gnt,btgm->bngm/dot_general | solution.py:258
  54.3 1.4 stack.74
  55.7 1.3 bitcast_subtract_fusion
  57.0 0.8 stack.75
  57.8 1.0 multiply_reduce_fusion.9
  60.0 33.0 %shard_map.84 = (f32[16,72,256]{2,1,0:T(8,128)}, f32[16,128,128]{2,1,0:T(8,128)}) custom-call(f32[72,256]{1,0:T(8,128)} %copy-done.14, f32[16,16]{1,0:T(8,128)} %rate_ref.1, f32[16,16]{1,0:T(8,128)} %get-tuple-element.76.coef_ref), custom_call_target="tpu_custom_call" | custom-call | tf_op jit(solution)/shard_map/pallas_call | solution.py:63
  93.0 2.6 %fusion.9 = f32[16,8,16,128]{3,2,1,0:T(8,128)S(1)} fusion(f32[16,128,128]{2,1,0:T(8,128)} %get-tuple-element.32, f32[8,128,16,16]{1,0,3,2:T(8,128)S(1)} %bitcast.241), kind=kOutput, calls=%fused_computation.31 | convolution fusion | flops 402653184 | bytes 3145728 | tf_op jit(solution)/shard_map/gts,btgm->bsgm/dot_general | solution.py:286
  95.7 1.8 %fusion.11 = f32[16,8,16,128]{3,2,1,0:T(8,128)} fusion(f32[16,128,128]{2,1,0:T(8,128)S(1)} %copy-done.8, bf16[8,128,16,16]{1,0,3,2:T(8,128)(2,1)S(1)} %bitcast.246), kind=kOutput, calls=%fused_computation.33 | convolution fusion | flops 201326592 | bytes 2621440 | tf_op jit(solution)/shard_map/gts,bsgm->btgm/dot_general | solution.py:285
  98.4 2.2 %multiply_reduce_fusion.3 = (f32[16,16,256]{2,1,0:T(8,128)S(1)}, f32[16,16,256]{2,1,0:T(8,128)S(1)}) fusion(f32[16,16]{1,0:T(8,128)S(1)} %copy-done.30, f32[16,16,256]{2,1,0:T(8,128)S(1)} %get-tuple-element.64, f32[16,16,256]{2,1,0:T(8,128)S(1)} %get-tuple-element.63, f32[16,16]{1,0:T(8,128)S(1)} %copy-done.29, f32[16,256]{1,0:T(8,128)S(1)} %copy-done.17, ...), kind=kLoop, calls=%fused_computation.3 | loop fusion | flops 8257536 | bytes 1067264 | tf_op jit(solution)/shard_map/reduce_sum | solution.py:307
  100.7 0.8 multiply_reduce_fusion.10
  101.5 0.8 copy.147
  102.4 1.9 %fusion.4 = f32[8,128,16,16]{1,3,0,2:T(8,128)S(1)} fusion(f32[16,8,16,128]{3,2,1,0:T(8,128)S(1)} %copy-done.7, f32[8,16,16,16]{1,3,0,2:T(8,128)S(1)} %copy-done.3, f32[16,16,16]{0,2,1:T(8,128)S(1)} %bitcast.255, f32[8,16,16]{1,0,2:T(8,128)S(1)} %get-tuple-element.81, f32[16,16]{1,0:T(8,128)} %copy-done.21, f32[16,16]{1,0:T(8,128)S(1)} %copy-done.18, ...), kind=kOutput, calls=%fused_computation.20 | convolution fusion | flops 50757632 | bytes 2255872 | tf_op jit(solution)/shard_map/gnt,bngm->btgm/dot_general | solution.py:326
  105.2 0.7 fusion.72
  105.9 2.1 %multiply_convert_fusion = bf16[1024,256]{1,0:T(8,128)(2,1)} fusion(f32[1024,256]{1,0:T(8,128)S(1)} %copy.120.inner_ref, f32[3,1024,256]{2,1,0:T(8,128)} %copy-done), kind=kLoop, calls=%fused_computation.38 | loop fusion | flops 524288 | bytes 2621440 | tf_op jit(solution)/shard_map/convert_element_type | solution.py:333
  108.1 1.7 %copy.128 = f32[8,16,16,16]{3,2,1,0:T(8,128)S(1)} copy(f32[8,16,16,16]{1,3,0,2:T(8,128)} %get-tuple-element.88) | data formatting | bytes 262144 | tf_op jit(solution)/shard_map/gnt,btgm->bngm/transpose | solution.py:258
  109.8 5.0 %multiply_reduce_fusion = f32[8,16,16,16]{3,2,1,0:T(8,128)} fusion(f32[8,16,16,16]{3,2,1,0:T(8,128)S(1)} %copy.128, f32[8,8,16,16]{3,2,1,0:T(8,128)} %select_bitcast_fusion), kind=kLoop, calls=%fused_computation | loop fusion | flops 491520 | bytes 327680 | tf_op jit(solution)/shard_map/reduce_sum | solution.py:259
  114.8 1.7 %copy.130 = f32[8,16,16,16]{1,3,0,2:T(8,128)S(1)} copy(f32[8,16,16,16]{3,2,1,0:T(8,128)} %multiply_reduce_fusion) | data formatting | bytes 262144 | tf_op jit(solution)/shard_map/reduce_sum | solution.py:259
  116.5 1.2 fusion.3
  118.6 0.8 fusion.71
  121.5 1.2 broadcast_in_dim.98.tile_ref
  122.7 30.0 %shard_map.85 = (f32[32,8,128]{2,1,0:T(8,128)}, bf16[3,1024,256]{2,1,0:T(8,128)(2,1)}) custom-call(f32[8,128]{1,0:T(8,128)} %broadcast_in_dim.98.tile_ref, f32[6,256]{1,0:T(8,128)} %reshape.429.rim_ref, bf16[1024,256]{1,0:T(8,128)(2,1)} %cot_ref.1, f32[1024,256]{1,0:T(8,128)} %copy-done.1, f32[1024,256]{1,0:T(8,128)} %copy-done.6, ...), custom_call_target="tpu_custom_call" | custom-call | tf_op jit(solution)/shard_map/pallas_call | solution.py:158
  152.7 1.5 slice_reduce_fusion.1
  155.6 2.7 %copy.191 = bf16[3,1024,256]{2,1,0:T(8,128)(2,1)} copy(bf16[3,1024,256]{2,1,0:T(8,128)(2,1)} %get-tuple-element.104) | data formatting | bytes 3145728
  (140 shorter events, 13.1 us)
Async XLA Ops:
  0.6 15.9 %copy-start.10 = (bf16[3,1024,256]{2,1,0:T(8,128)(2,1)S(1)}, bf16[3,1024,256]{2,1,0:T(8,128)(2,1)}, u32[]{:S(2)}) copy-start(bf16[3,1024,256]{2,1,0:T(8,128)(2,1)} %param.9) | copy-start | bytes 4718596
  1.5 15.1 %collective-permute-start = (bf16[3,2,256]{2,1,0:T(2,128)(2,1)S(1)}, bf16[3,2,256]{2,1,0:T(2,128)(2,1)S(1)}, u32[]{:S(2)}, u32[]{:S(2)}) collective-permute-start(bf16[3,2,256]{2,1,0:T(2,128)(2,1)S(1)} %slice.149), channel_id=1, source_target_pairs={{0,1},{1,2},{2,3},{3,4},{4,5},{5,6},{6,7},{7,8},{8,9},{9,10},{10,1... | collective-permute-start | bytes 9224 | tf_op jit(solution)/shard_map/ppermute | solution.py:182
  5.9 9.7 %copy-start.32 = (f32[8]{0:T(128)}, f32[8]{0:T(128)S(1)}, u32[]{:S(2)}) copy-start(f32[8]{0:T(128)S(1)} %get-tuple-element.93) | copy-start | bytes 100
  5.9 9.7 %copy-start.39 = (f32[8]{0:T(128)}, f32[8]{0:T(128)S(1)}, u32[]{:S(2)}) copy-start(f32[8]{0:T(128)S(1)} %get-tuple-element.94) | copy-start | bytes 100
  11.9 3.8 %copy-start.21 = (f32[16,16]{1,0:T(8,128)}, f32[16,16]{1,0:T(8,128)S(1)}, u32[]{:S(2)}) copy-start(f32[16,16]{1,0:T(8,128)S(1)} %get-tuple-element.78) | copy-start | bytes 3076
  15.9 4.9 %copy-start.16 = (f32[16,256]{1,0:T(8,128)}, f32[16,256]{1,0:T(8,128)S(1)}, u32[]{:S(2)}) copy-start(f32[16,256]{1,0:T(8,128)S(1)} %neg.48) | copy-start | bytes 49156
  17.6 1.7 %copy-start = (f32[3,1024,256]{2,1,0:T(8,128)}, f32[3,1024,256]{2,1,0:T(8,128)S(1)}, u32[]{:S(2)}) copy-start(f32[3,1024,256]{2,1,0:T(8,128)S(1)} %multiply_add_fusion) | copy-start | bytes 9437188
  21.1 0.8 copy-start.4
  39.7 4.3 %copy-start.27 = (pred[128,128]{1,0:T(8,128)(4,1)S(1)}, pred[128,128]{1,0:T(8,128)(4,1)}, u32[]{:S(2)}) copy-start(pred[128,128]{1,0:T(8,128)(4,1)} %fusion.54) | copy-start | bytes 49156
  44.0 2.1 %copy-start.15 = (f32[128,128]{1,0:T(8,128)S(1)}, f32[128,128]{1,0:T(8,128)}, u32[]{:S(2)}) copy-start(f32[128,128]{1,0:T(8,128)} %maximum_convert_fusion) | copy-start | bytes 196612
  44.0 2.2 %copy-start.19 = (f32[16,16]{1,0:T(8,128)S(1)}, f32[16,16]{1,0:T(8,128)}, u32[]{:S(2)}) copy-start(f32[16,16]{1,0:T(8,128)} %rate_ref.1) | copy-start | bytes 3076
  46.1 2.8 %copy-start.12 = (f32[1,16,16,128]{3,2,0,1:T(8,128)S(1)}, f32[1,16,16,128]{3,2,0,1:T(8,128)}, u32[]{:S(2)}) copy-start(f32[1,16,16,128]{3,2,0,1:T(8,128)} %get-tuple-element.69) | copy-start | bytes 393220
  46.1 2.8 %copy-start.13 = (f32[1,16,16,128]{3,2,0,1:T(8,128)S(1)}, f32[1,16,16,128]{3,2,0,1:T(8,128)}, u32[]{:S(2)}) copy-start(f32[1,16,16,128]{3,2,0,1:T(8,128)} %get-tuple-element.70) | copy-start | bytes 393220
  46.2 4.8 %copy-start.2 = (f32[8,16,16,16]{1,3,0,2:T(8,128)S(1)}, f32[8,16,16,16]{1,3,0,2:T(8,128)}, u32[]{:S(2)}) copy-start(f32[8,16,16,16]{1,3,0,2:T(8,128)} %copy.107) | copy-start | bytes 393220
  46.2 4.8 %copy-start.9 = (f32[8,16,16,16]{1,3,0,2:T(8,128)S(1)}, f32[8,16,16,16]{1,3,0,2:T(8,128)}, u32[]{:S(2)}) copy-start(f32[8,16,16,16]{1,3,0,2:T(8,128)} %copy.112) | copy-start | bytes 393220
  46.2 4.8 %copy-start.33 = (f32[8]{0:T(128)S(1)}, f32[8]{0:T(128)}, u32[]{:S(2)}) copy-start(f32[8]{0:T(128)} %copy-done.32) | copy-start | bytes 100
  57.0 2.3 %copy-start.31 = (f32[1,256]{1,0:T(1,128)S(1)}, f32[1,256]{1,0:T(1,128)}, u32[]{:S(2)}) copy-start(f32[1,256]{1,0:T(1,128)} %stack.74) | copy-start | bytes 3076
  58.8 36.9 %copy-start.5 = (bf16[32,8,8,128]{3,2,1,0:T(8,128)(2,1)S(1)}, bf16[32,8,8,128]{3,2,1,0:T(8,128)(2,1)}, u32[]{:S(2)}) copy-start(bf16[32,8,8,128]{3,2,1,0:T(8,128)(2,1)} %copy-done.4) | copy-start | bytes 1572868
  59.4 0.6 copy-start.14
  93.0 2.6 %copy-start.8 = (f32[16,128,128]{2,1,0:T(8,128)S(1)}, f32[16,128,128]{2,1,0:T(8,128)}, u32[]{:S(2)}) copy-start(f32[16,128,128]{2,1,0:T(8,128)} %get-tuple-element.32) | copy-start | bytes 3145732
  93.0 4.5 %copy-start.11 = (f32[16,72,256]{2,1,0:T(8,128)S(1)}, f32[16,72,256]{2,1,0:T(8,128)}, u32[]{:S(2)}) copy-start(f32[16,72,256]{2,1,0:T(8,128)} %get-tuple-element.33) | copy-start | bytes 3538948
  95.7 2.7 %copy-start.17 = (f32[16,256]{1,0:T(8,128)S(1)}, f32[16,256]{1,0:T(8,128)}, u32[]{:S(2)}) copy-start(f32[16,256]{1,0:T(8,128)} %copy-done.16) | copy-start | bytes 49156
  95.7 2.7 %copy-start.29 = (f32[16,16]{1,0:T(8,128)S(1)}, f32[16,16]{1,0:T(8,128)}, u32[]{:S(2)}) copy-start(f32[16,16]{1,0:T(8,128)} %get-tuple-element.84) | copy-start | bytes 3076
  95.7 2.7 %copy-start.30 = (f32[16,16]{1,0:T(8,128)S(1)}, f32[16,16]{1,0:T(8,128)}, u32[]{:S(2)}) copy-start(f32[16,16]{1,0:T(8,128)} %get-tuple-element.85) | copy-start | bytes 3076
  95.7 2.7 %copy-start.38 = (pred[16,16]{1,0:T(8,128)(4,1)S(1)}, pred[16,16]{1,0:T(8,128)(4,1)}, u32[]{:S(2)}) copy-start(pred[16,16]{1,0:T(8,128)(4,1)} %subtract_compare_fusion) | copy-start | bytes 772
  97.6 3.1 %copy-start.25 = (f32[16,256]{1,0:T(8,128)S(1)}, f32[16,256]{1,0:T(8,128)}, u32[]{:S(2)}) copy-start(f32[16,256]{1,0:T(8,128)} %exp.95) | copy-start | bytes 49156
  97.6 3.1 %copy-start.34 = (f32[16]{0:T(128)S(1)}, f32[16]{0:T(128)}, u32[]{:S(2)}) copy-start(f32[16]{0:T(128)} %get-tuple-element.95) | copy-start | bytes 196
  97.6 3.1 %copy-start.35 = (f32[16]{0:T(128)S(1)}, f32[16]{0:T(128)}, u32[]{:S(2)}) copy-start(f32[16]{0:T(128)} %get-tuple-element.96) | copy-start | bytes 196
  97.6 3.1 %copy-start.36 = (pred[16]{0:T(512)(128)(4,1)S(1)}, pred[16]{0:T(512)(128)(4,1)}, u32[]{:S(2)}) copy-start(pred[16]{0:T(512)(128)(4,1)} %get-tuple-element.97) | copy-start | bytes 52
  97.6 3.1 %copy-start.37 = (pred[16]{0:T(512)(128)(4,1)S(1)}, pred[16]{0:T(512)(128)(4,1)}, u32[]{:S(2)}) copy-start(pred[16]{0:T(512)(128)(4,1)} %get-tuple-element.98) | copy-start | bytes 52
  97.6 4.8 %copy-start.3 = (f32[8,16,16,16]{1,3,0,2:T(8,128)S(1)}, f32[8,16,16,16]{1,3,0,2:T(8,128)}, u32[]{:S(2)}) copy-start(f32[8,16,16,16]{1,3,0,2:T(8,128)} %copy.107) | copy-start | bytes 393220
  97.6 4.7 %copy-start.7 = (f32[16,8,16,128]{3,2,1,0:T(8,128)S(1)}, f32[16,8,16,128]{3,2,1,0:T(8,128)}, u32[]{:S(2)}) copy-start(f32[16,8,16,128]{3,2,1,0:T(8,128)} %fusion.11) | copy-start | bytes 3145732
  97.6 4.7 %copy-start.18 = (f32[16,16]{1,0:T(8,128)S(1)}, f32[16,16]{1,0:T(8,128)}, u32[]{:S(2)}) copy-start(f32[16,16]{1,0:T(8,128)} %get-tuple-element.76.coef_ref) | copy-start | bytes 3076
  104.6 3.4 %copy-start.24 = (f32[16,256]{1,0:T(8,128)S(1)}, f32[16,256]{1,0:T(8,128)}, u32[]{:S(2)}) copy-start(f32[16,256]{1,0:T(8,128)} %get-tuple-element.45) | copy-start | bytes 49156
  105.2 9.7 %copy-start.1 = (f32[1024,256]{1,0:T(8,128)}, f32[1024,256]{1,0:T(8,128)S(1)}, u32[]{:S(2)}) copy-start(f32[1024,256]{1,0:T(8,128)S(1)} %copy.120.inner_ref) | copy-start | bytes 3145732
  108.1 8.4 %copy-start.40 = (f32[128]{0:T(128)S(1)}, f32[128]{0:T(128)}, u32[]{:S(2)}) copy-start(f32[128]{0:T(128)} %iota_subtract_fusion.2) | copy-start | bytes 1540
  117.7 2.4 %copy-start.23 = (f32[16,256]{1,0:T(8,128)S(1)}, f32[16,256]{1,0:T(8,128)}, u32[]{:S(2)}) copy-start(f32[16,256]{1,0:T(8,128)} %get-tuple-element.48) | copy-start | bytes 49156
  117.7 2.6 %copy-start.22 = (f32[16,256]{1,0:T(8,128)S(1)}, f32[16,256]{1,0:T(8,128)}, u32[]{:S(2)}) copy-start(f32[16,256]{1,0:T(8,128)} %get-tuple-element.47) | copy-start | bytes 49156
  117.7 2.9 %copy-start.28 = (f32[2,256]{1,0:T(2,128)S(1)}, f32[2,256]{1,0:T(2,128)}, u32[]{:S(2)}) copy-start(f32[2,256]{1,0:T(2,128)} %slice_reduce_fusion) | copy-start | bytes 6148
  117.7 3.1 %copy-start.20 = (f32[16,16]{1,0:T(8,128)S(1)}, f32[16,16]{1,0:T(8,128)}, u32[]{:S(2)}) copy-start(f32[16,16]{1,0:T(8,128)} %rate_ref.1) | copy-start | bytes 3076
  117.7 3.1 %copy-start.26 = (f32[16,16]{1,0:T(8,128)S(1)}, f32[16,16]{1,0:T(8,128)}, u32[]{:S(2)}) copy-start(f32[16,16]{1,0:T(8,128)} %param.12) | copy-start | bytes 3076
  118.6 4.0 %copy-start.6 = (f32[1024,256]{1,0:T(8,128)}, f32[1024,256]{1,0:T(8,128)S(1)}, u32[]{:S(2)}) copy-start(f32[1024,256]{1,0:T(8,128)S(1)} %copy.132.grad_ref) | copy-start | bytes 3145732

commit v8 on v7

--- a/solution.py
+++ b/solution.py
@@ -12,7 +12,10 @@
 threepass = lax.Precision.HIGH
 
 
-def gather_kernel(axis, count, x_ref, rate_ref, coef_ref, o_ref, toe_ref, held, send_sem, recv_sem):
+def gather_kernel(
+    axis, count, x_ref, rate_ref, coef_ref, fresh_ref, cols_ref, o_ref, toe_ref, later_ref, held,
+    send_sem, recv_sem,
+):
     me = lax.axis_index(axis)
 
     def device(peer):
@@ -52,33 +55,43 @@
         return carry
 
     lax.fori_loop(0, toe_ref.shape[0], one_group, 0)
+    block_count = fresh_ref.shape[0]
+    step_pow = [jnp.exp(-cols_ref[...] * (span * float(k))) for k in range(block_count - 1)]
+    for block in range(block_count):
+        total = jnp.zeros(fresh_ref.shape[1:], jnp.float32)
+        for later in range(block + 1, block_count):
+            total = total + step_pow[later - block - 1] * fresh_ref[later]
+        later_ref[block] = total
     for copy in copies:
         copy.wait()
     held[me] = x_ref[...]
     o_ref[...] = held[...]
 
 
-def gather_along(value, axis, collective_id, rates, coefs, span):
+def gather_along(value, axis, collective_id, rates, coefs, span, fresh, cols):
     count = lax.axis_size(axis)
     return pl.pallas_call(
         functools.partial(gather_kernel, axis, count),
         out_shape=(
             jax.ShapeDtypeStruct((count,) + value.shape, value.dtype),
             jax.ShapeDtypeStruct((rates.shape[0], span, span), jnp.float32),
+            jax.ShapeDtypeStruct(fresh.shape, jnp.float32),
         ),
         in_specs=[
             pl.BlockSpec(memory_space=pltpu.VMEM),
             pl.BlockSpec(memory_space=pltpu.SMEM),
             pl.BlockSpec(memory_space=pltpu.SMEM),
+            pl.BlockSpec(memory_space=pltpu.VMEM),
+            pl.BlockSpec(memory_space=pltpu.VMEM),
         ],
-        out_specs=(pl.BlockSpec(memory_space=pltpu.VMEM), pl.BlockSpec(memory_space=pltpu.VMEM)),
+        out_specs=(pl.BlockSpec(memory_space=pltpu.VMEM),) * 3,
         scratch_shapes=[
             pltpu.VMEM((count,) + value.shape, value.dtype),
             pltpu.SemaphoreType.DMA((count - 1,)),
             pltpu.SemaphoreType.DMA((count - 1,)),
         ],
         compiler_params=pltpu.CompilerParams(collective_id=collective_id, has_side_effects=True),
-    )(value, rates, coefs)
+    )(value, rates, coefs, fresh, cols)
 
 
 def finish_kernel(
@@ -256,7 +269,6 @@
     first_local = first_acc.T + first_in
     lag_local = lag_acc.T - lag_in
     fresh_bwd = jnp.einsum("gnt,btgm->bngm", block_pow, e_blocks, precision=precise)
-    later_states = jnp.sum(jnp.swapaxes(span_weight, 0, 1) * fresh_bwd[None], axis=1)
     rates_ng = decay_rates.T[None, :, :, None]
     from_first = jnp.exp(-rates_ng * (block_len * block_ids[:, None, None, None]))
     from_last = jnp.exp(-rates_ng * (block_len * (block_count - 1.0 - block_ids[:, None, None, None])))
@@ -281,7 +293,11 @@
         partial_rows
     )
     rate_cols = jnp.repeat(decay_rates.T, members, axis=1)
-    gathered, toeplitz = gather_along(local_states, "ctx", 0, decay_rates, mode_coefs, block_len)
+    gathered, toeplitz, later_flat = gather_along(
+        local_states, "ctx", 0, decay_rates, mode_coefs, block_len,
+        fresh_bwd.reshape(block_count, order_count, channels), rate_cols,
+    )
+    later_states = later_flat.reshape(block_count, order_count, group_count, members)
     inside_fwd = jnp.einsum("gts,bsgm->btgm", toeplitz, z_wide, precision=threepass)
     inside_bwd = jnp.einsum("gts,btgm->bsgm", toeplitz, e_blocks, precision=precise)
     everyone = gathered[:, : state_rows.shape[0]].reshape(ctx_count, 4, order_count, channels)

time: 159 us -> 160 us (level)
  local copies, waits for them, and re-layouts: 34.7 us -> 36.8 us
  other arithmetic: 37 us -> 35.4 us
    reduce_sum x1 -> x0, other arithmetic: 5.03 us -> none  [per_device(): jnp.sum(jnp.swapaxes(span_weight, 0, 1) * fresh_bwd[None], axis=1)]
    reshape x0 -> x4, local copies, waits for them, and re-layouts: none -> 4.16 us  [the longest x2 3 us: per_device(): later_flat.reshape(block_count, order_count, group_count, members)]
    add x1, other arithmetic: 1.03 us -> 4 us  [short_conv(): summed + taps_table[:, offset, None, :] * row_data[:, start_row:start_row...]
    reduce_sum x1 -> x0, local copies, waits for them, and re-layouts: 1.66 us -> none  [per_device(): jnp.sum(jnp.swapaxes(span_weight, 0, 1) * fresh_bwd[None], axis=1)]
where the time goes in v8:
time: 160 us; the launch traced here: 159 us
  Pallas kernels  63.1 us (39%)
  local copies, waits for them, and re-layouts  36.8 us (23%)
  other arithmetic  35.4 us (22%)
  matrix products  17 us (11%)
  starting transfers between devices  4.36 us (3%)
  between operations  2.1 us (1%)
    pallas_call x1, Pallas kernels, gather_along(): pl.pallas_call(functools.partial(gather_kernel, axis, count), out_shape=(...  33 us
    pallas_call x1, Pallas kernels, finish_exchange(): pl.pallas_call(functools.partial(finish_kernel, fsdp_count, ctx_count), o...  30 us
    unnamed x89, local copies, waits for them, and re-layouts  7.77 us
    reduce_sum x1, other arithmetic, per_device(): jnp.sum(span_weight * (fresh_fwd[1][None] - block_len * block_steps * fre...  5.78 us
    ppermute x1, starting transfers between devices, passed_along(): lax.ppermute(value, axis, [(source, source + steps) for source in range(l...  4.36 us
    squeeze x2, local copies, waits for them, and re-layouts, per_device(): end_state = jnp.sum(from_last * fresh_fwd[0], axis=0)  4.27 us
    add x1, other arithmetic, short_conv(): summed + taps_table[:, offset, None, :] * row_data[:, start_row:start_row...  4 us
  transfers between devices with their start and end apart: 1, of which 0 were waited for; matrix products, arithmetic and copies ran while one was open for 7% of the time, Pallas kernels for 0%

profile of v8, /device:TPU:1, one launch (start us, length us, event | category | flops | bytes accessed | tf_op | source)
XLA Modules:
  0.0 158.7 jit_solution(15355438740009513350)
XLA Ops:
  1.3 4.4 %collective-permute-start = (bf16[3,2,256]{2,1,0:T(2,128)(2,1)S(1)}, bf16[3,2,256]{2,1,0:T(2,128)(2,1)S(1)}, u32[]{:S(2)}, u32[]{:S(2)}) collective-permute-start(bf16[3,2,256]{2,1,0:T(2,128)(2,1)S(1)} %slice.149), channel_id=1, source_target_pairs={{0,1},{1,2},{2,3},{3,4},{4,5},{5,6},{6,7},{7,8},{8,9},{9,10},{10,1... | collective-permute-start | bytes 9224 | tf_op jit(solution)/shard_map/ppermute | solution.py:195
  9.6 0.8 fusion.75
  11.2 1.3 fusion.65
  12.6 0.8 copy.105
  14.3 1.0 exponential_select_fusion.1
  15.3 0.8 exponential_multiply_fusion
  16.7 4.0 %multiply_add_fusion = f32[3,1024,256]{2,1,0:T(8,128)S(1)} fusion(bf16[3,1024,256]{2,1,0:T(8,128)(2,1)} %param.9, bf16[3,2,256]{2,1,0:T(2,128)(2,1)S(1)} %collective-permute-done, f32[3,256]{1,0:T(4,128)S(1)} %get-tuple-element.92, f32[3,256]{1,0:T(4,128)S(1)} %get-tuple-element.93, f32[3,256]{1,0:T(4,128)S(1)} %bitcast.259), kind=kLoop, calls=%fused_computation.5 | loop fusion | flops 11010048 | bytes 4730880 | tf_op jit(solution)/shard_map/add | solution.py:203
  20.7 1.7 %copy-done = f32[3,1024,256]{2,1,0:T(8,128)} copy-done((f32[3,1024,256]{2,1,0:T(8,128)}, f32[3,1024,256]{2,1,0:T(8,128)S(1)}, u32[]{:S(2)}) %copy-start) | copy-done | bytes 3145752
  22.3 1.5 slice_bitcast_fusion.6
  24.2 0.8 copy-done.4
  25.0 0.8 convolution_bitcast_fusion.1
  25.7 1.7 %slice_bitcast_fusion.3 = (f32[8,16,16,16]{1,3,0,2:T(8,128)}, f32[8,16,16,16]{1,3,0,2:T(8,128)}) fusion(f32[2,8,16,16,16]{2,4,0,1,3:T(8,128)S(1)} %convolution_bitcast_fusion.1), kind=kLoop, calls=%fused_computation.28 | loop fusion | bytes 524288 | tf_op jit(solution)/shard_map/squeeze | solution.py:275
  27.4 1.7 %copy.101 = f32[8,16,16,16]{3,2,1,0:T(8,128)S(1)} copy(f32[8,16,16,16]{1,3,0,2:T(8,128)} %get-tuple-element.64) | data formatting | bytes 262144 | tf_op jit(solution)/shard_map/squeeze | solution.py:278
  29.1 2.6 %copy.97 = f32[8,16,16,16]{3,2,1,0:T(8,128)} copy(f32[8,16,16,16]{1,3,0,2:T(8,128)} %get-tuple-element.63) | data formatting | bytes 262144 | tf_op jit(solution)/shard_map/squeeze | solution.py:275
  31.7 5.8 %multiply_reduce_fusion = (f32[8,16,16,16]{3,2,1,0:T(8,128)}, f32[8,16,16,16]{3,2,1,0:T(8,128)}) fusion(f32[8,8]{1,0:T(8,128)S(1)} %get-tuple-element.90, f32[8,16,16,16]{3,2,1,0:T(8,128)S(1)} %copy.101, f32[8,16,16,16]{3,2,1,0:T(8,128)} %copy.97, f32[8,8,16,16]{3,2,1,0:T(8,128)} %exponential_select_fusion.1), kind=kLoop, calls=%fused_computation | loop fusion | flops 1507328 | bytes 590080 | tf_op jit(solution)/shard_map/reduce_sum | solution.py:256
  37.5 2.7 %copy.98 = f32[8,16,16,16]{1,3,0,2:T(8,128)} copy(f32[8,16,16,16]{3,2,1,0:T(8,128)} %get-tuple-element.44) | data formatting | bytes 262144 | tf_op jit(solution)/shard_map/reduce_sum | solution.py:255
  40.1 2.6 %copy.102 = f32[8,16,16,16]{1,3,0,2:T(8,128)} copy(f32[8,16,16,16]{3,2,1,0:T(8,128)} %get-tuple-element.43) | data formatting | bytes 262144 | tf_op jit(solution)/shard_map/reduce_sum | solution.py:256
  42.8 1.5 convert_multiply_fusion
  44.3 1.3 copy.91
  45.6 1.4 copy.147
  47.1 2.1 %fusion.5 = f32[16,128,128]{2,1,0:T(8,128)S(1)} fusion(f32[8,128,16,16]{1,0,3,2:T(8,128)S(1)} %bitcast.236, bf16[8,128,16,16]{1,0,3,2:T(8,128)(2,1)} %bitcast.243, pred[128,128]{1,0:T(8,128)(4,1)S(1)} %copy-done.27), kind=kOutput, calls=%fused_computation.21 | convolution fusion | flops 402915328 | bytes 2637824 | tf_op jit(solution)/shard_map/btgm,bsgm->gts/dot_general | solution.py:262
  49.3 1.9 %fusion.6 = f32[2,16,16,128]{3,2,0,1:T(8,128)S(1)} fusion(f32[16,16]{1,0:T(8,128)S(1)} %copy-done.13, f32[1,16,128,128]{3,2,1,0:T(8,128)S(1)} %multiply_bitcast_fusion, f32[1,16,128,128]{3,2,1,0:T(8,128)S(1)} %bitcast.245), kind=kOutput, calls=%fused_computation.22 | convolution fusion | flops 101220352 | bytes 2360320 | tf_op jit(solution)/shard_map/kgts,gns->kgnt/dot_general | solution.py:266
  51.1 0.8 fusion.37
  52.0 2.0 %convolution_bitcast_fusion = f32[2,8,16,16,16]{2,4,1,3,0:T(8,128)S(1)} fusion(f32[8,128,16,16]{1,0,3,2:T(8,128)S(1)} %bitcast.237, f32[1,16,16,128]{3,2,0,1:T(8,128)S(1)} %copy-done.12, f32[1,16,16,128]{3,2,0,1:T(8,128)S(1)} %copy-done.11), kind=kOutput, calls=%fused_computation.9 | convolution fusion | flops 100728832 | bytes 1572864 | tf_op jit(solution)/shard_map/kgnt,btgm->kbngm/dot_general | solution.py:259
  54.0 2.8 %multiply_reduce_fusion.4 = (f32[16,16]{0,1:T(8,128)S(1)}, f32[16,16]{0,1:T(8,128)S(1)}, f32[16,16,16]{0,2,1:T(8,128)S(1)}, f32[16,16,16]{0,2,1:T(8,128)S(1)}, f32[8,16,16,16]{1,3,0,2:T(8,128)}) fusion(f32[8,16,16,16]{1,3,0,2:T(8,128)S(1)} %copy-done.2, f32[2,8,16,16,16]{2,4,1,3,0:T(8,128)S(1)} %convolution_bitcast_fusion, ...), kind=kOutput, calls=%fused_computation.42 | convolution fusion | flops 50748928 | bytes 1748000 | tf_op jit(solution)/shard_map/gnt,btgm->bngm/dot_general | solution.py:271
  57.4 1.3 stack.74
  58.7 1.3 bitcast_subtract_fusion
  60.0 0.8 stack.75
  60.8 1.0 multiply_reduce_fusion.8
  62.3 1.7 %copy.104 = f32[8,16,16,16]{3,2,1,0:T(8,128)S(1)} copy(f32[8,16,16,16]{1,3,0,2:T(8,128)} %get-tuple-element.91) | data formatting | bytes 262144 | tf_op jit(solution)/shard_map/gnt,btgm->bngm/transpose | solution.py:271
  64.1 1.1 reshape.426.fresh_ref
  65.8 33.0 %shard_map.84 = (f32[16,72,256]{2,1,0:T(8,128)}, f32[16,128,128]{2,1,0:T(8,128)}, f32[8,16,256]{2,1,0:T(8,128)}) custom-call(f32[72,256]{1,0:T(8,128)} %copy-done.15, f32[16,16]{1,0:T(8,128)} %rate_ref.1, f32[16,16]{1,0:T(8,128)} %get-tuple-element.80.coef_ref, f32[8,16,256]{2,1,0:T(8,128)} %reshape.426.fresh_ref, f32[16,256]{1,0:T(8,128)} %copy-done.17), custom_call_target="tpu_custom_call" | custom-call | tf_op jit(solution)/shard_map/pallas_call | solution.py:73
  98.8 2.6 %fusion.9 = f32[16,8,16,128]{3,2,1,0:T(8,128)S(1)} fusion(f32[16,128,128]{2,1,0:T(8,128)} %get-tuple-element.33, f32[8,128,16,16]{1,0,3,2:T(8,128)S(1)} %bitcast.239), kind=kOutput, calls=%fused_computation.30 | convolution fusion | flops 402653184 | bytes 3145728 | tf_op jit(solution)/shard_map/gts,btgm->bsgm/dot_general | solution.py:302
  101.5 1.8 %fusion.11 = f32[16,8,16,128]{3,2,1,0:T(8,128)} fusion(f32[16,128,128]{2,1,0:T(8,128)S(1)} %copy-done.8, bf16[8,128,16,16]{1,0,3,2:T(8,128)(2,1)S(1)} %bitcast.244), kind=kOutput, calls=%fused_computation.32 | convolution fusion | flops 201326592 | bytes 2621440 | tf_op jit(solution)/shard_map/gts,bsgm->btgm/dot_general | solution.py:301
  104.2 2.2 %multiply_reduce_fusion.2 = (f32[16,16,256]{2,1,0:T(8,128)S(1)}, f32[16,16,256]{2,1,0:T(8,128)S(1)}) fusion(f32[16,16]{1,0:T(8,128)S(1)} %copy-done.30, f32[16,16,256]{2,1,0:T(8,128)S(1)} %get-tuple-element.66, f32[16,16,256]{2,1,0:T(8,128)S(1)} %get-tuple-element.65, f32[16,16]{1,0:T(8,128)S(1)} %copy-done.29, f32[16,256]{1,0:T(8,128)S(1)} %copy-done.22, ...), kind=kLoop, calls=%fused_computation.2 | loop fusion | flops 8257536 | bytes 1067264 | tf_op jit(solution)/shard_map/reduce_sum | solution.py:323
  106.5 0.8 multiply_reduce_fusion.9
  107.3 0.8 copy.136
  108.2 1.9 %fusion.4 = f32[8,128,16,16]{1,3,0,2:T(8,128)S(1)} fusion(f32[16,8,16,128]{3,2,1,0:T(8,128)S(1)} %copy-done.7, f32[8,16,16,16]{1,3,0,2:T(8,128)S(1)} %copy-done.3, f32[16,16,16]{0,2,1:T(8,128)S(1)} %bitcast.253, f32[8,16,16]{1,0,2:T(8,128)S(1)} %get-tuple-element.84, f32[16,16]{1,0:T(8,128)} %copy-done.20, f32[16,16]{1,0:T(8,128)S(1)} %copy-done.18, ...), kind=kOutput, calls=%fused_computation.19 | convolution fusion | flops 50757632 | bytes 2255872 | tf_op jit(solution)/shard_map/gnt,bngm->btgm/dot_general | solution.py:342
  111.0 0.7 fusion.72
  111.8 2.1 %multiply_convert_fusion = bf16[1024,256]{1,0:T(8,128)(2,1)} fusion(f32[1024,256]{1,0:T(8,128)S(1)} %copy.111.inner_ref, f32[3,1024,256]{2,1,0:T(8,128)} %copy-done), kind=kLoop, calls=%fused_computation.37 | loop fusion | flops 524288 | bytes 2621440 | tf_op jit(solution)/shard_map/convert_element_type | solution.py:349
  114.0 1.3 reshape.431
  115.3 1.7 %copy.119 = f32[8,16,16,16]{1,3,0,2:T(8,128)S(1)} copy(f32[8,16,16,16]{3,2,1,0:T(8,128)} %reshape.431) | data formatting | bytes 262144 | tf_op jit(solution)/shard_map/reshape | solution.py:300
  117.0 1.2 fusion.3
  119.1 0.8 fusion.71
  122.0 1.2 broadcast_in_dim.93.tile_ref
  123.2 30.0 %shard_map.85 = (f32[32,8,128]{2,1,0:T(8,128)}, bf16[3,1024,256]{2,1,0:T(8,128)(2,1)}) custom-call(f32[8,128]{1,0:T(8,128)} %broadcast_in_dim.93.tile_ref, f32[6,256]{1,0:T(8,128)} %reshape.432.rim_ref, bf16[1024,256]{1,0:T(8,128)(2,1)} %cot_ref.1, f32[1024,256]{1,0:T(8,128)} %copy-done.1, f32[1024,256]{1,0:T(8,128)} %copy-done.6, ...), custom_call_target="tpu_custom_call" | custom-call | tf_op jit(solution)/shard_map/pallas_call | solution.py:171
  153.2 1.5 slice_reduce_fusion.1
  156.1 2.7 %copy.180 = bf16[3,1024,256]{2,1,0:T(8,128)(2,1)} copy(bf16[3,1024,256]{2,1,0:T(8,128)(2,1)} %get-tuple-element.107) | data formatting | bytes 3145728
  (139 shorter events, 14.3 us)
Async XLA Ops:
  1.3 15.3 %collective-permute-start = (bf16[3,2,256]{2,1,0:T(2,128)(2,1)S(1)}, bf16[3,2,256]{2,1,0:T(2,128)(2,1)S(1)}, u32[]{:S(2)}, u32[]{:S(2)}) collective-permute-start(bf16[3,2,256]{2,1,0:T(2,128)(2,1)S(1)} %slice.149), channel_id=1, source_target_pairs={{0,1},{1,2},{2,3},{3,4},{4,5},{5,6},{6,7},{7,8},{8,9},{9,10},{10,1... | collective-permute-start | bytes 9224 | tf_op jit(solution)/shard_map/ppermute | solution.py:195
  5.9 9.4 %copy-start.32 = (f32[8]{0:T(128)}, f32[8]{0:T(128)S(1)}, u32[]{:S(2)}) copy-start(f32[8]{0:T(128)S(1)} %get-tuple-element.96) | copy-start | bytes 100
  5.9 9.4 %copy-start.39 = (f32[8]{0:T(128)}, f32[8]{0:T(128)S(1)}, u32[]{:S(2)}) copy-start(f32[8]{0:T(128)S(1)} %get-tuple-element.97) | copy-start | bytes 100
  12.5 4.2 %copy-start.20 = (f32[16,16]{1,0:T(8,128)}, f32[16,16]{1,0:T(8,128)S(1)}, u32[]{:S(2)}) copy-start(f32[16,16]{1,0:T(8,128)S(1)} %get-tuple-element.81) | copy-start | bytes 3076
  13.5 3.1 %copy-start.17 = (f32[16,256]{1,0:T(8,128)}, f32[16,256]{1,0:T(8,128)S(1)}, u32[]{:S(2)}) copy-start(f32[16,256]{1,0:T(8,128)S(1)} %reshape.427.cols_ref) | copy-start | bytes 49156
  20.7 1.7 %copy-start = (f32[3,1024,256]{2,1,0:T(8,128)}, f32[3,1024,256]{2,1,0:T(8,128)S(1)}, u32[]{:S(2)}) copy-start(f32[3,1024,256]{2,1,0:T(8,128)S(1)} %multiply_add_fusion) | copy-start | bytes 9437188
  24.2 0.8 copy-start.4
  42.8 4.3 %copy-start.27 = (pred[128,128]{1,0:T(8,128)(4,1)S(1)}, pred[128,128]{1,0:T(8,128)(4,1)}, u32[]{:S(2)}) copy-start(pred[128,128]{1,0:T(8,128)(4,1)} %fusion.54) | copy-start | bytes 49156
  47.0 2.1 %copy-start.16 = (f32[128,128]{1,0:T(8,128)S(1)}, f32[128,128]{1,0:T(8,128)}, u32[]{:S(2)}) copy-start(f32[128,128]{1,0:T(8,128)} %maximum_convert_fusion) | copy-start | bytes 196612
  47.1 2.2 %copy-start.13 = (f32[16,16]{1,0:T(8,128)S(1)}, f32[16,16]{1,0:T(8,128)}, u32[]{:S(2)}) copy-start(f32[16,16]{1,0:T(8,128)} %rate_ref.1) | copy-start | bytes 3076
  49.2 2.8 %copy-start.11 = (f32[1,16,16,128]{3,2,0,1:T(8,128)S(1)}, f32[1,16,16,128]{3,2,0,1:T(8,128)}, u32[]{:S(2)}) copy-start(f32[1,16,16,128]{3,2,0,1:T(8,128)} %get-tuple-element.73) | copy-start | bytes 393220
  49.2 2.8 %copy-start.12 = (f32[1,16,16,128]{3,2,0,1:T(8,128)S(1)}, f32[1,16,16,128]{3,2,0,1:T(8,128)}, u32[]{:S(2)}) copy-start(f32[1,16,16,128]{3,2,0,1:T(8,128)} %get-tuple-element.74) | copy-start | bytes 393220
  49.3 4.8 %copy-start.2 = (f32[8,16,16,16]{1,3,0,2:T(8,128)S(1)}, f32[8,16,16,16]{1,3,0,2:T(8,128)}, u32[]{:S(2)}) copy-start(f32[8,16,16,16]{1,3,0,2:T(8,128)} %copy.98) | copy-start | bytes 393220
  49.3 4.8 %copy-start.9 = (f32[8,16,16,16]{1,3,0,2:T(8,128)S(1)}, f32[8,16,16,16]{1,3,0,2:T(8,128)}, u32[]{:S(2)}) copy-start(f32[8,16,16,16]{1,3,0,2:T(8,128)} %copy.102) | copy-start | bytes 393220
  49.3 4.8 %copy-start.33 = (f32[8]{0:T(128)S(1)}, f32[8]{0:T(128)}, u32[]{:S(2)}) copy-start(f32[8]{0:T(128)} %copy-done.32) | copy-start | bytes 100
  61.7 3.4 %copy-start.31 = (f32[1,256]{1,0:T(1,128)S(1)}, f32[1,256]{1,0:T(1,128)}, u32[]{:S(2)}) copy-start(f32[1,256]{1,0:T(1,128)} %stack.74) | copy-start | bytes 3076
  62.3 39.1 %copy-start.5 = (bf16[32,8,8,128]{3,2,1,0:T(8,128)(2,1)S(1)}, bf16[32,8,8,128]{3,2,1,0:T(8,128)(2,1)}, u32[]{:S(2)}) copy-start(bf16[32,8,8,128]{3,2,1,0:T(8,128)(2,1)} %copy-done.4) | copy-start | bytes 1572868
  65.2 0.6 copy-start.15
  98.8 2.6 %copy-start.8 = (f32[16,128,128]{2,1,0:T(8,128)S(1)}, f32[16,128,128]{2,1,0:T(8,128)}, u32[]{:S(2)}) copy-start(f32[16,128,128]{2,1,0:T(8,128)} %get-tuple-element.33) | copy-start | bytes 3145732
  98.8 4.5 %copy-start.10 = (f32[16,72,256]{2,1,0:T(8,128)S(1)}, f32[16,72,256]{2,1,0:T(8,128)}, u32[]{:S(2)}) copy-start(f32[16,72,256]{2,1,0:T(8,128)} %get-tuple-element.34) | copy-start | bytes 3538948
  101.5 2.7 %copy-start.22 = (f32[16,256]{1,0:T(8,128)S(1)}, f32[16,256]{1,0:T(8,128)}, u32[]{:S(2)}) copy-start(f32[16,256]{1,0:T(8,128)} %get-tuple-element.72) | copy-start | bytes 49156
  101.5 2.7 %copy-start.29 = (f32[16,16]{1,0:T(8,128)S(1)}, f32[16,16]{1,0:T(8,128)}, u32[]{:S(2)}) copy-start(f32[16,16]{1,0:T(8,128)} %get-tuple-element.87) | copy-start | bytes 3076
  101.5 2.7 %copy-start.30 = (f32[16,16]{1,0:T(8,128)S(1)}, f32[16,16]{1,0:T(8,128)}, u32[]{:S(2)}) copy-start(f32[16,16]{1,0:T(8,128)} %get-tuple-element.88) | copy-start | bytes 3076
  101.5 2.7 %copy-start.38 = (pred[16,16]{1,0:T(8,128)(4,1)S(1)}, pred[16,16]{1,0:T(8,128)(4,1)}, u32[]{:S(2)}) copy-start(pred[16,16]{1,0:T(8,128)(4,1)} %subtract_compare_fusion) | copy-start | bytes 772
  103.3 3.1 %copy-start.21 = (f32[16,256]{1,0:T(8,128)S(1)}, f32[16,256]{1,0:T(8,128)}, u32[]{:S(2)}) copy-start(f32[16,256]{1,0:T(8,128)} %get-tuple-element.71) | copy-start | bytes 49156
  103.3 3.1 %copy-start.34 = (pred[16]{0:T(512)(128)(4,1)S(1)}, pred[16]{0:T(512)(128)(4,1)}, u32[]{:S(2)}) copy-start(pred[16]{0:T(512)(128)(4,1)} %get-tuple-element.100) | copy-start | bytes 52
  103.3 3.1 %copy-start.35 = (pred[16]{0:T(512)(128)(4,1)S(1)}, pred[16]{0:T(512)(128)(4,1)}, u32[]{:S(2)}) copy-start(pred[16]{0:T(512)(128)(4,1)} %get-tuple-element.101) | copy-start | bytes 52
  103.4 3.1 %copy-start.36 = (f32[16]{0:T(128)S(1)}, f32[16]{0:T(128)}, u32[]{:S(2)}) copy-start(f32[16]{0:T(128)} %get-tuple-element.98) | copy-start | bytes 196
  103.4 3.1 %copy-start.37 = (f32[16]{0:T(128)S(1)}, f32[16]{0:T(128)}, u32[]{:S(2)}) copy-start(f32[16]{0:T(128)} %get-tuple-element.99) | copy-start | bytes 196
  103.4 4.8 %copy-start.3 = (f32[8,16,16,16]{1,3,0,2:T(8,128)S(1)}, f32[8,16,16,16]{1,3,0,2:T(8,128)}, u32[]{:S(2)}) copy-start(f32[8,16,16,16]{1,3,0,2:T(8,128)} %copy.98) | copy-start | bytes 393220
  103.4 4.8 %copy-start.7 = (f32[16,8,16,128]{3,2,1,0:T(8,128)S(1)}, f32[16,8,16,128]{3,2,1,0:T(8,128)}, u32[]{:S(2)}) copy-start(f32[16,8,16,128]{3,2,1,0:T(8,128)} %fusion.11) | copy-start | bytes 3145732
  103.4 4.8 %copy-start.18 = (f32[16,16]{1,0:T(8,128)S(1)}, f32[16,16]{1,0:T(8,128)}, u32[]{:S(2)}) copy-start(f32[16,16]{1,0:T(8,128)} %get-tuple-element.80.coef_ref) | copy-start | bytes 3076
  110.4 3.4 %copy-start.25 = (f32[16,256]{1,0:T(8,128)S(1)}, f32[16,256]{1,0:T(8,128)}, u32[]{:S(2)}) copy-start(f32[16,256]{1,0:T(8,128)} %get-tuple-element.47) | copy-start | bytes 49156
  110.4 3.5 %copy-start.19 = (f32[8,16,256]{2,1,0:T(8,128)S(1)}, f32[8,16,256]{2,1,0:T(8,128)}, u32[]{:S(2)}) copy-start(f32[8,16,256]{2,1,0:T(8,128)} %get-tuple-element.35) | copy-start | bytes 393220
  111.0 7.2 %copy-start.1 = (f32[1024,256]{1,0:T(8,128)}, f32[1024,256]{1,0:T(8,128)S(1)}, u32[]{:S(2)}) copy-start(f32[1024,256]{1,0:T(8,128)S(1)} %copy.111.inner_ref) | copy-start | bytes 3145732
  111.0 6.0 %copy-start.40 = (f32[128]{0:T(128)S(1)}, f32[128]{0:T(128)}, u32[]{:S(2)}) copy-start(f32[128]{0:T(128)} %iota_subtract_fusion.2) | copy-start | bytes 1540
  118.2 2.4 %copy-start.24 = (f32[16,256]{1,0:T(8,128)S(1)}, f32[16,256]{1,0:T(8,128)}, u32[]{:S(2)}) copy-start(f32[16,256]{1,0:T(8,128)} %get-tuple-element.50) | copy-start | bytes 49156
  118.2 2.6 %copy-start.23 = (f32[16,256]{1,0:T(8,128)S(1)}, f32[16,256]{1,0:T(8,128)}, u32[]{:S(2)}) copy-start(f32[16,256]{1,0:T(8,128)} %get-tuple-element.49) | copy-start | bytes 49156
  118.2 2.9 %copy-start.28 = (f32[2,256]{1,0:T(2,128)S(1)}, f32[2,256]{1,0:T(2,128)}, u32[]{:S(2)}) copy-start(f32[2,256]{1,0:T(2,128)} %slice_reduce_fusion) | copy-start | bytes 6148
  118.2 3.1 %copy-start.14 = (f32[16,16]{1,0:T(8,128)S(1)}, f32[16,16]{1,0:T(8,128)}, u32[]{:S(2)}) copy-start(f32[16,16]{1,0:T(8,128)} %rate_ref.1) | copy-start | bytes 3076
  118.2 3.1 %copy-start.26 = (f32[16,16]{1,0:T(8,128)S(1)}, f32[16,16]{1,0:T(8,128)}, u32[]{:S(2)}) copy-start(f32[16,16]{1,0:T(8,128)} %param.12) | copy-start | bytes 3076
  119.1 4.0 %copy-start.6 = (f32[1024,256]{1,0:T(8,128)}, f32[1024,256]{1,0:T(8,128)S(1)}, u32[]{:S(2)}) copy-start(f32[1024,256]{1,0:T(8,128)S(1)} %copy.121.grad_ref) | copy-start | bytes 3145732

commit v9 on v7

--- a/solution.py
+++ b/solution.py
@@ -146,7 +146,10 @@
         )
     conv_rows(early, tokens - early)
     tiles_held[f_me] = tile_ref[...]
-    tiles_out[...] = tiles_held[...]
+    total = tiles_held[0]
+    for slot in range(1, fsdp_count):
+        total = total + tiles_held[slot]
+    tiles_out[...] = total
 
 
 def finish_exchange(tile, rim, cot, inner, grad, value, key, taps):
@@ -158,7 +161,7 @@
     return pl.pallas_call(
         functools.partial(finish_kernel, fsdp_count, ctx_count),
         out_shape=(
-            jax.ShapeDtypeStruct((fsdp_count,) + tile.shape, tile.dtype),
+            jax.ShapeDtypeStruct(tile.shape, tile.dtype),
             jax.ShapeDtypeStruct((3, tokens, channels), jnp.bfloat16),
         ),
         in_specs=[pl.BlockSpec(memory_space=pltpu.VMEM)] * 8,
@@ -347,7 +350,7 @@
     square_tiles, feature_grads = finish_exchange(
         square_tile, rim_send, cotangent, inner_flat, grad_flat, value_part, key_part, short_taps
     )
-    squares = jnp.sum(square_tiles[:, 0, 0])
+    squares = square_tiles[0, 0]
     factor = jnp.minimum(1.0, lax.rsqrt(squares / entry_count + 1e-06))
     clipped = summed * factor
     return (mixer_output, feature_grads, clipped[0], clipped[1])

time: 159 us -> 159 us (level)
  no operation moved by 1% of the time
where the time goes in v9:
time: 159 us; the launch traced here: 158 us
  Pallas kernels  63 us (40%)
  local copies, waits for them, and re-layouts  35.9 us (23%)
  other arithmetic  35.5 us (22%)
  matrix products  17 us (11%)
  starting transfers between devices  4.36 us (3%)
  between operations  2.11 us (1%)
    pallas_call x1, Pallas kernels, gather_along(): pl.pallas_call(functools.partial(gather_kernel, axis, count), out_shape=(...  33 us
    pallas_call x1, Pallas kernels, finish_exchange(): pl.pallas_call(functools.partial(finish_kernel, fsdp_count, ctx_count), o...  30 us
    unnamed x89, local copies, waits for them, and re-layouts  7.84 us
    reduce_sum x1, other arithmetic, per_device(): jnp.sum(span_weight * (fresh_fwd[1][None] - block_len * block_steps * fre...  5.78 us
    reduce_sum x1, other arithmetic, per_device(): jnp.sum(jnp.swapaxes(span_weight, 0, 1) * fresh_bwd[None], axis=1)  5.03 us
    ppermute x1, starting transfers between devices, passed_along(): lax.ppermute(value, axis, [(source, source + steps) for source in range(l...  4.36 us
    squeeze x2, local copies, waits for them, and re-layouts, per_device(): end_state = jnp.sum(from_last * fresh_fwd[0], axis=0)  3.31 us
  transfers between devices with their start and end apart: 1, of which 0 were waited for; matrix products, arithmetic and copies ran while one was open for 7% of the time, Pallas kernels for 0%

profile of v9, /device:TPU:1, one launch (start us, length us, event | category | flops | bytes accessed | tf_op | source)
XLA Modules:
  0.0 157.8 jit_solution(10001836855224394435)
XLA Ops:
  0.6 0.8 slice.149
  1.5 4.4 %collective-permute-start = (bf16[3,2,256]{2,1,0:T(2,128)(2,1)S(1)}, bf16[3,2,256]{2,1,0:T(2,128)(2,1)S(1)}, u32[]{:S(2)}, u32[]{:S(2)}) collective-permute-start(bf16[3,2,256]{2,1,0:T(2,128)(2,1)S(1)} %slice.149), channel_id=1, source_target_pairs={{0,1},{1,2},{2,3},{3,4},{4,5},{5,6},{6,7},{7,8},{8,9},{9,10},{10,1... | collective-permute-start | bytes 9224 | tf_op jit(solution)/shard_map/ppermute | solution.py:185
  9.7 0.8 fusion.75
  10.6 1.3 fusion.65
  12.1 1.0 select_bitcast_fusion
  13.2 1.0 exponential_select_fusion.1
  14.2 0.8 exponential_multiply_fusion
  16.6 1.0 multiply_add_fusion
  17.6 1.7 %copy-done = f32[3,1024,256]{2,1,0:T(8,128)} copy-done((f32[3,1024,256]{2,1,0:T(8,128)}, f32[3,1024,256]{2,1,0:T(8,128)S(1)}, u32[]{:S(2)}) %copy-start) | copy-done | bytes 3145752
  19.2 1.5 slice_bitcast_fusion.6
  21.1 0.8 copy-done.4
  21.9 0.8 convolution_bitcast_fusion.1
  22.7 1.6 %slice_bitcast_fusion.3 = (f32[8,16,16,16]{1,3,0,2:T(8,128)}, f32[8,16,16,16]{1,3,0,2:T(8,128)}) fusion(f32[2,8,16,16,16]{2,4,0,1,3:T(8,128)S(1)} %convolution_bitcast_fusion.1), kind=kLoop, calls=%fused_computation.29 | loop fusion | bytes 524288 | tf_op jit(solution)/shard_map/squeeze | solution.py:266
  24.3 1.7 %copy.106 = f32[8,16,16,16]{3,2,1,0:T(8,128)S(1)} copy(f32[8,16,16,16]{1,3,0,2:T(8,128)} %get-tuple-element.61) | data formatting | bytes 262144 | tf_op jit(solution)/shard_map/squeeze | solution.py:266
  26.0 2.6 %copy.110 = f32[8,16,16,16]{3,2,1,0:T(8,128)} copy(f32[8,16,16,16]{1,3,0,2:T(8,128)} %get-tuple-element.62) | data formatting | bytes 262144 | tf_op jit(solution)/shard_map/squeeze | solution.py:269
  28.7 5.8 %multiply_reduce_fusion.1 = (f32[8,16,16,16]{3,2,1,0:T(8,128)}, f32[8,16,16,16]{3,2,1,0:T(8,128)}) fusion(f32[8,8]{1,0:T(8,128)S(1)} %copy.111, f32[8,16,16,16]{3,2,1,0:T(8,128)} %copy.110, f32[8,16,16,16]{3,2,1,0:T(8,128)S(1)} %copy.106, f32[8,8,16,16]{3,2,1,0:T(8,128)} %exponential_select_fusion.1), kind=kLoop, calls=%fused_computation.1 | loop fusion | flops 1507328 | bytes 590080 | tf_op jit(solution)/shard_map/reduce_sum | solution.py:246
  34.4 2.7 %copy.107 = f32[8,16,16,16]{1,3,0,2:T(8,128)} copy(f32[8,16,16,16]{3,2,1,0:T(8,128)} %get-tuple-element.42) | data formatting | bytes 262144 | tf_op jit(solution)/shard_map/reduce_sum | solution.py:245
  37.1 2.6 %copy.112 = f32[8,16,16,16]{1,3,0,2:T(8,128)} copy(f32[8,16,16,16]{3,2,1,0:T(8,128)} %get-tuple-element.41) | data formatting | bytes 262144 | tf_op jit(solution)/shard_map/reduce_sum | solution.py:246
  39.7 1.5 convert_multiply_fusion
  41.2 1.3 copy.98
  42.5 1.4 copy.158
  44.0 2.1 %fusion.5 = f32[16,128,128]{2,1,0:T(8,128)S(1)} fusion(f32[8,128,16,16]{1,0,3,2:T(8,128)S(1)} %bitcast.239, bf16[8,128,16,16]{1,0,3,2:T(8,128)(2,1)} %bitcast.246, pred[128,128]{1,0:T(8,128)(4,1)S(1)} %copy-done.27), kind=kOutput, calls=%fused_computation.22 | convolution fusion | flops 402915328 | bytes 2637824 | tf_op jit(solution)/shard_map/btgm,bsgm->gts/dot_general | solution.py:252
  46.2 1.9 %fusion.6 = f32[2,16,16,128]{3,2,0,1:T(8,128)S(1)} fusion(f32[16,16]{1,0:T(8,128)S(1)} %copy-done.19, f32[1,16,128,128]{3,2,1,0:T(8,128)S(1)} %multiply_bitcast_fusion, f32[1,16,128,128]{3,2,1,0:T(8,128)S(1)} %bitcast.248), kind=kOutput, calls=%fused_computation.23 | convolution fusion | flops 101220352 | bytes 2360320 | tf_op jit(solution)/shard_map/kgts,gns->kgnt/dot_general | solution.py:256
  48.1 0.8 fusion.37
  48.9 2.0 %convolution_bitcast_fusion = f32[2,8,16,16,16]{2,4,1,3,0:T(8,128)S(1)} fusion(f32[8,128,16,16]{1,0,3,2:T(8,128)S(1)} %bitcast.240, f32[1,16,16,128]{3,2,0,1:T(8,128)S(1)} %copy-done.13, f32[1,16,16,128]{3,2,0,1:T(8,128)S(1)} %copy-done.12), kind=kOutput, calls=%fused_computation.10 | convolution fusion | flops 100728832 | bytes 1572864 | tf_op jit(solution)/shard_map/kgnt,btgm->kbngm/dot_general | solution.py:249
  51.0 2.8 %multiply_reduce_fusion.5 = (f32[16,16]{0,1:T(8,128)S(1)}, f32[16,16]{0,1:T(8,128)S(1)}, f32[16,16,16]{0,2,1:T(8,128)S(1)}, f32[16,16,16]{0,2,1:T(8,128)S(1)}, f32[8,16,16,16]{1,3,0,2:T(8,128)}) fusion(f32[8,16,16,16]{1,3,0,2:T(8,128)S(1)} %copy-done.2, f32[2,8,16,16,16]{2,4,1,3,0:T(8,128)S(1)} %convolution_bitcast_fusion, ...), kind=kOutput, calls=%fused_computation.43 | convolution fusion | flops 50748928 | bytes 1748000 | tf_op jit(solution)/shard_map/gnt,btgm->bngm/dot_general | solution.py:261
  54.3 1.4 stack.74
  55.7 1.3 bitcast_subtract_fusion
  57.0 0.8 stack.75
  57.8 1.0 multiply_reduce_fusion.9
  60.0 33.0 %shard_map.84 = (f32[16,72,256]{2,1,0:T(8,128)}, f32[16,128,128]{2,1,0:T(8,128)}) custom-call(f32[72,256]{1,0:T(8,128)} %copy-done.14, f32[16,16]{1,0:T(8,128)} %rate_ref.1, f32[16,16]{1,0:T(8,128)} %get-tuple-element.76.coef_ref), custom_call_target="tpu_custom_call" | custom-call | tf_op jit(solution)/shard_map/pallas_call | solution.py:63
  93.0 2.6 %fusion.9 = f32[16,8,16,128]{3,2,1,0:T(8,128)S(1)} fusion(f32[16,128,128]{2,1,0:T(8,128)} %get-tuple-element.32, f32[8,128,16,16]{1,0,3,2:T(8,128)S(1)} %bitcast.242), kind=kOutput, calls=%fused_computation.31 | convolution fusion | flops 402653184 | bytes 3145728 | tf_op jit(solution)/shard_map/gts,btgm->bsgm/dot_general | solution.py:289
  95.7 1.8 %fusion.11 = f32[16,8,16,128]{3,2,1,0:T(8,128)} fusion(f32[16,128,128]{2,1,0:T(8,128)S(1)} %copy-done.8, bf16[8,128,16,16]{1,0,3,2:T(8,128)(2,1)S(1)} %bitcast.247), kind=kOutput, calls=%fused_computation.33 | convolution fusion | flops 201326592 | bytes 2621440 | tf_op jit(solution)/shard_map/gts,bsgm->btgm/dot_general | solution.py:288
  98.4 2.2 %multiply_reduce_fusion.3 = (f32[16,16,256]{2,1,0:T(8,128)S(1)}, f32[16,16,256]{2,1,0:T(8,128)S(1)}) fusion(f32[16,16]{1,0:T(8,128)S(1)} %copy-done.30, f32[16,16,256]{2,1,0:T(8,128)S(1)} %get-tuple-element.64, f32[16,16,256]{2,1,0:T(8,128)S(1)} %get-tuple-element.63, f32[16,16]{1,0:T(8,128)S(1)} %copy-done.29, f32[16,256]{1,0:T(8,128)S(1)} %copy-done.17, ...), kind=kLoop, calls=%fused_computation.3 | loop fusion | flops 8257536 | bytes 1067264 | tf_op jit(solution)/shard_map/reduce_sum | solution.py:310
  100.7 0.8 multiply_reduce_fusion.10
  101.5 0.8 copy.147
  102.4 1.9 %fusion.4 = f32[8,128,16,16]{1,3,0,2:T(8,128)S(1)} fusion(f32[16,8,16,128]{3,2,1,0:T(8,128)S(1)} %copy-done.7, f32[8,16,16,16]{1,3,0,2:T(8,128)S(1)} %copy-done.3, f32[16,16,16]{0,2,1:T(8,128)S(1)} %bitcast.256, f32[8,16,16]{1,0,2:T(8,128)S(1)} %get-tuple-element.81, f32[16,16]{1,0:T(8,128)} %copy-done.21, f32[16,16]{1,0:T(8,128)S(1)} %copy-done.18, ...), kind=kOutput, calls=%fused_computation.20 | convolution fusion | flops 50757632 | bytes 2255872 | tf_op jit(solution)/shard_map/gnt,bngm->btgm/dot_general | solution.py:329
  105.2 0.7 fusion.72
  105.9 2.1 %multiply_convert_fusion = bf16[1024,256]{1,0:T(8,128)(2,1)} fusion(f32[1024,256]{1,0:T(8,128)S(1)} %copy.120.inner_ref, f32[3,1024,256]{2,1,0:T(8,128)} %copy-done), kind=kLoop, calls=%fused_computation.38 | loop fusion | flops 524288 | bytes 2621440 | tf_op jit(solution)/shard_map/convert_element_type | solution.py:336
  108.1 1.7 %copy.128 = f32[8,16,16,16]{3,2,1,0:T(8,128)S(1)} copy(f32[8,16,16,16]{1,3,0,2:T(8,128)} %get-tuple-element.88) | data formatting | bytes 262144 | tf_op jit(solution)/shard_map/gnt,btgm->bngm/transpose | solution.py:261
  109.8 5.0 %multiply_reduce_fusion = f32[8,16,16,16]{3,2,1,0:T(8,128)} fusion(f32[8,16,16,16]{3,2,1,0:T(8,128)S(1)} %copy.128, f32[8,8,16,16]{3,2,1,0:T(8,128)} %select_bitcast_fusion), kind=kLoop, calls=%fused_computation | loop fusion | flops 491520 | bytes 327680 | tf_op jit(solution)/shard_map/reduce_sum | solution.py:262
  114.8 1.7 %copy.130 = f32[8,16,16,16]{1,3,0,2:T(8,128)S(1)} copy(f32[8,16,16,16]{3,2,1,0:T(8,128)} %multiply_reduce_fusion) | data formatting | bytes 262144 | tf_op jit(solution)/shard_map/reduce_sum | solution.py:262
  116.5 1.2 fusion.3
  118.6 0.8 fusion.71
  121.5 1.2 broadcast_in_dim.98.tile_ref
  122.7 30.0 %shard_map.85 = (f32[8,128]{1,0:T(8,128)}, bf16[3,1024,256]{2,1,0:T(8,128)(2,1)}) custom-call(f32[8,128]{1,0:T(8,128)} %broadcast_in_dim.98.tile_ref, f32[6,256]{1,0:T(8,128)} %reshape.436.rim_ref, bf16[1024,256]{1,0:T(8,128)(2,1)} %cot_ref.1, f32[1024,256]{1,0:T(8,128)} %copy-done.1, f32[1024,256]{1,0:T(8,128)} %copy-done.6, ...), custom_call_target="tpu_custom_call" | custom-call | tf_op jit(solution)/shard_map/pallas_call | solution.py:161
  152.7 1.2 slice.177
  155.2 2.7 %copy.191 = bf16[3,1024,256]{2,1,0:T(8,128)(2,1)} copy(bf16[3,1024,256]{2,1,0:T(8,128)(2,1)} %get-tuple-element.104) | data formatting | bytes 3145728
  (140 shorter events, 13.1 us)
Async XLA Ops:
  0.6 15.9 %copy-start.10 = (bf16[3,1024,256]{2,1,0:T(8,128)(2,1)S(1)}, bf16[3,1024,256]{2,1,0:T(8,128)(2,1)}, u32[]{:S(2)}) copy-start(bf16[3,1024,256]{2,1,0:T(8,128)(2,1)} %param.9) | copy-start | bytes 4718596
  1.5 15.1 %collective-permute-start = (bf16[3,2,256]{2,1,0:T(2,128)(2,1)S(1)}, bf16[3,2,256]{2,1,0:T(2,128)(2,1)S(1)}, u32[]{:S(2)}, u32[]{:S(2)}) collective-permute-start(bf16[3,2,256]{2,1,0:T(2,128)(2,1)S(1)} %slice.149), channel_id=1, source_target_pairs={{0,1},{1,2},{2,3},{3,4},{4,5},{5,6},{6,7},{7,8},{8,9},{9,10},{10,1... | collective-permute-start | bytes 9224 | tf_op jit(solution)/shard_map/ppermute | solution.py:185
  5.9 9.7 %copy-start.32 = (f32[8]{0:T(128)}, f32[8]{0:T(128)S(1)}, u32[]{:S(2)}) copy-start(f32[8]{0:T(128)S(1)} %get-tuple-element.93) | copy-start | bytes 100
  5.9 9.7 %copy-start.39 = (f32[8]{0:T(128)}, f32[8]{0:T(128)S(1)}, u32[]{:S(2)}) copy-start(f32[8]{0:T(128)S(1)} %get-tuple-element.94) | copy-start | bytes 100
  11.9 3.8 %copy-start.21 = (f32[16,16]{1,0:T(8,128)}, f32[16,16]{1,0:T(8,128)S(1)}, u32[]{:S(2)}) copy-start(f32[16,16]{1,0:T(8,128)S(1)} %get-tuple-element.78) | copy-start | bytes 3076
  15.9 4.9 %copy-start.16 = (f32[16,256]{1,0:T(8,128)}, f32[16,256]{1,0:T(8,128)S(1)}, u32[]{:S(2)}) copy-start(f32[16,256]{1,0:T(8,128)S(1)} %neg.48) | copy-start | bytes 49156
  17.6 1.7 %copy-start = (f32[3,1024,256]{2,1,0:T(8,128)}, f32[3,1024,256]{2,1,0:T(8,128)S(1)}, u32[]{:S(2)}) copy-start(f32[3,1024,256]{2,1,0:T(8,128)S(1)} %multiply_add_fusion) | copy-start | bytes 9437188
  21.1 0.8 copy-start.4
  39.7 4.3 %copy-start.27 = (pred[128,128]{1,0:T(8,128)(4,1)S(1)}, pred[128,128]{1,0:T(8,128)(4,1)}, u32[]{:S(2)}) copy-start(pred[128,128]{1,0:T(8,128)(4,1)} %fusion.54) | copy-start | bytes 49156
  44.0 2.1 %copy-start.15 = (f32[128,128]{1,0:T(8,128)S(1)}, f32[128,128]{1,0:T(8,128)}, u32[]{:S(2)}) copy-start(f32[128,128]{1,0:T(8,128)} %maximum_convert_fusion) | copy-start | bytes 196612
  44.0 2.2 %copy-start.19 = (f32[16,16]{1,0:T(8,128)S(1)}, f32[16,16]{1,0:T(8,128)}, u32[]{:S(2)}) copy-start(f32[16,16]{1,0:T(8,128)} %rate_ref.1) | copy-start | bytes 3076
  46.1 2.8 %copy-start.12 = (f32[1,16,16,128]{3,2,0,1:T(8,128)S(1)}, f32[1,16,16,128]{3,2,0,1:T(8,128)}, u32[]{:S(2)}) copy-start(f32[1,16,16,128]{3,2,0,1:T(8,128)} %get-tuple-element.69) | copy-start | bytes 393220
  46.1 2.8 %copy-start.13 = (f32[1,16,16,128]{3,2,0,1:T(8,128)S(1)}, f32[1,16,16,128]{3,2,0,1:T(8,128)}, u32[]{:S(2)}) copy-start(f32[1,16,16,128]{3,2,0,1:T(8,128)} %get-tuple-element.70) | copy-start | bytes 393220
  46.2 4.8 %copy-start.2 = (f32[8,16,16,16]{1,3,0,2:T(8,128)S(1)}, f32[8,16,16,16]{1,3,0,2:T(8,128)}, u32[]{:S(2)}) copy-start(f32[8,16,16,16]{1,3,0,2:T(8,128)} %copy.107) | copy-start | bytes 393220
  46.2 4.8 %copy-start.9 = (f32[8,16,16,16]{1,3,0,2:T(8,128)S(1)}, f32[8,16,16,16]{1,3,0,2:T(8,128)}, u32[]{:S(2)}) copy-start(f32[8,16,16,16]{1,3,0,2:T(8,128)} %copy.112) | copy-start | bytes 393220
  46.2 4.8 %copy-start.33 = (f32[8]{0:T(128)S(1)}, f32[8]{0:T(128)}, u32[]{:S(2)}) copy-start(f32[8]{0:T(128)} %copy-done.32) | copy-start | bytes 100
  57.0 2.3 %copy-start.31 = (f32[1,256]{1,0:T(1,128)S(1)}, f32[1,256]{1,0:T(1,128)}, u32[]{:S(2)}) copy-start(f32[1,256]{1,0:T(1,128)} %stack.74) | copy-start | bytes 3076
  58.8 36.9 %copy-start.5 = (bf16[32,8,8,128]{3,2,1,0:T(8,128)(2,1)S(1)}, bf16[32,8,8,128]{3,2,1,0:T(8,128)(2,1)}, u32[]{:S(2)}) copy-start(bf16[32,8,8,128]{3,2,1,0:T(8,128)(2,1)} %copy-done.4) | copy-start | bytes 1572868
  59.4 0.6 copy-start.14
  93.0 2.6 %copy-start.8 = (f32[16,128,128]{2,1,0:T(8,128)S(1)}, f32[16,128,128]{2,1,0:T(8,128)}, u32[]{:S(2)}) copy-start(f32[16,128,128]{2,1,0:T(8,128)} %get-tuple-element.32) | copy-start | bytes 3145732
  93.0 4.5 %copy-start.11 = (f32[16,72,256]{2,1,0:T(8,128)S(1)}, f32[16,72,256]{2,1,0:T(8,128)}, u32[]{:S(2)}) copy-start(f32[16,72,256]{2,1,0:T(8,128)} %get-tuple-element.33) | copy-start | bytes 3538948
  95.7 2.7 %copy-start.17 = (f32[16,256]{1,0:T(8,128)S(1)}, f32[16,256]{1,0:T(8,128)}, u32[]{:S(2)}) copy-start(f32[16,256]{1,0:T(8,128)} %copy-done.16) | copy-start | bytes 49156
  95.7 2.7 %copy-start.29 = (f32[16,16]{1,0:T(8,128)S(1)}, f32[16,16]{1,0:T(8,128)}, u32[]{:S(2)}) copy-start(f32[16,16]{1,0:T(8,128)} %get-tuple-element.84) | copy-start | bytes 3076
  95.7 2.7 %copy-start.30 = (f32[16,16]{1,0:T(8,128)S(1)}, f32[16,16]{1,0:T(8,128)}, u32[]{:S(2)}) copy-start(f32[16,16]{1,0:T(8,128)} %get-tuple-element.85) | copy-start | bytes 3076
  95.7 2.7 %copy-start.38 = (pred[16,16]{1,0:T(8,128)(4,1)S(1)}, pred[16,16]{1,0:T(8,128)(4,1)}, u32[]{:S(2)}) copy-start(pred[16,16]{1,0:T(8,128)(4,1)} %subtract_compare_fusion) | copy-start | bytes 772
  97.6 3.1 %copy-start.25 = (f32[16,256]{1,0:T(8,128)S(1)}, f32[16,256]{1,0:T(8,128)}, u32[]{:S(2)}) copy-start(f32[16,256]{1,0:T(8,128)} %exp.95) | copy-start | bytes 49156
  97.6 3.1 %copy-start.34 = (f32[16]{0:T(128)S(1)}, f32[16]{0:T(128)}, u32[]{:S(2)}) copy-start(f32[16]{0:T(128)} %get-tuple-element.95) | copy-start | bytes 196
  97.6 3.1 %copy-start.35 = (f32[16]{0:T(128)S(1)}, f32[16]{0:T(128)}, u32[]{:S(2)}) copy-start(f32[16]{0:T(128)} %get-tuple-element.96) | copy-start | bytes 196
  97.6 3.1 %copy-start.36 = (pred[16]{0:T(512)(128)(4,1)S(1)}, pred[16]{0:T(512)(128)(4,1)}, u32[]{:S(2)}) copy-start(pred[16]{0:T(512)(128)(4,1)} %get-tuple-element.97) | copy-start | bytes 52
  97.6 3.1 %copy-start.37 = (pred[16]{0:T(512)(128)(4,1)S(1)}, pred[16]{0:T(512)(128)(4,1)}, u32[]{:S(2)}) copy-start(pred[16]{0:T(512)(128)(4,1)} %get-tuple-element.98) | copy-start | bytes 52
  97.6 4.8 %copy-start.3 = (f32[8,16,16,16]{1,3,0,2:T(8,128)S(1)}, f32[8,16,16,16]{1,3,0,2:T(8,128)}, u32[]{:S(2)}) copy-start(f32[8,16,16,16]{1,3,0,2:T(8,128)} %copy.107) | copy-start | bytes 393220
  97.6 4.7 %copy-start.7 = (f32[16,8,16,128]{3,2,1,0:T(8,128)S(1)}, f32[16,8,16,128]{3,2,1,0:T(8,128)}, u32[]{:S(2)}) copy-start(f32[16,8,16,128]{3,2,1,0:T(8,128)} %fusion.11) | copy-start | bytes 3145732
  97.6 4.7 %copy-start.18 = (f32[16,16]{1,0:T(8,128)S(1)}, f32[16,16]{1,0:T(8,128)}, u32[]{:S(2)}) copy-start(f32[16,16]{1,0:T(8,128)} %get-tuple-element.76.coef_ref) | copy-start | bytes 3076
  104.6 3.4 %copy-start.24 = (f32[16,256]{1,0:T(8,128)S(1)}, f32[16,256]{1,0:T(8,128)}, u32[]{:S(2)}) copy-start(f32[16,256]{1,0:T(8,128)} %get-tuple-element.45) | copy-start | bytes 49156
  105.2 9.7 %copy-start.1 = (f32[1024,256]{1,0:T(8,128)}, f32[1024,256]{1,0:T(8,128)S(1)}, u32[]{:S(2)}) copy-start(f32[1024,256]{1,0:T(8,128)S(1)} %copy.120.inner_ref) | copy-start | bytes 3145732
  108.1 8.4 %copy-start.40 = (f32[128]{0:T(128)S(1)}, f32[128]{0:T(128)}, u32[]{:S(2)}) copy-start(f32[128]{0:T(128)} %iota_subtract_fusion.2) | copy-start | bytes 1540
  117.7 2.4 %copy-start.23 = (f32[16,256]{1,0:T(8,128)S(1)}, f32[16,256]{1,0:T(8,128)}, u32[]{:S(2)}) copy-start(f32[16,256]{1,0:T(8,128)} %get-tuple-element.48) | copy-start | bytes 49156
  117.7 2.6 %copy-start.22 = (f32[16,256]{1,0:T(8,128)S(1)}, f32[16,256]{1,0:T(8,128)}, u32[]{:S(2)}) copy-start(f32[16,256]{1,0:T(8,128)} %get-tuple-element.47) | copy-start | bytes 49156
  117.7 2.9 %copy-start.28 = (f32[2,256]{1,0:T(2,128)S(1)}, f32[2,256]{1,0:T(2,128)}, u32[]{:S(2)}) copy-start(f32[2,256]{1,0:T(2,128)} %slice_reduce_fusion) | copy-start | bytes 6148
  117.7 3.1 %copy-start.20 = (f32[16,16]{1,0:T(8,128)S(1)}, f32[16,16]{1,0:T(8,128)}, u32[]{:S(2)}) copy-start(f32[16,16]{1,0:T(8,128)} %rate_ref.1) | copy-start | bytes 3076
  117.7 3.1 %copy-start.26 = (f32[16,16]{1,0:T(8,128)S(1)}, f32[16,16]{1,0:T(8,128)}, u32[]{:S(2)}) copy-start(f32[16,16]{1,0:T(8,128)} %param.12) | copy-start | bytes 3076
  118.6 4.0 %copy-start.6 = (f32[1024,256]{1,0:T(8,128)}, f32[1024,256]{1,0:T(8,128)S(1)}, u32[]{:S(2)}) copy-start(f32[1024,256]{1,0:T(8,128)S(1)} %copy.132.grad_ref) | copy-start | bytes 3145732

commit v10 on v9

--- a/solution.py
+++ b/solution.py
@@ -277,7 +277,7 @@
     state_rows = jnp.stack([end_state, end_lagged, start_state, second_moment]).reshape(
         4 * order_count, channels
     )
-    payload_rows = -(-(state_rows.shape[0] + partial_rows.shape[0]) // 8) * 8
+    payload_rows = state_rows.shape[0] + partial_rows.shape[0]
     local_states = jnp.zeros((payload_rows, channels), jnp.float32)
     local_states = local_states.at[: state_rows.shape[0]].set(state_rows)
     local_states = local_states.at[state_rows.shape[0] : state_rows.shape[0] + partial_rows.shape[0]].set(

time: 159 us -> 151 us (0.950)
  local copies, waits for them, and re-layouts: 35.9 us -> 33.1 us
  other arithmetic: 35.5 us -> 33 us
  matrix products: 17 us -> 14.9 us
    another operation x2, local copies, waits for them, and re-layouts: 2.15 us -> 0.16 us  [per_device(): partial_rows = jnp.stack([first_local, lag_local]).reshape(-1, channels)]
    unnamed x89 -> x81, local copies, waits for them, and re-layouts: 7.84 us -> 7.17 us
where the time goes in v10:
time: 151 us; the launch traced here: 150 us
  Pallas kernels  63 us (42%)
  local copies, waits for them, and re-layouts  33.1 us (22%)
  other arithmetic  33 us (22%)
  matrix products  14.9 us (10%)
  starting transfers between devices  4.36 us (3%)
  between operations  2.11 us (1%)
    pallas_call x1, Pallas kernels, gather_along(): pl.pallas_call(functools.partial(gather_kernel, axis, count), out_shape=(...  33 us
    pallas_call x1, Pallas kernels, finish_exchange(): pl.pallas_call(functools.partial(finish_kernel, fsdp_count, ctx_count), o...  30 us
    unnamed x81, local copies, waits for them, and re-layouts  7.17 us
    reduce_sum x1, other arithmetic, per_device(): jnp.sum(span_weight * (fresh_fwd[1][None] - block_len * block_steps * fre...  5.75 us
    reduce_sum x1, other arithmetic, per_device(): jnp.sum(jnp.swapaxes(span_weight, 0, 1) * fresh_bwd[None], axis=1)  5.01 us
    ppermute x1, starting transfers between devices, passed_along(): lax.ppermute(value, axis, [(source, source + steps) for source in range(l...  4.36 us
    squeeze x2, local copies, waits for them, and re-layouts, per_device(): end_state = jnp.sum(from_last * fresh_fwd[0], axis=0)  3.3 us
  transfers between devices with their start and end apart: 1, of which 0 were waited for; matrix products, arithmetic and copies ran while one was open for 7% of the time, Pallas kernels for 0%

profile of v10, /device:TPU:1, one launch (start us, length us, event | category | flops | bytes accessed | tf_op | source)
XLA Modules:
  0.0 150.4 jit_solution(4036590090390191771)
XLA Ops:
  0.6 0.8 slice.149
  1.5 4.4 %collective-permute-start = (bf16[3,2,256]{2,1,0:T(2,128)(2,1)S(1)}, bf16[3,2,256]{2,1,0:T(2,128)(2,1)S(1)}, u32[]{:S(2)}, u32[]{:S(2)}) collective-permute-start(bf16[3,2,256]{2,1,0:T(2,128)(2,1)S(1)} %slice.149), channel_id=1, source_target_pairs={{0,1},{1,2},{2,3},{3,4},{4,5},{5,6},{6,7},{7,8},{8,9},{9,10},{10,1... | collective-permute-start | bytes 9224 | tf_op jit(solution)/shard_map/ppermute | solution.py:185
  5.9 0.6 fusion.54
  6.5 0.6 maximum_convert_fusion
  7.2 0.7 fusion.60
  9.7 0.8 fusion.75
  10.5 1.3 fusion.65
  12.1 1.0 select_bitcast_fusion
  13.1 1.0 exponential_select_fusion.1
  14.2 0.8 exponential_multiply_fusion
  16.5 1.0 multiply_add_fusion
  17.5 1.7 %copy-done = f32[3,1024,256]{2,1,0:T(8,128)} copy-done((f32[3,1024,256]{2,1,0:T(8,128)}, f32[3,1024,256]{2,1,0:T(8,128)S(1)}, u32[]{:S(2)}) %copy-start) | copy-done | bytes 3145752
  19.2 1.5 %slice_bitcast_fusion.6 = (f32[1024,256]{1,0:T(8,128)}, f32[1024,256]{1,0:T(8,128)}, bf16[1,1024,256]{2,1,0:T(8,128)(2,1)S(1)}) fusion(f32[3,1024,256]{2,1,0:T(8,128)S(1)} %multiply_add_fusion), kind=kLoop, calls=%fused_computation.51 | loop fusion | flops 524288 | bytes 4718592 | tf_op jit(solution)/shard_map/squeeze | solution.py:212
  21.1 0.8 copy-done.4
  21.8 0.8 convolution_bitcast_fusion.1
  22.6 1.6 %slice_bitcast_fusion.3 = (f32[8,16,16,16]{1,3,0,2:T(8,128)}, f32[8,16,16,16]{1,3,0,2:T(8,128)}) fusion(f32[2,8,16,16,16]{2,4,0,1,3:T(8,128)S(1)} %convolution_bitcast_fusion.1), kind=kLoop, calls=%fused_computation.29 | loop fusion | bytes 524288 | tf_op jit(solution)/shard_map/squeeze | solution.py:266
  24.2 1.7 %copy.106 = f32[8,16,16,16]{3,2,1,0:T(8,128)S(1)} copy(f32[8,16,16,16]{1,3,0,2:T(8,128)} %get-tuple-element.60) | data formatting | bytes 262144 | tf_op jit(solution)/shard_map/squeeze | solution.py:266
  25.9 2.6 %copy.110 = f32[8,16,16,16]{3,2,1,0:T(8,128)} copy(f32[8,16,16,16]{1,3,0,2:T(8,128)} %get-tuple-element.61) | data formatting | bytes 262144 | tf_op jit(solution)/shard_map/squeeze | solution.py:269
  28.5 5.8 %multiply_reduce_fusion.1 = (f32[8,16,16,16]{3,2,1,0:T(8,128)}, f32[8,16,16,16]{3,2,1,0:T(8,128)}) fusion(f32[8,8]{1,0:T(8,128)S(1)} %copy.111, f32[8,16,16,16]{3,2,1,0:T(8,128)} %copy.110, f32[8,16,16,16]{3,2,1,0:T(8,128)S(1)} %copy.106, f32[8,8,16,16]{3,2,1,0:T(8,128)} %exponential_select_fusion.1), kind=kLoop, calls=%fused_computation.1 | loop fusion | flops 1507328 | bytes 590080 | tf_op jit(solution)/shard_map/reduce_sum | solution.py:246
  34.3 2.6 %copy.107 = f32[8,16,16,16]{1,3,0,2:T(8,128)} copy(f32[8,16,16,16]{3,2,1,0:T(8,128)} %get-tuple-element.42) | data formatting | bytes 262144 | tf_op jit(solution)/shard_map/reduce_sum | solution.py:245
  36.9 2.6 %copy.112 = f32[8,16,16,16]{1,3,0,2:T(8,128)} copy(f32[8,16,16,16]{3,2,1,0:T(8,128)} %get-tuple-element.41) | data formatting | bytes 262144 | tf_op jit(solution)/shard_map/reduce_sum | solution.py:246
  39.5 1.5 convert_multiply_fusion
  41.1 1.3 copy.98
  42.4 1.4 copy.158
  44.2 2.0 %convolution_bitcast_fusion = f32[2,8,16,16,16]{2,4,1,3,0:T(8,128)S(1)} fusion(f32[8,128,16,16]{1,0,3,2:T(8,128)S(1)} %bitcast.239, f32[1,16,16,128]{3,2,0,1:T(8,128)S(1)} %copy-done.12, f32[1,16,16,128]{3,2,0,1:T(8,128)S(1)} %copy-done.11), kind=kOutput, calls=%fused_computation.10 | convolution fusion | flops 100728832 | bytes 1572864 | tf_op jit(solution)/shard_map/kgnt,btgm->kbngm/dot_general | solution.py:249
  46.2 2.7 %multiply_reduce_fusion.5 = (f32[16,16]{0,1:T(8,128)S(1)}, f32[16,16]{0,1:T(8,128)S(1)}, f32[16,16,16]{0,2,1:T(8,128)S(1)}, f32[16,16,16]{0,2,1:T(8,128)S(1)}, f32[8,16,16,16]{1,3,0,2:T(8,128)}) fusion(f32[8,16,16,16]{1,3,0,2:T(8,128)S(1)} %copy-done.2, f32[2,8,16,16,16]{2,4,1,3,0:T(8,128)S(1)} %convolution_bitcast_fusion, ...), kind=kOutput, calls=%fused_computation.43 | convolution fusion | flops 50748928 | bytes 1748000 | tf_op jit(solution)/shard_map/gnt,btgm->bngm/dot_general | solution.py:261
  49.6 1.0 fusion.5
  50.7 1.9 %fusion.6 = f32[2,16,16,128]{3,2,0,1:T(8,128)S(1)} fusion(f32[16,16]{1,0:T(8,128)S(1)} %copy-done.17, f32[1,16,128,128]{3,2,1,0:T(8,128)S(1)} %multiply_bitcast_fusion, f32[1,16,128,128]{3,2,1,0:T(8,128)S(1)} %bitcast.248), kind=kOutput, calls=%fused_computation.23 | convolution fusion | flops 101220352 | bytes 2360320 | tf_op jit(solution)/shard_map/kgts,gns->kgnt/dot_general | solution.py:256
  53.0 0.6 pad_maximum_fusion.3.x_ref
  53.6 33.0 %shard_map.84 = (f32[16,66,256]{2,1,0:T(8,128)}, f32[16,128,128]{2,1,0:T(8,128)}) custom-call(f32[66,256]{1,0:T(8,128)} %pad_maximum_fusion.3.x_ref, f32[16,16]{1,0:T(8,128)} %rate_ref.1, f32[16,16]{1,0:T(8,128)} %get-tuple-element.76.coef_ref), custom_call_target="tpu_custom_call" | custom-call | tf_op jit(solution)/shard_map/pallas_call | solution.py:63
  86.6 2.6 %fusion.9 = f32[16,8,16,128]{3,2,1,0:T(8,128)S(1)} fusion(f32[16,128,128]{2,1,0:T(8,128)} %get-tuple-element.32, f32[8,128,16,16]{1,0,3,2:T(8,128)S(1)} %bitcast.242), kind=kOutput, calls=%fused_computation.31 | convolution fusion | flops 402653184 | bytes 3145728 | tf_op jit(solution)/shard_map/gts,btgm->bsgm/dot_general | solution.py:289
  89.3 0.8 fusion.11
  90.3 0.6 slice_reduce_fusion
  91.0 2.2 %multiply_reduce_fusion.3 = (f32[16,16,256]{2,1,0:T(8,128)S(1)}, f32[16,16,256]{2,1,0:T(8,128)S(1)}) fusion(f32[16,16]{1,0:T(8,128)S(1)} %copy-done.28, f32[16,16,256]{2,1,0:T(8,128)S(1)} %get-tuple-element.63, f32[16,16,256]{2,1,0:T(8,128)S(1)} %get-tuple-element.62, f32[16,16]{1,0:T(8,128)S(1)} %copy-done.27, f32[16,256]{1,0:T(8,128)S(1)} %copy-done.15, ...), kind=kLoop, calls=%fused_computation.3 | loop fusion | flops 8257536 | bytes 1067264 | tf_op jit(solution)/shard_map/reduce_sum | solution.py:310
  93.3 0.8 multiply_reduce_fusion.10
  94.1 0.8 copy.147
  95.0 1.9 %fusion.4 = f32[8,128,16,16]{1,3,0,2:T(8,128)S(1)} fusion(f32[16,8,16,128]{3,2,1,0:T(8,128)S(1)} %fusion.11, f32[8,16,16,16]{1,3,0,2:T(8,128)S(1)} %copy-done.3, f32[16,16,16]{0,2,1:T(8,128)S(1)} %bitcast.256, f32[8,16,16]{1,0,2:T(8,128)S(1)} %get-tuple-element.81, f32[16,16]{1,0:T(8,128)} %copy-done.19, f32[16,16]{1,0:T(8,128)S(1)} %copy-done.16, ...), kind=kOutput, calls=%fused_computation.20 | convolution fusion | flops 50757632 | bytes 2255872 | tf_op jit(solution)/shard_map/gnt,bngm->btgm/dot_general | solution.py:329
  97.8 0.7 fusion.72
  98.5 2.1 %multiply_convert_fusion = bf16[1024,256]{1,0:T(8,128)(2,1)} fusion(f32[1024,256]{1,0:T(8,128)S(1)} %copy.120.inner_ref, f32[3,1024,256]{2,1,0:T(8,128)} %copy-done), kind=kLoop, calls=%fused_computation.38 | loop fusion | flops 524288 | bytes 2621440 | tf_op jit(solution)/shard_map/convert_element_type | solution.py:336
  100.7 1.7 %copy.128 = f32[8,16,16,16]{3,2,1,0:T(8,128)S(1)} copy(f32[8,16,16,16]{1,3,0,2:T(8,128)} %get-tuple-element.88) | data formatting | bytes 262144 | tf_op jit(solution)/shard_map/gnt,btgm->bngm/transpose | solution.py:261
  102.4 5.0 %multiply_reduce_fusion = f32[8,16,16,16]{3,2,1,0:T(8,128)} fusion(f32[8,16,16,16]{3,2,1,0:T(8,128)S(1)} %copy.128, f32[8,8,16,16]{3,2,1,0:T(8,128)} %select_bitcast_fusion), kind=kLoop, calls=%fused_computation | loop fusion | flops 491520 | bytes 327680 | tf_op jit(solution)/shard_map/reduce_sum | solution.py:262
  107.5 1.7 %copy.130 = f32[8,16,16,16]{1,3,0,2:T(8,128)S(1)} copy(f32[8,16,16,16]{3,2,1,0:T(8,128)} %multiply_reduce_fusion) | data formatting | bytes 262144 | tf_op jit(solution)/shard_map/reduce_sum | solution.py:262
  109.1 1.2 fusion.3
  111.2 0.8 fusion.71
  114.1 1.2 broadcast_in_dim.98.tile_ref
  115.3 30.0 %shard_map.85 = (f32[8,128]{1,0:T(8,128)}, bf16[3,1024,256]{2,1,0:T(8,128)(2,1)}) custom-call(f32[8,128]{1,0:T(8,128)} %broadcast_in_dim.98.tile_ref, f32[6,256]{1,0:T(8,128)} %reshape.436.rim_ref, bf16[1024,256]{1,0:T(8,128)(2,1)} %cot_ref.1, f32[1024,256]{1,0:T(8,128)} %copy-done.1, f32[1024,256]{1,0:T(8,128)} %copy-done.6, ...), custom_call_target="tpu_custom_call" | custom-call | tf_op jit(solution)/shard_map/pallas_call | solution.py:161
  145.3 1.2 slice.177
  147.8 2.7 %copy.190 = bf16[3,1024,256]{2,1,0:T(8,128)(2,1)} copy(bf16[3,1024,256]{2,1,0:T(8,128)(2,1)} %get-tuple-element.104) | data formatting | bytes 3145728
  (131 shorter events, 10.0 us)
Async XLA Ops:
  0.6 15.9 %copy-start.9 = (bf16[3,1024,256]{2,1,0:T(8,128)(2,1)S(1)}, bf16[3,1024,256]{2,1,0:T(8,128)(2,1)}, u32[]{:S(2)}) copy-start(bf16[3,1024,256]{2,1,0:T(8,128)(2,1)} %param.9) | copy-start | bytes 4718596
  1.5 15.0 %collective-permute-start = (bf16[3,2,256]{2,1,0:T(2,128)(2,1)S(1)}, bf16[3,2,256]{2,1,0:T(2,128)(2,1)S(1)}, u32[]{:S(2)}, u32[]{:S(2)}) collective-permute-start(bf16[3,2,256]{2,1,0:T(2,128)(2,1)S(1)} %slice.149), channel_id=1, source_target_pairs={{0,1},{1,2},{2,3},{3,4},{4,5},{5,6},{6,7},{7,8},{8,9},{9,10},{10,1... | collective-permute-start | bytes 9224 | tf_op jit(solution)/shard_map/ppermute | solution.py:185
  5.9 9.7 %copy-start.34 = (f32[8]{0:T(128)}, f32[8]{0:T(128)S(1)}, u32[]{:S(2)}) copy-start(f32[8]{0:T(128)S(1)} %get-tuple-element.94) | copy-start | bytes 100
  11.8 3.8 %copy-start.19 = (f32[16,16]{1,0:T(8,128)}, f32[16,16]{1,0:T(8,128)S(1)}, u32[]{:S(2)}) copy-start(f32[16,16]{1,0:T(8,128)S(1)} %get-tuple-element.78) | copy-start | bytes 3076
  15.9 4.9 %copy-start.14 = (f32[16,256]{1,0:T(8,128)}, f32[16,256]{1,0:T(8,128)S(1)}, u32[]{:S(2)}) copy-start(f32[16,256]{1,0:T(8,128)S(1)} %neg.48) | copy-start | bytes 49156
  17.5 1.7 %copy-start = (f32[3,1024,256]{2,1,0:T(8,128)}, f32[3,1024,256]{2,1,0:T(8,128)S(1)}, u32[]{:S(2)}) copy-start(f32[3,1024,256]{2,1,0:T(8,128)S(1)} %multiply_add_fusion) | copy-start | bytes 9437188
  21.0 0.8 copy-start.4
  39.5 4.3 %copy-start.35 = (f32[8]{0:T(128)S(1)}, f32[8]{0:T(128)}, u32[]{:S(2)}) copy-start(f32[8]{0:T(128)} %copy-done.34) | copy-start | bytes 100
  41.0 3.1 %copy-start.11 = (f32[1,16,16,128]{3,2,0,1:T(8,128)S(1)}, f32[1,16,16,128]{3,2,0,1:T(8,128)}, u32[]{:S(2)}) copy-start(f32[1,16,16,128]{3,2,0,1:T(8,128)} %get-tuple-element.69) | copy-start | bytes 393220
  41.1 3.1 %copy-start.12 = (f32[1,16,16,128]{3,2,0,1:T(8,128)S(1)}, f32[1,16,16,128]{3,2,0,1:T(8,128)}, u32[]{:S(2)}) copy-start(f32[1,16,16,128]{3,2,0,1:T(8,128)} %get-tuple-element.70) | copy-start | bytes 393220
  43.8 2.4 %copy-start.2 = (f32[8,16,16,16]{1,3,0,2:T(8,128)S(1)}, f32[8,16,16,16]{1,3,0,2:T(8,128)}, u32[]{:S(2)}) copy-start(f32[8,16,16,16]{1,3,0,2:T(8,128)} %copy.107) | copy-start | bytes 393220
  43.8 2.4 %copy-start.8 = (f32[8,16,16,16]{1,3,0,2:T(8,128)S(1)}, f32[8,16,16,16]{1,3,0,2:T(8,128)}, u32[]{:S(2)}) copy-start(f32[8,16,16,16]{1,3,0,2:T(8,128)} %copy.112) | copy-start | bytes 393220
  46.2 3.3 %copy-start.5 = (bf16[32,8,8,128]{3,2,1,0:T(8,128)(2,1)S(1)}, bf16[32,8,8,128]{3,2,1,0:T(8,128)(2,1)}, u32[]{:S(2)}) copy-start(bf16[32,8,8,128]{3,2,1,0:T(8,128)(2,1)} %copy-done.4) | copy-start | bytes 1572868
  46.2 3.3 %copy-start.25 = (pred[128,128]{1,0:T(8,128)(4,1)S(1)}, pred[128,128]{1,0:T(8,128)(4,1)}, u32[]{:S(2)}) copy-start(pred[128,128]{1,0:T(8,128)(4,1)} %fusion.54) | copy-start | bytes 49156
  49.6 1.0 copy-start.13
  49.6 1.1 copy-start.17
  86.6 2.6 %copy-start.7 = (f32[16,128,128]{2,1,0:T(8,128)S(1)}, f32[16,128,128]{2,1,0:T(8,128)}, u32[]{:S(2)}) copy-start(f32[16,128,128]{2,1,0:T(8,128)} %get-tuple-element.32) | copy-start | bytes 3145732
  86.6 3.6 %copy-start.10 = (f32[16,66,256]{2,1,0:T(8,128)S(1)}, f32[16,66,256]{2,1,0:T(8,128)}, u32[]{:S(2)}) copy-start(f32[16,66,256]{2,1,0:T(8,128)} %get-tuple-element.33) | copy-start | bytes 3244036
  89.3 1.7 %copy-start.15 = (f32[16,256]{1,0:T(8,128)S(1)}, f32[16,256]{1,0:T(8,128)}, u32[]{:S(2)}) copy-start(f32[16,256]{1,0:T(8,128)} %copy-done.14) | copy-start | bytes 49156
  89.3 1.7 %copy-start.27 = (f32[16,16]{1,0:T(8,128)S(1)}, f32[16,16]{1,0:T(8,128)}, u32[]{:S(2)}) copy-start(f32[16,16]{1,0:T(8,128)} %get-tuple-element.84) | copy-start | bytes 3076
  89.3 1.7 %copy-start.28 = (f32[16,16]{1,0:T(8,128)S(1)}, f32[16,16]{1,0:T(8,128)}, u32[]{:S(2)}) copy-start(f32[16,16]{1,0:T(8,128)} %get-tuple-element.85) | copy-start | bytes 3076
  89.3 1.7 %copy-start.33 = (pred[16,16]{1,0:T(8,128)(4,1)S(1)}, pred[16,16]{1,0:T(8,128)(4,1)}, u32[]{:S(2)}) copy-start(pred[16,16]{1,0:T(8,128)(4,1)} %subtract_compare_fusion) | copy-start | bytes 772
  90.1 3.1 %copy-start.23 = (f32[16,256]{1,0:T(8,128)S(1)}, f32[16,256]{1,0:T(8,128)}, u32[]{:S(2)}) copy-start(f32[16,256]{1,0:T(8,128)} %exp.95) | copy-start | bytes 49156
  90.2 3.1 %copy-start.29 = (f32[16]{0:T(128)S(1)}, f32[16]{0:T(128)}, u32[]{:S(2)}) copy-start(f32[16]{0:T(128)} %get-tuple-element.95) | copy-start | bytes 196
  90.2 3.1 %copy-start.30 = (f32[16]{0:T(128)S(1)}, f32[16]{0:T(128)}, u32[]{:S(2)}) copy-start(f32[16]{0:T(128)} %get-tuple-element.96) | copy-start | bytes 196
  90.2 3.1 %copy-start.31 = (pred[16]{0:T(512)(128)(4,1)S(1)}, pred[16]{0:T(512)(128)(4,1)}, u32[]{:S(2)}) copy-start(pred[16]{0:T(512)(128)(4,1)} %get-tuple-element.97) | copy-start | bytes 52
  90.2 3.1 %copy-start.32 = (pred[16]{0:T(512)(128)(4,1)S(1)}, pred[16]{0:T(512)(128)(4,1)}, u32[]{:S(2)}) copy-start(pred[16]{0:T(512)(128)(4,1)} %get-tuple-element.98) | copy-start | bytes 52
  90.2 4.8 %copy-start.3 = (f32[8,16,16,16]{1,3,0,2:T(8,128)S(1)}, f32[8,16,16,16]{1,3,0,2:T(8,128)}, u32[]{:S(2)}) copy-start(f32[8,16,16,16]{1,3,0,2:T(8,128)} %copy.107) | copy-start | bytes 393220
  90.2 4.8 %copy-start.16 = (f32[16,16]{1,0:T(8,128)S(1)}, f32[16,16]{1,0:T(8,128)}, u32[]{:S(2)}) copy-start(f32[16,16]{1,0:T(8,128)} %get-tuple-element.76.coef_ref) | copy-start | bytes 3076
  97.2 3.4 %copy-start.22 = (f32[16,256]{1,0:T(8,128)S(1)}, f32[16,256]{1,0:T(8,128)}, u32[]{:S(2)}) copy-start(f32[16,256]{1,0:T(8,128)} %get-tuple-element.45) | copy-start | bytes 49156
  97.8 9.7 %copy-start.1 = (f32[1024,256]{1,0:T(8,128)}, f32[1024,256]{1,0:T(8,128)S(1)}, u32[]{:S(2)}) copy-start(f32[1024,256]{1,0:T(8,128)S(1)} %copy.120.inner_ref) | copy-start | bytes 3145732
  100.7 8.4 %copy-start.36 = (f32[128]{0:T(128)S(1)}, f32[128]{0:T(128)}, u32[]{:S(2)}) copy-start(f32[128]{0:T(128)} %iota_subtract_fusion.2) | copy-start | bytes 1540
  110.3 2.4 %copy-start.21 = (f32[16,256]{1,0:T(8,128)S(1)}, f32[16,256]{1,0:T(8,128)}, u32[]{:S(2)}) copy-start(f32[16,256]{1,0:T(8,128)} %get-tuple-element.48) | copy-start | bytes 49156
  110.3 2.6 %copy-start.20 = (f32[16,256]{1,0:T(8,128)S(1)}, f32[16,256]{1,0:T(8,128)}, u32[]{:S(2)}) copy-start(f32[16,256]{1,0:T(8,128)} %get-tuple-element.47) | copy-start | bytes 49156
  110.3 2.9 %copy-start.26 = (f32[2,256]{1,0:T(2,128)S(1)}, f32[2,256]{1,0:T(2,128)}, u32[]{:S(2)}) copy-start(f32[2,256]{1,0:T(2,128)} %slice_reduce_fusion) | copy-start | bytes 6148
  110.3 3.1 %copy-start.18 = (f32[16,16]{1,0:T(8,128)S(1)}, f32[16,16]{1,0:T(8,128)}, u32[]{:S(2)}) copy-start(f32[16,16]{1,0:T(8,128)} %rate_ref.1) | copy-start | bytes 3076
  110.3 3.1 %copy-start.24 = (f32[16,16]{1,0:T(8,128)S(1)}, f32[16,16]{1,0:T(8,128)}, u32[]{:S(2)}) copy-start(f32[16,16]{1,0:T(8,128)} %param.12) | copy-start | bytes 3076
  111.2 4.0 %copy-start.6 = (f32[1024,256]{1,0:T(8,128)}, f32[1024,256]{1,0:T(8,128)S(1)}, u32[]{:S(2)}) copy-start(f32[1024,256]{1,0:T(8,128)S(1)} %copy.132.grad_ref) | copy-start | bytes 3145732
